TPU v7x, 32 devices: a whole 2x2x4 slice. The times are simulated.
32 devices in a mesh: row: 2 (over y), col: 4 (over x, core), frame: 4 (over z).
Axes of the slice: x: 2, y: 2, z: 4, core: 2. Of those that a mesh axis runs over, the one named last changes fastest.
Arguments:
- video: float32 [16, 576, 1024], P('frame', 'row', 'col'), may hold values from -60 to 60
- multiplier: float32 [16, 576, 1024], P('frame', 'row', 'col'), may hold values from -3 to 3
- foreground: float32 [16, 576, 1024], P('frame', 'row', 'col'), may hold values from -6 to 6
- basis: float32 [16, 576, 1024], P(None, 'row', 'col'), may hold values from -40 to 40
- coefficients: float32 [16, 16], P('frame'), may hold values from -10 to 10
Outputs:
- new_foreground: float32 [16, 576, 1024], P('frame', 'row', 'col')
- new_coefficients: float32 [16, 16], P('frame')
- new_basis: float32 [16, 576, 1024], P(None, ('row', 'frame'), 'col')
All inputs are finite; a program needn't handle non-finite values.
Results may differ from a plain program's by a relative error of at most 0.0003.
Values sent between devices are 32-bit elements; how exact they have to be, the bound alone decides.
A program may use at most 128 MiB of HBM per device.

v0:
```python
import functools

import jax
import jax.numpy as jnp
from jax import lax
from jax.experimental import pallas as pl
from jax.experimental.pallas import tpu as pltpu
from jax.sharding import PartitionSpec as P

PASSES = 3


relax_rate = 0.8
smooth_weight = 0.5
smooth_floor = 0.25
shrink_level = 0.4
dual_scale = 0.8
ridge_share = 0.1


def with_halo(block, sides, width):
    for axis, dim in sides:
        count = lax.axis_size(axis)
        forward = [(i, i + 1) for i in range(count - 1)]
        backward = [(target, source) for source, target in forward]
        low = lax.ppermute(
            lax.slice_in_dim(block, block.shape[dim] - width, None, axis=dim), axis, forward
        )
        high = lax.ppermute(lax.slice_in_dim(block, 0, width, axis=dim), axis, backward)
        block = jnp.concatenate([low, block, high], axis=dim)
    return block


def forward_cells(padded, direction, shape):
    starts = [0, 0, 0]
    starts[direction] = 1
    limits = [starts[axis_dim] + shape[axis_dim] for axis_dim in range(3)]
    return lax.slice(padded, starts, limits)


def descend(padded, source, anchor, extent):
    shape = tuple((int(length) - 1 for length in padded.shape))
    here_cells = padded[:-1, :-1, :-1]
    slopes = []
    for direction in range(3):
        ahead_cells = forward_cells(padded, direction, shape)
        places = anchor[direction] + jnp.arange(shape[direction], dtype=jnp.int32)
        inside = (places >= 0) & (places < extent[direction] - 1)
        layout = [1, 1, 1]
        layout[direction] = shape[direction]
        inside = inside.reshape(layout)
        slopes.append(jnp.where(inside, ahead_cells - here_cells, jnp.zeros_like(here_cells)))
    weight = lax.rsqrt(
        smooth_floor + slopes[0] * slopes[0] + slopes[1] * slopes[1] + slopes[2] * slopes[2]
    )
    fluxes = [slope_part * weight for slope_part in slopes]
    spread = (
        fluxes[0][1:, 1:, 1:]
        - fluxes[0][:-1, 1:, 1:]
        + (fluxes[1][1:, 1:, 1:] - fluxes[1][1:, :-1, 1:])
        + (fluxes[2][1:, 1:, 1:] - fluxes[2][1:, 1:, :-1])
    )
    center = padded[1:-1, 1:-1, 1:-1]
    return center + relax_rate * (source - center + smooth_weight * spread)


def solve_definite(matrix, right_side):
    factor_lower = jnp.linalg.cholesky(matrix)
    half_solved = lax.linalg.triangular_solve(factor_lower, right_side, left_side=True, lower=True)
    return lax.linalg.triangular_solve(
        factor_lower, half_solved, left_side=True, lower=True, transpose_a=True
    )


def local(video, multiplier, foreground, basis, coefficients):
    highest = lax.Precision.HIGHEST
    frames_here, rows_here, cols_here = video.shape
    rank_size = basis.shape[0]
    frame_count = lax.axis_size("frame")
    row_count = lax.axis_size("row")
    col_count = lax.axis_size("col")
    extent = (frames_here * frame_count, rows_here * row_count, cols_here * col_count)
    frame_slot = lax.axis_index("frame")
    corner = (
        frame_slot * frames_here,
        lax.axis_index("row") * rows_here,
        lax.axis_index("col") * cols_here,
    )
    pixels = rows_here * cols_here
    flat_basis = basis.reshape(rank_size, pixels)
    background = jnp.dot(coefficients, flat_basis, precision=highest).reshape(video.shape)
    target = video - background + dual_scale * multiplier
    current = foreground
    for sweep in range(PASSES):
        padded = with_halo(current, (("row", 1), ("col", 2), ("frame", 0)), 1)
        current = descend(padded, target, tuple((start_cell - 1 for start_cell in corner)), extent)
    shrunk = current - jnp.clip(current, -shrink_level, shrink_level)
    residual_target = video + dual_scale * multiplier - shrunk
    flat_target = residual_target.reshape(frames_here, pixels)
    gram_part = jnp.dot(flat_basis, flat_basis.T, precision=highest)
    cross_part = jnp.dot(flat_basis, flat_target.T, precision=highest)
    gram_sum, cross_sum = lax.psum((gram_part, cross_part), ("row", "col"))
    identity_matrix = jnp.eye(rank_size, dtype=gram_sum.dtype)
    pixel_ridge = ridge_share * pixels * row_count * col_count
    coeff_rows = solve_definite(
        gram_sum + pixel_ridge * identity_matrix, cross_sum + pixel_ridge * coefficients.T
    )
    total_part = jnp.dot(coeff_rows, flat_target, precision=highest).reshape(
        rank_size, rows_here, cols_here
    )
    frame_gram_part = jnp.dot(coeff_rows, coeff_rows.T, precision=highest)
    owned_rows = rows_here // frame_count
    owned_sums = lax.psum_scatter(total_part, "frame", scatter_dimension=1, tiled=True)
    frame_gram = lax.psum(frame_gram_part, "frame")
    old_owned = lax.dynamic_slice_in_dim(basis, frame_slot * owned_rows, owned_rows, 1)
    frame_ridge = ridge_share * frames_here * frame_count
    right_side = (owned_sums + frame_ridge * old_owned).reshape(rank_size, owned_rows * cols_here)
    new_basis = solve_definite(frame_gram + frame_ridge * identity_matrix, right_side)
    return (shrunk, coeff_rows.T, new_basis.reshape(rank_size, owned_rows, cols_here))


MESH = pl.DeviceIdType.MESH
CHUNK = 24


def eliminate(matrix, size):
    lanes = lax.broadcasted_iota(jnp.int32, matrix.shape, 1)
    rows = lax.broadcasted_iota(jnp.int32, matrix.shape, 0)
    for k in range(size):
        pivot = matrix[k : k + 1, k : k + 1]
        scaled = matrix[k : k + 1, :] / pivot
        column = jnp.sum(jnp.where(lanes == k, matrix, 0.0), axis=1, keepdims=True)
        matrix = jnp.where(rows == k, scaled, matrix - column * scaled)
    return matrix


def kernel(
    sizes, coeff_ref, video_hbm, mult_hbm, fore_hbm, basis_hbm,
    shrunk_hbm, rows_out, new_basis_hbm,
    field, video, mult, basis, anchor, target, result, owned,
    packed, arrived, corner, edge_next, edge_flux, first_cols,
    sums, parts, shares, square, table, table_smem,
    in_sems, out_sems, halo_send, halo_recv, part_send, part_recv,
    share_send, share_recv, move_send, move_recv, small_sem, barrier_own,
):
    F, H, W, rank, nr, nc, nz = sizes
    r = lax.axis_index("row")
    c = lax.axis_index("col")
    z = lax.axis_index("frame")
    own = H // nz

    def inside(dr, dc, dz):
        ok = None
        for at, step, count in ((r, dr, nr), (c, dc, nc), (z, dz, nz)):
            if step != 0:
                test = (at + step >= 0) & (at + step < count)
                ok = test if ok is None else ok & test
        return ok

    loads = []
    for i, (src, dst) in enumerate(
        (
            (fore_hbm, field.at[0, 1 : F + 1, 8 : H + 8, :]),
            (basis_hbm, basis),
            (video_hbm, video),
            (mult_hbm, mult),
        )
    ):
        copy = pltpu.make_async_copy(src, dst, in_sems.at[i])
        copy.start()
        loads.append(copy)

    barrier = pltpu.get_barrier_semaphore()
    for d in range(1, nr * nc):
        other = lax.rem(r * nc + c + d, nr * nc)
        pl.semaphore_signal(
            barrier, inc=1, device_id=(other // nc, lax.rem(other, nc), z), device_id_type=MESH
        )
    for d in range(1, nz):
        pl.semaphore_signal(
            barrier, inc=1, device_id=(r, c, lax.rem(z + d, nz)), device_id_type=MESH
        )
    diagonals = ((1, 0, -1), (-1, 0, 1), (0, 1, -1), (0, -1, 1))
    for step in diagonals:
        @pl.when(inside(*step))
        def _(step=step):
            pl.semaphore_signal(
                barrier,
                inc=1,
                device_id=(r + step[0], c + step[1], z + step[2]),
                device_id_type=MESH,
            )
    expected = jnp.int32(nr * nc - 1 + nz - 1)
    for step in diagonals:
        expected = expected + inside(*step).astype(jnp.int32)
    pl.semaphore_wait(barrier, expected)

    lane_h = lax.broadcasted_iota(jnp.int32, (H, 128), 1)

    def pack_columns(k):
        for side in range(2):
            tile = jnp.zeros((H, 128), jnp.float32)
            for f in range(F):
                at = 0 if side == 0 else W - 1
                lanes = field[k, f + 1, 8 : H + 8, (at // 128) * 128 : (at // 128) * 128 + 128]
                column = lanes[:, at % 128 : at % 128 + 1]
                tile = jnp.where(lane_h == f, column, tile)
            if side == 0:
                first_cols[...] = tile
            packed[k, side] = tile.T[:8, :]

    def halo_list(k):
        fk = field.at[k]
        mid = slice(1, F + 1)
        return (
            (packed.at[k, 0], arrived.at[k, 0], (0, -1, 0)),
            (packed.at[k, 1], arrived.at[k, 1], (0, 1, 0)),
            (packed.at[k, 0], arrived.at[k, 2], (0, -1, 1)),
            (packed.at[k, 1], arrived.at[k, 3], (0, 1, -1)),
            (fk.at[mid, H : H + 8, :], fk.at[mid, 0:8, :], (1, 0, 0)),
            (fk.at[mid, 8:16, :], fk.at[mid, H + 8 : H + 16, :], (-1, 0, 0)),
            (fk.at[F, 8:16, :], fk.at[0, H + 8 : H + 16, :], (-1, 0, 1)),
            (fk.at[1, H : H + 8, :], fk.at[F + 1, 0:8, :], (1, 0, -1)),
            (fk.at[mid, H : H + 8, 0:128], corner.at[k, 0], (1, -1, 0)),
            (fk.at[mid, 8:16, W - 128 : W], corner.at[k, 1], (-1, 1, 0)),
        ) + tuple(
            face
            for b in range(nz)
            for rows in (slice(8 + b * own, 8 + (b + 1) * own),)
            for face in (
                (fk.at[F, rows, :], fk.at[0, rows, :], (0, 0, 1)),
                (fk.at[1, rows, :], fk.at[F + 1, rows, :], (0, 0, -1)),
            )
        )

    def halo_copy(k, i, src, dst, step):
        return pltpu.make_async_remote_copy(
            src_ref=src, dst_ref=dst,
            send_sem=halo_send.at[k, i], recv_sem=halo_recv.at[k, i],
            device_id=(r + step[0], c + step[1], z + step[2]), device_id_type=MESH,
        )

    def send_halos(k, which):
        every = halo_list(k)
        for i in which:
            src, dst, step = every[i]

            @pl.when(inside(*step))
            def _(i=i, src=src, dst=dst, step=step):
                halo_copy(k, i, src, dst, step).start()

    def wait_halos(k):
        for i, (src, dst, step) in enumerate(halo_list(k)):
            @pl.when(inside(*(-s for s in step)))
            def _(i=i, src=src, dst=dst, step=step):
                halo_copy(k, i, src, dst, step).wait_recv()

    def finish_sends(k):
        for i, (src, dst, step) in enumerate(halo_list(k)):
            @pl.when(inside(*step))
            def _(i=i, src=src, dst=dst, step=step):
                halo_copy(k, i, src, dst, step).wait_send()

    def prepare_columns(k):
        tall = jnp.concatenate([arrived[k, 0], jnp.zeros((120, H), jnp.float32)], axis=0).T
        edge = jnp.concatenate([arrived[k, 2], jnp.zeros((120, H), jnp.float32)], axis=0).T
        tile = jnp.where(lane_h == 0, edge[:, F - 1 : F], pltpu.roll(tall, 1, 1))
        edge_next[8 : H + 8, :] = tile
        lane8 = lax.broadcasted_iota(jnp.int32, (8, 128), 1)
        top = jnp.zeros((8, 128), jnp.float32)
        bottom = jnp.zeros((1, 128), jnp.float32)
        for f in range(F):
            top = jnp.where(lane8 == f + 1, corner[k, 0, f][:, 0:1], top)
            bottom = jnp.where(lane8[:1] == f, corner[k, 1, f][0:1, 127:128], bottom)
        edge_next[0:8, :] = top
        edge_next[H + 8 : H + 16, :] = jnp.zeros((8, 128), jnp.float32)
        here = jnp.concatenate([arrived[k, 1], jnp.zeros((120, H), jnp.float32)], axis=0).T
        edge = jnp.concatenate([arrived[k, 3], jnp.zeros((120, H), jnp.float32)], axis=0).T
        ahead = jnp.where(lane_h == F - 1, edge[:, 0:1], pltpu.roll(here, 127, 1))
        slope0 = jnp.where((lane_h == F - 1) & (z == nz - 1), 0.0, ahead - here)
        row_h = lax.broadcasted_iota(jnp.int32, (H, 128), 0)
        below = jnp.where(row_h == H - 1, bottom, pltpu.roll(here, H - 1, 0))
        slope1 = jnp.where((row_h == H - 1) & (r == nr - 1), 0.0, below - here)
        slope2 = first_cols[...] - here
        weight = lax.rsqrt(smooth_floor + slope0 * slope0 + slope1 * slope1 + slope2 * slope2)
        edge_flux[...] = jnp.where(c == 0, 0.0, slope2 * weight)

    def sweep(k, last, base):
        @pl.loop(0, own // CHUNK)
        def _(step):
            start = pl.multiple_of(base + step * CHUNK, 8)
            R = CHUNK
            lane_t = lax.broadcasted_iota(jnp.int32, (R + 8, 128), 1)
            row_t = lax.broadcasted_iota(jnp.int32, (R + 8, W), 0) + (r * H + start - 8)
            lane_w = lax.broadcasted_iota(jnp.int32, (R + 8, W), 1)
            blocked = (row_t < 0) | (row_t >= nr * H - 1)
            columns = edge_next[pl.ds(start, R + 8), :]
            fluxes_in = edge_flux[pl.ds(start, R), :]
            now = field[k, 0, pl.ds(start, R + 16), :]
            flux0_before = None
            for f in range(-1, F):
                after = field[k, f + 2, pl.ds(start, R + 16), :]
                here = now[: R + 8]
                below = pltpu.roll(now, R + 15, 0)[: R + 8]
                ahead = after[: R + 8]
                wall = columns[:, f + 1 : f + 2]
                beyond = jnp.where(c == nc - 1, here, jnp.broadcast_to(wall, here.shape))
                right = jnp.where(lane_w == W - 1, beyond, pltpu.roll(here, W - 1, 1))
                slope0 = ahead - here
                if f == F - 1:
                    slope0 = jnp.where(z == nz - 1, 0.0, slope0)
                slope1 = jnp.where(blocked, 0.0, below - here)
                slope2 = right - here
                weight = lax.rsqrt(
                    smooth_floor + slope0 * slope0 + slope1 * slope1 + slope2 * slope2
                )
                flux0 = (slope0 * weight)[8:]
                if f < 0:
                    flux0 = jnp.where(z == 0, 0.0, flux0)
                else:
                    flux1 = jnp.where(row_t < 0, 0.0, slope1 * weight)
                    flux2 = (slope2 * weight)[8:]
                    above = pltpu.roll(flux1, 1, 0)[8:]
                    left = jnp.where(
                        lane_w[8:] == 0,
                        jnp.broadcast_to(fluxes_in[:, f : f + 1], flux2.shape),
                        pltpu.roll(flux2, 1, 1),
                    )
                    spread = flux0 - flux0_before + (flux1[8:] - above) + (flux2 - left)
                    center = here[8:]
                    at = pl.ds(start, R)
                    value = center + relax_rate * (
                        target[f, at, :] - center + smooth_weight * spread
                    )
                    if last:
                        shrunk = value - jnp.clip(value, -shrink_level, shrink_level)
                        result[f, at, :] = shrunk
                        anchor[f, at, :] = anchor[f, at, :] - shrunk
                    else:
                        field[k + 1, f + 1, pl.ds(start + 8, R), :] = value
                flux0_before = flux0
                now = after

    def products(left_of, right_of, lefts, rights, store):
        zero = jnp.zeros((8, 128), jnp.float32)

        def body(step, totals):
            rows = pl.ds(pl.multiple_of(step * 8, 8), 8)
            a = [left_of[i, rows, :] for i in lefts]
            b = [right_of[j, rows, :] for j in rights]
            out = []
            for x in range(len(lefts)):
                for y in range(len(rights)):
                    prod = a[x] * b[y]
                    total = totals[len(out)]
                    for w in range(W // 128):
                        total = total + prod[:, w * 128 : w * 128 + 128]
                    out.append(total)
            return tuple(out)

        totals = lax.fori_loop(0, H // 8, body, (zero,) * (len(lefts) * len(rights)), unroll=2)
        n = 0
        for i in lefts:
            for j in rights:
                store(i, j, jnp.sum(totals[n], axis=0, keepdims=True))
                n += 1

    loads[0].wait()
    send_halos(0, range(10, 10 + 2 * nz))
    send_halos(0, range(4, 10))
    pack_columns(0)
    send_halos(0, range(4))
    loads[1].wait()

    def store_gram(i, j, value):
        sums[j, i : i + 1, :] = value
        if i // 4 != j // 4:
            sums[i, j : j + 1, :] = value

    for i in range(0, rank, 4):
        for j in range(i, rank, 4):
            products(basis, basis, range(i, i + 4), range(j, j + 4), store_gram)

    loads[2].wait()
    loads[3].wait()

    @pl.loop(0, H // 8)
    def _(step):
        rows = pl.ds(pl.multiple_of(step * 8, 8), 8)
        totals = [None] * F
        for q in range(rank):
            plane = basis[q, rows, :]
            for f in range(F):
                term = coeff_ref[f, q] * plane
                totals[f] = term if totals[f] is None else totals[f] + term
        for f in range(F):
            lifted = dual_scale * mult[f, rows, :]
            anchor[f, rows, :] = video[f, rows, :] + lifted
            target[f, rows, :] = video[f, rows, :] - totals[f] + lifted

    def move(d):
        there = lax.rem(z + d, nz)
        rows = pl.ds(pl.multiple_of(there * own, 8), own)
        return pltpu.make_async_remote_copy(
            src_ref=anchor.at[:, rows, :], dst_ref=owned.at[pl.ds(z * F, F)],
            send_sem=move_send.at[d], recv_sem=move_recv.at[d],
            device_id=(r, c, there), device_id_type=MESH,
        )

    def take(d):
        source = lax.rem(z - d + nz, nz)
        rows = pl.ds(pl.multiple_of(z * own, 8), own)
        return pltpu.make_async_remote_copy(
            src_ref=anchor.at[:, rows, :], dst_ref=owned.at[pl.ds(source * F, F)],
            send_sem=move_send.at[d], recv_sem=move_recv.at[d],
            device_id=(r, c, source), device_id_type=MESH,
        )

    for k in range(PASSES):
        wait_halos(k)
        prepare_columns(k)
        if k < PASSES - 1:
            for b in range(nz):
                sweep(k, False, b * own)
                send_halos(k + 1, (10 + 2 * b, 11 + 2 * b))
            send_halos(k + 1, range(4, 10))
            pack_columns(k + 1)
            send_halos(k + 1, range(4))
        else:
            for d in range(1, nz + 1):
                sweep(k, True, lax.rem(z + d, nz) * own)
                if d < nz:
                    move(d).start()

    out_copy = pltpu.make_async_copy(result, shrunk_hbm, out_sems.at[0])
    out_copy.start()

    my_rows = pl.ds(pl.multiple_of(z * own, 8), own)
    keep = pltpu.make_async_copy(
        anchor.at[:, my_rows, :], owned.at[pl.ds(z * F, F)], small_sem.at[0]
    )
    keep.start()

    def store_cross(i, j, value):
        sums[rank + j, i : i + 1, :] = value

    for i in range(0, rank, 4):
        products(basis, anchor, range(i, i + 4), range(F), store_cross)

    lane_r = lax.broadcasted_iota(jnp.int32, (rank, 128), 1)
    row_r = lax.broadcasted_iota(jnp.int32, (rank, 128), 0)
    part = jnp.zeros((rank, 128), jnp.float32)
    for q in range(rank + F):
        part = jnp.where(lane_r == q, jnp.sum(sums[q], axis=1, keepdims=True), part)
    group = nr * nc
    me = r * nc + c
    parts[me] = part

    def share_part(d):
        other = lax.rem(me + d, group)
        return pltpu.make_async_remote_copy(
            src_ref=parts.at[me], dst_ref=parts.at[me],
            send_sem=part_send.at[d], recv_sem=part_recv.at[d],
            device_id=(other // nc, lax.rem(other, nc), z), device_id_type=MESH,
        )

    def take_part(d):
        other = lax.rem(me - d + group, group)
        return pltpu.make_async_remote_copy(
            src_ref=parts.at[me], dst_ref=parts.at[other],
            send_sem=part_send.at[d], recv_sem=part_recv.at[d],
            device_id=(other // nc, lax.rem(other, nc), z), device_id_type=MESH,
        )

    for d in range(1, group):
        share_part(d).start()
    for d in range(1, group):
        take_part(d).wait_recv()
    total = parts[0]
    for i in range(1, group):
        total = total + parts[i]
    pixel_ridge = ridge_share * H * W * group
    diagonal = lane_r == row_r
    before = jnp.zeros((rank, 128), jnp.float32)
    for q in range(rank):
        for f in range(F):
            before = jnp.where((row_r == q) & (lane_r == rank + f), coeff_ref[f, q], before)
    total = total + pixel_ridge * (jnp.where(diagonal, 1.0, 0.0) + before)
    solved = eliminate(total, rank)
    shares[z] = solved
    rows_out[...] = solved

    def share_rows(d):
        return pltpu.make_async_remote_copy(
            src_ref=shares.at[z], dst_ref=shares.at[z],
            send_sem=share_send.at[d], recv_sem=share_recv.at[d],
            device_id=(r, c, lax.rem(z + d, nz)), device_id_type=MESH,
        )

    def take_rows(d):
        source = lax.rem(z - d + nz, nz)
        return pltpu.make_async_remote_copy(
            src_ref=shares.at[z], dst_ref=shares.at[source],
            send_sem=share_send.at[d], recv_sem=share_recv.at[d],
            device_id=(r, c, source), device_id_type=MESH,
        )

    for d in range(1, nz):
        share_rows(d).start()
    for d in range(1, nz):
        take_rows(d).wait_recv()
    frames = F * nz
    wide = jnp.zeros((rank, 128), jnp.float32)
    for i in range(nz):
        placed = shares[i] if i == 0 else pltpu.roll(shares[i], i * F, 1)
        wide = jnp.where(
            (lane_r >= rank + i * F) & (lane_r < rank + (i + 1) * F), placed, wide
        )
    square[...] = jnp.zeros_like(square)
    square[0:rank, :] = wide
    gram = lax.dot_general(
        wide, square[...], (((1,), (1,)), ((), ())),
        precision=lax.Precision.HIGHEST, preferred_element_type=jnp.float32,
    )
    frame_ridge = ridge_share * frames
    system = jnp.where(diagonal, gram + frame_ridge, gram) + wide
    system = system + jnp.where(lane_r == row_r + rank + frames, frame_ridge, 0.0)
    table[...] = eliminate(system, rank)
    to_scalar = pltpu.make_async_copy(table, table_smem, small_sem.at[1])
    to_scalar.start()
    to_scalar.wait()
    keep.wait()
    for d in range(1, nz):
        take(d).wait_recv()

    @pl.loop(0, own // 8)
    def _(step):
        rows = pl.ds(pl.multiple_of(step * 8, 8), 8)
        old = pl.ds(pl.multiple_of(z * own + step * 8, 8), 8)

        for half in range(0, rank, 8):
            totals = [None] * 8
            for f in range(frames + rank):
                plane = owned[f, rows, :] if f < frames else basis[f - frames, old, :]
                for q in range(8):
                    term = table_smem[half + q, rank + f] * plane
                    totals[q] = term if totals[q] is None else totals[q] + term
            for q in range(8):
                target_rows = totals[q]
                barrier_own[half + q, rows, :] = target_rows

    last_copy = pltpu.make_async_copy(barrier_own, new_basis_hbm, out_sems.at[1])
    last_copy.start()
    for k in range(PASSES):
        finish_sends(k)
    for d in range(1, nz):
        move(d).wait_send()
        share_rows(d).wait_send()
    for d in range(1, group):
        share_part(d).wait_send()
    out_copy.wait()
    last_copy.wait()


def whole_kernel(video, multiplier, foreground, basis, coefficients):
    F, H, W = video.shape
    rank = basis.shape[0]
    nr, nc, nz = (lax.axis_size(name) for name in ("row", "col", "frame"))
    f32 = jnp.float32
    own = H // nz
    group = nr * nc
    vmem = pltpu.VMEM
    dma = pltpu.SemaphoreType.DMA
    shrunk, rows, new_basis = pl.pallas_call(
        functools.partial(kernel, (F, H, W, rank, nr, nc, nz)),
        out_shape=(
            jax.ShapeDtypeStruct((F, H, W), f32),
            jax.ShapeDtypeStruct((rank, 128), f32),
            jax.ShapeDtypeStruct((rank, own, W), f32),
        ),
        in_specs=[pl.BlockSpec(memory_space=pltpu.SMEM)]
        + [pl.BlockSpec(memory_space=pl.ANY)] * 4,
        out_specs=(
            pl.BlockSpec(memory_space=pl.ANY),
            pl.BlockSpec(memory_space=pltpu.VMEM),
            pl.BlockSpec(memory_space=pl.ANY),
        ),
        scratch_shapes=[
            vmem((PASSES, F + 2, H + 16, W), f32),
            vmem((F, H, W), f32),
            vmem((F, H, W), f32),
            vmem((rank, H, W), f32),
            vmem((F, H, W), f32),
            vmem((F, H, W), f32),
            vmem((F, H, W), f32),
            vmem((F * nz, own, W), f32),
            vmem((PASSES, 2, 8, H), f32),
            vmem((PASSES, 4, 8, H), f32),
            vmem((PASSES, 2, F, 8, 128), f32),
            vmem((H + 16, 128), f32),
            vmem((H, 128), f32),
            vmem((H, 128), f32),
            vmem((rank + F, rank, 128), f32),
            vmem((group, rank, 128), f32),
            vmem((nz, rank, 128), f32),
            vmem((128, 128), f32),
            vmem((rank, 128), f32),
            pltpu.SMEM((rank, 128), f32),
            dma((4,)),
            dma((2,)),
            dma((PASSES, 10 + 2 * nz)),
            dma((PASSES, 10 + 2 * nz)),
            dma((group,)),
            dma((group,)),
            dma((nz,)),
            dma((nz,)),
            dma((nz,)),
            dma((nz,)),
            dma((2,)),
            vmem((rank, own, W), f32),
        ],
        compiler_params=pltpu.CompilerParams(
            collective_id=0, has_side_effects=True, vmem_limit_bytes=60 * 1024 * 1024
        ),
    )(coefficients, video, multiplier, foreground, basis)
    return (shrunk, rows[:, rank : rank + F].T, new_basis)


def body(video, multiplier, foreground, basis, coefficients):
    F, H, W = video.shape
    rank = basis.shape[0]
    nz = lax.axis_size("frame")
    fits = (
        H % nz == 0 and (H // nz) % 8 == 0 and (H // nz) % CHUNK == 0 and W % 128 == 0
        and F <= 8 and rank % 8 == 0 and 2 * rank + F * nz <= 128
    )
    run = whole_kernel if fits else local
    return run(video, multiplier, foreground, basis, coefficients)


def solution(mesh):
    placed = (
        P("frame", "row", "col"),
        P("frame", "row", "col"),
        P("frame", "row", "col"),
        P(None, "row", "col"),
        P("frame", None),
    )
    return jax.shard_map(
        body,
        mesh=mesh,
        in_specs=placed,
        out_specs=(P("frame", "row", "col"), P("frame", None), P(None, ("row", "frame"), "col")),
        check_vma=False,
    )
```

profile of v0, /device:TPU:0, one launch (start us, length us, event | category | flops | bytes accessed | tf_op | source)
XLA Modules:
  0.0 79.9 jit_solution(1259226077281428121)
XLA Ops:
  0.6 74.4 %shard_map.76 = (f32[4,288,256]{2,1,0:T(8,128)}, f32[16,128]{1,0:T(8,128)}, f32[16,72,256]{2,1,0:T(8,128)}) custom-call(f32[4,16]{1,0:T(4,128)} %coeff_ref.1, f32[4,288,256]{2,1,0:T(8,128)} %video_hbm.1, f32[4,288,256]{2,1,0:T(8,128)} %mult_hbm.1, f32[4,288,256]{2,1,0:T(8,128)} %fore_hbm.1, f32[16,288,256]{2,1,0:T(8,128)} %basis_hbm.1), custom_call_target="tpu_custom_call" | custom-call | tf_op jit(solution)/shard_map/pallas_call | solution.py:574
  75.0 0.8 slice_bitcast_fusion
  75.8 0.7 copy.8
  76.4 0.0 copy-start
  76.5 2.5 %copy.11 = f32[4,288,256]{2,1,0:T(8,128)} copy(f32[4,288,256]{2,1,0:T(8,128)} %get-tuple-element.15) | data formatting | bytes 2359296
  78.9 0.0 copy-done
  78.9 1.0 %copy.12 = f32[16,72,256]{2,1,0:T(8,128)} copy(f32[16,72,256]{2,1,0:T(8,128)S(1)} %copy-done) | data formatting | bytes 2359296
Async XLA Ops:
  76.4 2.5 %copy-start = (f32[16,72,256]{2,1,0:T(8,128)S(1)}, f32[16,72,256]{2,1,0:T(8,128)}, u32[]{:S(2)}) copy-start(f32[16,72,256]{2,1,0:T(8,128)} %get-tuple-element.17) | copy-start | bytes 3538948
where the time goes:
time: 80.2 us; the launch traced here: 79.9 us
  Pallas kernels  74.4 us (93%)
  local copies, waits for them, and re-layouts  4.9 us (6%)
    pallas_call x1, Pallas kernels, whole_kernel(): pl.pallas_call(functools.partial(kernel, (F, H, W, rank, nr, nc, nz)), ou...  74.4 us
    unnamed x5, local copies, waits for them, and re-layouts  4.13 us

commit v1 on v0

--- a/solution.py
+++ b/solution.py
@@ -135,19 +135,21 @@
 
 
 def kernel(
-    sizes, coeff_ref, video_hbm, mult_hbm, fore_hbm, basis_hbm,
-    shrunk_hbm, rows_out, new_basis_hbm,
-    field, video, mult, basis, anchor, target, result, owned,
+    sizes, coeff_hbm, video_hbm, mult_hbm, fore_hbm, basis_hbm,
+    result, coeff_out, fresh,
+    field0, field1, field2, video, mult, basis, anchor, target, owned,
     packed, arrived, corner, edge_next, edge_flux, first_cols,
-    sums, parts, shares, square, table, table_smem,
-    in_sems, out_sems, halo_send, halo_recv, part_send, part_recv,
-    share_send, share_recv, move_send, move_recv, small_sem, barrier_own,
+    cross, sums, parts, shares, square, table, coeff_ref, table_smem,
+    in_sems, halo_send, halo_recv, part_send, part_recv,
+    share_send, share_recv, move_send, move_recv, small_sem,
 ):
+    field = (field0, field1, field2)
     F, H, W, rank, nr, nc, nz = sizes
     r = lax.axis_index("row")
     c = lax.axis_index("col")
     z = lax.axis_index("frame")
     own = H // nz
+    pieces = own // CHUNK
 
     def inside(dr, dc, dz):
         ok = None
@@ -156,19 +158,6 @@
                 test = (at + step >= 0) & (at + step < count)
                 ok = test if ok is None else ok & test
         return ok
-
-    loads = []
-    for i, (src, dst) in enumerate(
-        (
-            (fore_hbm, field.at[0, 1 : F + 1, 8 : H + 8, :]),
-            (basis_hbm, basis),
-            (video_hbm, video),
-            (mult_hbm, mult),
-        )
-    ):
-        copy = pltpu.make_async_copy(src, dst, in_sems.at[i])
-        copy.start()
-        loads.append(copy)
 
     barrier = pltpu.get_barrier_semaphore()
     for d in range(1, nr * nc):
@@ -193,6 +182,20 @@
     expected = jnp.int32(nr * nc - 1 + nz - 1)
     for step in diagonals:
         expected = expected + inside(*step).astype(jnp.int32)
+    loads = []
+    for i, (src, dst) in enumerate(
+        (
+            (fore_hbm, field0.at[1 : F + 1, 8 : H + 8, :]),
+            (coeff_hbm, coeff_ref),
+            (video_hbm, video),
+            (mult_hbm, mult),
+            (basis_hbm, basis),
+        )
+    ):
+        copy = pltpu.make_async_copy(src, dst, in_sems.at[i])
+        copy.start()
+        loads.append(copy)
+
     pl.semaphore_wait(barrier, expected)
 
     lane_h = lax.broadcasted_iota(jnp.int32, (H, 128), 1)
@@ -202,7 +205,7 @@
             tile = jnp.zeros((H, 128), jnp.float32)
             for f in range(F):
                 at = 0 if side == 0 else W - 1
-                lanes = field[k, f + 1, 8 : H + 8, (at // 128) * 128 : (at // 128) * 128 + 128]
+                lanes = field[k][f + 1, 8 : H + 8, (at // 128) * 128 : (at // 128) * 128 + 128]
                 column = lanes[:, at % 128 : at % 128 + 1]
                 tile = jnp.where(lane_h == f, column, tile)
             if side == 0:
@@ -210,17 +213,17 @@
             packed[k, side] = tile.T[:8, :]
 
     def halo_list(k):
-        fk = field.at[k]
+        fk = field[k]
         mid = slice(1, F + 1)
         return (
             (packed.at[k, 0], arrived.at[k, 0], (0, -1, 0)),
             (packed.at[k, 1], arrived.at[k, 1], (0, 1, 0)),
-            (packed.at[k, 0], arrived.at[k, 2], (0, -1, 1)),
-            (packed.at[k, 1], arrived.at[k, 3], (0, 1, -1)),
+            (packed.at[k, 0, F - 1 : F], arrived.at[k, 2, F - 1 : F], (0, -1, 1)),
+            (packed.at[k, 1, 0:1], arrived.at[k, 3, 0:1], (0, 1, -1)),
             (fk.at[mid, H : H + 8, :], fk.at[mid, 0:8, :], (1, 0, 0)),
             (fk.at[mid, 8:16, :], fk.at[mid, H + 8 : H + 16, :], (-1, 0, 0)),
-            (fk.at[F, 8:16, :], fk.at[0, H + 8 : H + 16, :], (-1, 0, 1)),
-            (fk.at[1, H : H + 8, :], fk.at[F + 1, 0:8, :], (1, 0, -1)),
+            (fk.at[F, 8:9, :], fk.at[0, H + 8 : H + 9, :], (-1, 0, 1)),
+            (fk.at[1, H + 7 : H + 8, :], fk.at[F + 1, 7:8, :], (1, 0, -1)),
             (fk.at[mid, H : H + 8, 0:128], corner.at[k, 0], (1, -1, 0)),
             (fk.at[mid, 8:16, W - 128 : W], corner.at[k, 1], (-1, 1, 0)),
         ) + tuple(
@@ -249,8 +252,11 @@
             def _(i=i, src=src, dst=dst, step=step):
                 halo_copy(k, i, src, dst, step).start()
 
-    def wait_halos(k):
-        for i, (src, dst, step) in enumerate(halo_list(k)):
+    def wait_halos(k, which):
+        every = halo_list(k)
+        for i in which:
+            src, dst, step = every[i]
+
             @pl.when(inside(*(-s for s in step)))
             def _(i=i, src=src, dst=dst, step=step):
                 halo_copy(k, i, src, dst, step).wait_recv()
@@ -285,10 +291,10 @@
         weight = lax.rsqrt(smooth_floor + slope0 * slope0 + slope1 * slope1 + slope2 * slope2)
         edge_flux[...] = jnp.where(c == 0, 0.0, slope2 * weight)
 
-    def sweep(k, last, base):
-        @pl.loop(0, own // CHUNK)
+    def sweep(k, last, block):
+        @pl.loop(0, pieces)
         def _(step):
-            start = pl.multiple_of(base + step * CHUNK, 8)
+            start = pl.multiple_of(block * own + step * CHUNK, 8)
             R = CHUNK
             lane_t = lax.broadcasted_iota(jnp.int32, (R + 8, 128), 1)
             row_t = lax.broadcasted_iota(jnp.int32, (R + 8, W), 0) + (r * H + start - 8)
@@ -296,10 +302,10 @@
             blocked = (row_t < 0) | (row_t >= nr * H - 1)
             columns = edge_next[pl.ds(start, R + 8), :]
             fluxes_in = edge_flux[pl.ds(start, R), :]
-            now = field[k, 0, pl.ds(start, R + 16), :]
+            now = field[k][0, pl.ds(start, R + 16), :]
             flux0_before = None
             for f in range(-1, F):
-                after = field[k, f + 2, pl.ds(start, R + 16), :]
+                after = field[k][f + 2, pl.ds(start, R + 16), :]
                 here = now[: R + 8]
                 below = pltpu.roll(now, R + 15, 0)[: R + 8]
                 ahead = after[: R + 8]
@@ -337,15 +343,17 @@
                         result[f, at, :] = shrunk
                         anchor[f, at, :] = anchor[f, at, :] - shrunk
                     else:
-                        field[k + 1, f + 1, pl.ds(start + 8, R), :] = value
+                        field[k + 1][f + 1, pl.ds(start + 8, R), :] = value
                 flux0_before = flux0
                 now = after
-
-    def products(left_of, right_of, lefts, rights, store):
-        zero = jnp.zeros((8, 128), jnp.float32)
-
+            if last:
+                @pl.when((z != block) & ~held(block))
+                def _():
+                    move(block, step).start()
+
+    def products(left_of, right_of, lefts, rights, first, count, start, store):
         def body(step, totals):
-            rows = pl.ds(pl.multiple_of(step * 8, 8), 8)
+            rows = pl.ds(pl.multiple_of(first + step * 8, 8), 8)
             a = [left_of[i, rows, :] for i in lefts]
             b = [right_of[j, rows, :] for j in rights]
             out = []
@@ -358,31 +366,67 @@
                     out.append(total)
             return tuple(out)
 
-        totals = lax.fori_loop(0, H // 8, body, (zero,) * (len(lefts) * len(rights)), unroll=2)
+        totals = lax.fori_loop(
+            0, count // 8, body, tuple(start(i, j) for i in lefts for j in rights), unroll=2 if count % 16 == 0 else 1
+        )
         n = 0
         for i in lefts:
             for j in rights:
-                store(i, j, jnp.sum(totals[n], axis=0, keepdims=True))
+                store(i, j, totals[n])
                 n += 1
 
+    def held(block):
+        right = (z < block) & (block == nz - 1) & (nz - 1 - z >= 2)
+        left = (z > block) & (block == z - 1) & (z >= 2)
+        return right | left
+
+    def move(block, piece):
+        rows = pl.ds(pl.multiple_of(block * own + piece * CHUNK, 8), CHUNK)
+        spot = pl.ds(pl.multiple_of(piece * CHUNK, 8), CHUNK)
+        return pltpu.make_async_remote_copy(
+            src_ref=anchor.at[:, rows, :], dst_ref=owned.at[pl.ds(z * F, F), spot, :],
+            send_sem=move_send.at[block, piece], recv_sem=move_recv.at[z, piece],
+            device_id=(r, c, block), device_id_type=MESH,
+        )
+
+    def take(source, piece):
+        rows = pl.ds(pl.multiple_of(z * own + piece * CHUNK, 8), CHUNK)
+        spot = pl.ds(pl.multiple_of(piece * CHUNK, 8), CHUNK)
+        return pltpu.make_async_remote_copy(
+            src_ref=anchor.at[:, rows, :], dst_ref=owned.at[pl.ds(source * F, F), spot, :],
+            send_sem=move_send.at[source, piece], recv_sem=move_recv.at[source, piece],
+            device_id=(r, c, source), device_id_type=MESH,
+        )
+
     loads[0].wait()
-    send_halos(0, range(10, 10 + 2 * nz))
+    send_halos(0, (10, 11))
     send_halos(0, range(4, 10))
     pack_columns(0)
     send_halos(0, range(4))
-    loads[1].wait()
+    send_halos(0, range(12, 10 + 2 * nz))
+    zero_tile = jnp.zeros((8, 128), jnp.float32)
 
     def store_gram(i, j, value):
-        sums[j, i : i + 1, :] = value
+        row = jnp.sum(value, axis=0, keepdims=True)
+        sums[j, i : i + 1, :] = row
         if i // 4 != j // 4:
-            sums[i, j : j + 1, :] = value
-
-    for i in range(0, rank, 4):
-        for j in range(i, rank, 4):
-            products(basis, basis, range(i, i + 4), range(j, j + 4), store_gram)
-
-    loads[2].wait()
-    loads[3].wait()
+            sums[i, j : j + 1, :] = row
+
+    gram_blocks = [(i, j) for i in range(0, rank, 4) for j in range(i, rank, 4)]
+
+    def gram_part(which):
+        for n in which:
+            i, j = gram_blocks[n]
+            products(
+                basis, basis, range(i, i + 4), range(j, j + 4), 0, H,
+                lambda i, j: zero_tile, store_gram,
+            )
+
+    def store_cross(i, j, value):
+        cross[j, i] = value
+
+    for load in loads[1:]:
+        load.wait()
 
     @pl.loop(0, H // 8)
     def _(step):
@@ -398,54 +442,38 @@
             anchor[f, rows, :] = video[f, rows, :] + lifted
             target[f, rows, :] = video[f, rows, :] - totals[f] + lifted
 
-    def move(d):
-        there = lax.rem(z + d, nz)
-        rows = pl.ds(pl.multiple_of(there * own, 8), own)
-        return pltpu.make_async_remote_copy(
-            src_ref=anchor.at[:, rows, :], dst_ref=owned.at[pl.ds(z * F, F)],
-            send_sem=move_send.at[d], recv_sem=move_recv.at[d],
-            device_id=(r, c, there), device_id_type=MESH,
-        )
-
-    def take(d):
-        source = lax.rem(z - d + nz, nz)
-        rows = pl.ds(pl.multiple_of(z * own, 8), own)
-        return pltpu.make_async_remote_copy(
-            src_ref=anchor.at[:, rows, :], dst_ref=owned.at[pl.ds(source * F, F)],
-            send_sem=move_send.at[d], recv_sem=move_recv.at[d],
-            device_id=(r, c, source), device_id_type=MESH,
-        )
-
+    count = len(gram_blocks)
+    cuts = (0, count * 2 // 5, count * 7 // 10, count)
+    gram_part(range(cuts[0], cuts[1]))
     for k in range(PASSES):
-        wait_halos(k)
+        last = k == PASSES - 1
+        wait_halos(k, range(10))
         prepare_columns(k)
-        if k < PASSES - 1:
-            for b in range(nz):
-                sweep(k, False, b * own)
+        for b in range(nz):
+            if b == 0:
+                wait_halos(k, (10, 11))
+            if b + 1 < nz:
+                wait_halos(k, (12 + 2 * b, 13 + 2 * b))
+            sweep(k, last, b)
+            if last:
+                for i in range(0, rank, 4):
+                    products(
+                        basis, anchor, range(i, i + 4), range(F), b * own, own,
+                        (lambda i, j: zero_tile) if b == 0 else (lambda i, j: cross[j, i]),
+                        store_cross,
+                    )
+            elif 2 * b < nz:
                 send_halos(k + 1, (10 + 2 * b, 11 + 2 * b))
+        if not last:
             send_halos(k + 1, range(4, 10))
             pack_columns(k + 1)
             send_halos(k + 1, range(4))
-        else:
-            for d in range(1, nz + 1):
-                sweep(k, True, lax.rem(z + d, nz) * own)
-                if d < nz:
-                    move(d).start()
-
-    out_copy = pltpu.make_async_copy(result, shrunk_hbm, out_sems.at[0])
-    out_copy.start()
-
-    my_rows = pl.ds(pl.multiple_of(z * own, 8), own)
-    keep = pltpu.make_async_copy(
-        anchor.at[:, my_rows, :], owned.at[pl.ds(z * F, F)], small_sem.at[0]
-    )
-    keep.start()
-
-    def store_cross(i, j, value):
-        sums[rank + j, i : i + 1, :] = value
-
-    for i in range(0, rank, 4):
-        products(basis, anchor, range(i, i + 4), range(F), store_cross)
+            send_halos(k + 1, range(10 + 2 * ((nz + 1) // 2), 10 + 2 * nz))
+            gram_part(range(cuts[k + 1], cuts[k + 2]))
+
+    for j in range(F):
+        for i in range(rank):
+            sums[rank + j, i : i + 1, :] = jnp.sum(cross[j, i], axis=0, keepdims=True)
 
     lane_r = lax.broadcasted_iota(jnp.int32, (rank, 128), 1)
     row_r = lax.broadcasted_iota(jnp.int32, (rank, 128), 0)
@@ -474,21 +502,20 @@
 
     for d in range(1, group):
         share_part(d).start()
-    for d in range(1, group):
-        take_part(d).wait_recv()
-    total = parts[0]
-    for i in range(1, group):
-        total = total + parts[i]
     pixel_ridge = ridge_share * H * W * group
     diagonal = lane_r == row_r
     before = jnp.zeros((rank, 128), jnp.float32)
     for q in range(rank):
         for f in range(F):
             before = jnp.where((row_r == q) & (lane_r == rank + f), coeff_ref[f, q], before)
+    for d in range(1, group):
+        take_part(d).wait_recv()
+    total = parts[0]
+    for i in range(1, group):
+        total = total + parts[i]
     total = total + pixel_ridge * (jnp.where(diagonal, 1.0, 0.0) + before)
     solved = eliminate(total, rank)
     shares[z] = solved
-    rows_out[...] = solved
 
     def share_rows(d):
         return pltpu.make_async_remote_copy(
@@ -507,6 +534,14 @@
 
     for d in range(1, nz):
         share_rows(d).start()
+    for b in range(nz):
+        @pl.when((z != b) & held(b))
+        def _(b=b):
+            for p in range(pieces):
+                move(b, p).start()
+    square[...] = jnp.zeros_like(square)
+    square[0:rank, :] = solved
+    coeff_out[...] = square[...].T[rank : rank + F, 0:rank]
     for d in range(1, nz):
         take_rows(d).wait_recv()
     frames = F * nz
@@ -516,7 +551,6 @@
         wide = jnp.where(
             (lane_r >= rank + i * F) & (lane_r < rank + (i + 1) * F), placed, wide
         )
-    square[...] = jnp.zeros_like(square)
     square[0:rank, :] = wide
     gram = lax.dot_general(
         wide, square[...], (((1,), (1,)), ((), ())),
@@ -529,37 +563,64 @@
     to_scalar = pltpu.make_async_copy(table, table_smem, small_sem.at[1])
     to_scalar.start()
     to_scalar.wait()
-    keep.wait()
-    for d in range(1, nz):
-        take(d).wait_recv()
+    my_base = z * own
 
     @pl.loop(0, own // 8)
     def _(step):
         rows = pl.ds(pl.multiple_of(step * 8, 8), 8)
-        old = pl.ds(pl.multiple_of(z * own + step * 8, 8), 8)
-
+        old = pl.ds(pl.multiple_of(my_base + step * 8, 8), 8)
         for half in range(0, rank, 8):
             totals = [None] * 8
-            for f in range(frames + rank):
-                plane = owned[f, rows, :] if f < frames else basis[f - frames, old, :]
+            for f in range(F + rank):
+                plane = anchor[f, old, :] if f < F else basis[f - F, old, :]
+                place = rank + z * F + f if f < F else rank + frames + f - F
                 for q in range(8):
-                    term = table_smem[half + q, rank + f] * plane
+                    term = table_smem[half + q, place] * plane
                     totals[q] = term if totals[q] is None else totals[q] + term
             for q in range(8):
-                target_rows = totals[q]
-                barrier_own[half + q, rows, :] = target_rows
-
-    last_copy = pltpu.make_async_copy(barrier_own, new_basis_hbm, out_sems.at[1])
-    last_copy.start()
+                fresh[half + q, rows, :] = totals[q]
+
+    for n in range(nz - 1):
+        near = n + (n >= z).astype(jnp.int32)
+        far = nz - 1 - (n + (n >= nz - 1 - z).astype(jnp.int32))
+        source = jnp.where(2 * z < nz, near, far)
+
+        @pl.loop(0, pieces)
+        def _(piece, source=source):
+            take(source, piece).wait_recv()
+            for step in range(CHUNK // 8):
+                rows = pl.ds(pl.multiple_of(piece * CHUNK + step * 8, 8), 8)
+                planes = [owned[source * F + f, rows, :] for f in range(F)]
+                for q in range(rank):
+                    value = fresh[q, rows, :]
+                    for f in range(F):
+                        value = value + table_smem[q, rank + source * F + f] * planes[f]
+                    fresh[q, rows, :] = value
+
     for k in range(PASSES):
         finish_sends(k)
+    for b in range(nz):
+        @pl.when(z != b)
+        def _(b=b):
+            for p in range(pieces):
+                move(b, p).wait_send()
     for d in range(1, nz):
-        move(d).wait_send()
         share_rows(d).wait_send()
     for d in range(1, group):
         share_part(d).wait_send()
-    out_copy.wait()
-    last_copy.wait()
+
+
+def deliver(shrunk, coeff, fresh, shrunk_hbm, coeff_hbm, fresh_hbm, sems):
+    copies = [
+        pltpu.make_async_copy(source, place, sems.at[i])
+        for i, (source, place) in enumerate(
+            ((fresh, fresh_hbm), (shrunk, shrunk_hbm), (coeff, coeff_hbm))
+        )
+    ]
+    for copy in copies:
+        copy.start()
+    for copy in copies:
+        copy.wait()
 
 
 def whole_kernel(video, multiplier, foreground, basis, coefficients):
@@ -571,26 +632,19 @@
     group = nr * nc
     vmem = pltpu.VMEM
     dma = pltpu.SemaphoreType.DMA
-    shrunk, rows, new_basis = pl.pallas_call(
+    pieces = own // CHUNK
+    hbm = pl.BlockSpec(memory_space=pl.ANY)
+    on_chip = pl.BlockSpec(memory_space=pltpu.VMEM)
+    found = pl.pallas_call(
         functools.partial(kernel, (F, H, W, rank, nr, nc, nz)),
-        out_shape=(
-            jax.ShapeDtypeStruct((F, H, W), f32),
-            jax.ShapeDtypeStruct((rank, 128), f32),
-            jax.ShapeDtypeStruct((rank, own, W), f32),
-        ),
-        in_specs=[pl.BlockSpec(memory_space=pltpu.SMEM)]
-        + [pl.BlockSpec(memory_space=pl.ANY)] * 4,
-        out_specs=(
-            pl.BlockSpec(memory_space=pl.ANY),
-            pl.BlockSpec(memory_space=pltpu.VMEM),
-            pl.BlockSpec(memory_space=pl.ANY),
-        ),
-        scratch_shapes=[
-            vmem((PASSES, F + 2, H + 16, W), f32),
+        out_shape=(vmem((F, H, W), f32), vmem((F, rank), f32), vmem((rank, own, W), f32)),
+        in_specs=[hbm] * 5,
+        out_specs=[on_chip] * 3,
+        scratch_shapes=[vmem((F + 2, H + 16, W), f32)] * PASSES
+        + [
             vmem((F, H, W), f32),
             vmem((F, H, W), f32),
             vmem((rank, H, W), f32),
-            vmem((F, H, W), f32),
             vmem((F, H, W), f32),
             vmem((F, H, W), f32),
             vmem((F * nz, own, W), f32),
@@ -600,30 +654,45 @@
             vmem((H + 16, 128), f32),
             vmem((H, 128), f32),
             vmem((H, 128), f32),
+            vmem((F, rank, 8, 128), f32),
             vmem((rank + F, rank, 128), f32),
             vmem((group, rank, 128), f32),
             vmem((nz, rank, 128), f32),
             vmem((128, 128), f32),
             vmem((rank, 128), f32),
+            pltpu.SMEM((F, rank), f32),
             pltpu.SMEM((rank, 128), f32),
-            dma((4,)),
-            dma((2,)),
+            dma((5,)),
             dma((PASSES, 10 + 2 * nz)),
             dma((PASSES, 10 + 2 * nz)),
             dma((group,)),
             dma((group,)),
             dma((nz,)),
             dma((nz,)),
-            dma((nz,)),
-            dma((nz,)),
+            dma((nz, pieces)),
+            dma((nz, pieces)),
             dma((2,)),
-            vmem((rank, own, W), f32),
         ],
         compiler_params=pltpu.CompilerParams(
-            collective_id=0, has_side_effects=True, vmem_limit_bytes=60 * 1024 * 1024
+            collective_id=0, has_side_effects=True, vmem_limit_bytes=32 * 1024 * 1024
         ),
-    )(coefficients, video, multiplier, foreground, basis)
-    return (shrunk, rows[:, rank : rank + F].T, new_basis)
+    )(
+        *(
+            pltpu.with_memory_space_constraint(x, pltpu.HBM)
+            for x in (coefficients, video, multiplier, foreground, basis)
+        )
+    )
+    return pl.pallas_call(
+        deliver,
+        out_shape=(
+            jax.ShapeDtypeStruct((F, H, W), f32),
+            jax.ShapeDtypeStruct((F, rank), f32),
+            jax.ShapeDtypeStruct((rank, own, W), f32),
+        ),
+        in_specs=[on_chip] * 3,
+        out_specs=[hbm] * 3,
+        scratch_shapes=[dma((3,))],
+    )(*(pltpu.with_memory_space_constraint(x, pltpu.VMEM) for x in found))
 
 
 def body(video, multiplier, foreground, basis, coefficients):

time: 80.2 us -> 61.5 us (0.77)
  the two profiles are of different devices: /device:TPU:0 before, /device:TPU:30 now
where the time goes in v1:
time: 61.5 us; the launch traced here: 61.3 us
  Pallas kernels  60.7 us (99%)
  between operations  0.64 us (1%)
    pallas_call x1, Pallas kernels, whole_kernel(): pl.pallas_call(functools.partial(kernel, (F, H, W, rank, nr, nc, nz)), ou...  59.3 us
    pallas_call x1, Pallas kernels, whole_kernel(): pl.pallas_call(deliver, out_shape=(jax.ShapeDtypeStruct((F, H, W), f32),...  1.43 us

profile of v1, /device:TPU:30, one launch (start us, length us, event | category | flops | bytes accessed | tf_op | source)
XLA Modules:
  0.0 61.3 jit_solution(17887271031898105409)
XLA Ops:
  0.6 59.3 %shard_map.76 = (f32[4,288,256]{2,1,0:T(8,128)S(1)}, f32[4,16]{1,0:T(4,128)S(1)}, f32[16,72,256]{2,1,0:T(8,128)S(1)}) custom-call(f32[4,16]{1,0:T(4,128)} %coeff_hbm.1, f32[4,288,256]{2,1,0:T(8,128)} %video_hbm.1, f32[4,288,256]{2,1,0:T(8,128)} %mult_hbm.1, f32[4,288,256]{2,1,0:T(8,128)} %fore_hbm.1, f32[16,288,256]{2,1,0:T(8,128)} %basis_hbm.1), custom_call_target="tpu_custom_call" | custom-call | tf_op jit(solution)/shard_map/pallas_call | solution.py:638
  59.9 1.4 %shard_map.77 = (f32[4,288,256]{2,1,0:T(8,128)}, f32[4,16]{1,0:T(4,128)}, f32[16,72,256]{2,1,0:T(8,128)}) custom-call(f32[4,288,256]{2,1,0:T(8,128)S(1)} %get-tuple-element.6.shrunk, f32[4,16]{1,0:T(4,128)S(1)} %get-tuple-element.7.coeff, f32[16,72,256]{2,1,0:T(8,128)S(1)} %get-tuple-element.8.fresh), custom_call_target="tpu_custom_call" | custom-call | tf_op jit(solution)/shard_map/pallas_call | solution.py:685

commit v2 on v1

--- a/solution.py
+++ b/solution.py
@@ -138,10 +138,10 @@
     sizes, coeff_hbm, video_hbm, mult_hbm, fore_hbm, basis_hbm,
     result, coeff_out, fresh,
     field0, field1, field2, video, mult, basis, anchor, target, owned,
-    packed, arrived, corner, edge_next, edge_flux, first_cols,
-    cross, sums, parts, shares, square, table, coeff_ref, table_smem,
+    packed, arrived, corner, edge_next, edge_flux, first_cols, left_now, left_next,
+    cross, sums, grams, parts, shares, square, table, coeff_ref, table_smem,
     in_sems, halo_send, halo_recv, part_send, part_recv,
-    share_send, share_recv, move_send, move_recv, small_sem,
+    gram_send, gram_recv, share_send, share_recv, move_send, move_recv, small_sem,
 ):
     field = (field0, field1, field2)
     F, H, W, rank, nr, nc, nz = sizes
@@ -150,6 +150,19 @@
     z = lax.axis_index("frame")
     own = H // nz
     pieces = own // CHUNK
+    half = H // 2
+    flip = lax.rem(r, 2)
+
+    steps = H // CHUNK
+
+    def chunk_at(step):
+        return step + flip * (steps - 1 - 2 * step)
+
+    def rows_at(step, offset=0):
+        return pl.ds(pl.multiple_of(offset + chunk_at(step) * CHUNK, 8), CHUNK)
+
+    def half_start(h):
+        return pl.multiple_of((h + flip * (1 - 2 * h)) * half, 8)
 
     def inside(dr, dc, dz):
         ok = None
@@ -158,6 +171,28 @@
                 test = (at + step >= 0) & (at + step < count)
                 ok = test if ok is None else ok & test
         return ok
+
+    halves = [pl.ds(half_start(h), half) for h in range(2)]
+    loads = [
+        pltpu.make_async_copy(src, dst, in_sems.at[i])
+        for i, (src, dst) in enumerate(
+            [
+                (
+                    fore_hbm.at[:, halves[h], :],
+                    field0.at[1 : F + 1, pl.ds(pl.multiple_of(half_start(h) + 8, 8), half), :],
+                )
+                for h in range(2)
+            ]
+            + [(coeff_hbm, coeff_ref)]
+            + [
+                (src.at[:, rows, :], dst.at[:, rows, :])
+                for rows in halves
+                for src, dst in ((video_hbm, video), (mult_hbm, mult), (basis_hbm, basis))
+            ]
+        )
+    ]
+    for load in loads[:2]:
+        load.start()
 
     barrier = pltpu.get_barrier_semaphore()
     for d in range(1, nr * nc):
@@ -182,58 +217,48 @@
     expected = jnp.int32(nr * nc - 1 + nz - 1)
     for step in diagonals:
         expected = expected + inside(*step).astype(jnp.int32)
-    loads = []
-    for i, (src, dst) in enumerate(
-        (
-            (fore_hbm, field0.at[1 : F + 1, 8 : H + 8, :]),
-            (coeff_hbm, coeff_ref),
-            (video_hbm, video),
-            (mult_hbm, mult),
-            (basis_hbm, basis),
-        )
-    ):
-        copy = pltpu.make_async_copy(src, dst, in_sems.at[i])
-        copy.start()
-        loads.append(copy)
+    for load in loads[2:]:
+        load.start()
 
     pl.semaphore_wait(barrier, expected)
 
-    lane_h = lax.broadcasted_iota(jnp.int32, (H, 128), 1)
-
-    def pack_columns(k):
-        for side in range(2):
-            tile = jnp.zeros((H, 128), jnp.float32)
-            for f in range(F):
-                at = 0 if side == 0 else W - 1
-                lanes = field[k][f + 1, 8 : H + 8, (at // 128) * 128 : (at // 128) * 128 + 128]
-                column = lanes[:, at % 128 : at % 128 + 1]
-                tile = jnp.where(lane_h == f, column, tile)
-            if side == 0:
-                first_cols[...] = tile
-            packed[k, side] = tile.T[:8, :]
+    lane_h = lax.broadcasted_iota(jnp.int32, (half, 128), 1)
+
+    def pack_columns(k, h):
+        base = half_start(h)
+        tile = jnp.zeros((half, 128), jnp.float32)
+        for f in range(F):
+            for lane, at in ((f, 0), (8 + f, W - 1)):
+                lanes = field[k][f + 1, pl.ds(base + 8, half), (at // 128) * 128 : (at // 128) * 128 + 128]
+                tile = jnp.where(lane_h == lane, lanes[:, at % 128 : at % 128 + 1], tile)
+        first_cols[pl.ds(base, half), :] = tile
+        packed[k, h] = tile.T[:16, :]
+
+    strips = range(8, 12)
+    corners = (12, 13)
+
+    def columns_of(h):
+        return range(4 * h, 4 * h + 4)
 
     def halo_list(k):
         fk = field[k]
         mid = slice(1, F + 1)
-        return (
-            (packed.at[k, 0], arrived.at[k, 0], (0, -1, 0)),
-            (packed.at[k, 1], arrived.at[k, 1], (0, 1, 0)),
-            (packed.at[k, 0, F - 1 : F], arrived.at[k, 2, F - 1 : F], (0, -1, 1)),
-            (packed.at[k, 1, 0:1], arrived.at[k, 3, 0:1], (0, 1, -1)),
+        return tuple(
+            strip
+            for h in range(2)
+            for strip in (
+                (packed.at[k, h, 0:F], arrived.at[k, h, 1 : F + 1], (0, -1, 0)),
+                (packed.at[k, h, 8 : 8 + F], arrived.at[k, h, 8 : 8 + F], (0, 1, 0)),
+                (packed.at[k, h, F - 1 : F], arrived.at[k, h, 0:1], (0, -1, 1)),
+                (packed.at[k, h, 8:9], arrived.at[k, h, 8 + F : 9 + F], (0, 1, -1)),
+            )
+        ) + (
             (fk.at[mid, H : H + 8, :], fk.at[mid, 0:8, :], (1, 0, 0)),
             (fk.at[mid, 8:16, :], fk.at[mid, H + 8 : H + 16, :], (-1, 0, 0)),
             (fk.at[F, 8:9, :], fk.at[0, H + 8 : H + 9, :], (-1, 0, 1)),
             (fk.at[1, H + 7 : H + 8, :], fk.at[F + 1, 7:8, :], (1, 0, -1)),
             (fk.at[mid, H : H + 8, 0:128], corner.at[k, 0], (1, -1, 0)),
             (fk.at[mid, 8:16, W - 128 : W], corner.at[k, 1], (-1, 1, 0)),
-        ) + tuple(
-            face
-            for b in range(nz)
-            for rows in (slice(8 + b * own, 8 + (b + 1) * own),)
-            for face in (
-                (fk.at[F, rows, :], fk.at[0, rows, :], (0, 0, 1)),
-                (fk.at[1, rows, :], fk.at[F + 1, rows, :], (0, 0, -1)),
-            )
         )
 
     def halo_copy(k, i, src, dst, step):
@@ -243,6 +268,28 @@
             device_id=(r + step[0], c + step[1], z + step[2]), device_id_type=MESH,
         )
 
+    def face(k, step, up):
+        fk = field[k]
+        rows = rows_at(step, 8)
+        at = 14 + 2 * step + (0 if up else 1)
+        mine, theirs = (F, 0) if up else (1, F + 1)
+        src = fore_hbm.at[mine - 1, rows_at(step)] if k == 0 else fk.at[mine, rows]
+        return halo_copy(k, at, src, fk.at[theirs, rows], (0, 0, 1 if up else -1))
+
+    def send_faces(k, low, high):
+        @pl.loop(low, high)
+        def _(step):
+            for up in (True, False):
+                @pl.when(inside(0, 0, 1 if up else -1))
+                def _(up=up):
+                    face(k, step, up).start()
+
+    def wait_face(k, step):
+        for up in (True, False):
+            @pl.when(inside(0, 0, -1 if up else 1))
+            def _(up=up):
+                face(k, step, up).wait_recv()
+
     def send_halos(k, which):
         every = halo_list(k)
         for i in which:
@@ -267,89 +314,94 @@
             def _(i=i, src=src, dst=dst, step=step):
                 halo_copy(k, i, src, dst, step).wait_send()
 
-    def prepare_columns(k):
-        tall = jnp.concatenate([arrived[k, 0], jnp.zeros((120, H), jnp.float32)], axis=0).T
-        edge = jnp.concatenate([arrived[k, 2], jnp.zeros((120, H), jnp.float32)], axis=0).T
-        tile = jnp.where(lane_h == 0, edge[:, F - 1 : F], pltpu.roll(tall, 1, 1))
-        edge_next[8 : H + 8, :] = tile
-        lane8 = lax.broadcasted_iota(jnp.int32, (8, 128), 1)
-        top = jnp.zeros((8, 128), jnp.float32)
-        bottom = jnp.zeros((1, 128), jnp.float32)
-        for f in range(F):
-            top = jnp.where(lane8 == f + 1, corner[k, 0, f][:, 0:1], top)
-            bottom = jnp.where(lane8[:1] == f, corner[k, 1, f][0:1, 127:128], bottom)
-        edge_next[0:8, :] = top
-        edge_next[H + 8 : H + 16, :] = jnp.zeros((8, 128), jnp.float32)
-        here = jnp.concatenate([arrived[k, 1], jnp.zeros((120, H), jnp.float32)], axis=0).T
-        edge = jnp.concatenate([arrived[k, 3], jnp.zeros((120, H), jnp.float32)], axis=0).T
-        ahead = jnp.where(lane_h == F - 1, edge[:, 0:1], pltpu.roll(here, 127, 1))
-        slope0 = jnp.where((lane_h == F - 1) & (z == nz - 1), 0.0, ahead - here)
-        row_h = lax.broadcasted_iota(jnp.int32, (H, 128), 0)
-        below = jnp.where(row_h == H - 1, bottom, pltpu.roll(here, H - 1, 0))
-        slope1 = jnp.where((row_h == H - 1) & (r == nr - 1), 0.0, below - here)
-        slope2 = first_cols[...] - here
+        @pl.loop(0, steps)
+        def _(step):
+            for up in (True, False):
+                @pl.when(inside(0, 0, 1 if up else -1))
+                def _(up=up):
+                    face(k, step, up).wait_send()
+
+    def prepare_columns(k, h):
+        base = half_start(h)
+        spread = jnp.concatenate(
+            [arrived[k, h], jnp.zeros((112, half), jnp.float32)], axis=0
+        ).T
+        edge_next[pl.ds(base + 8, half), :] = spread
+        left_now[pl.ds(base, half), :] = pltpu.roll(spread, 120, 1)
+        left_next[pl.ds(base, half), :] = pltpu.roll(spread, 119, 1)
+        low, count, bottom = base, half, jnp.zeros((1, 128), jnp.float32)
+        if h == 1:
+            lane8 = lax.broadcasted_iota(jnp.int32, (8, 128), 1)
+            top = jnp.zeros((8, 128), jnp.float32)
+            for f in range(F):
+                top = jnp.where(lane8 == f + 1, corner[k, 0, f][:, 0:1], top)
+                bottom = jnp.where(lane8[:1] == f, corner[k, 1, f][0:1, 127:128], bottom)
+            edge_next[0:8, :] = top
+            low, count = pl.multiple_of((1 - flip) * (half - 8), 8), half + 8
+        here = left_now[pl.ds(low, count), :]
+        ahead = left_next[pl.ds(low, count), :]
+        lane = lax.broadcasted_iota(jnp.int32, (count, 128), 1)
+        row = lax.broadcasted_iota(jnp.int32, (count, 128), 0) + low
+        slope0 = jnp.where((lane == F - 1) & (z == nz - 1), 0.0, ahead - here)
+        after = left_now[pl.ds(low, count + 8), :]
+        below = jnp.where(row == H - 1, bottom, pltpu.roll(after, count + 7, 0)[:count])
+        slope1 = jnp.where((row == H - 1) & (r == nr - 1), 0.0, below - here)
+        slope2 = first_cols[pl.ds(low, count), :] - here
         weight = lax.rsqrt(smooth_floor + slope0 * slope0 + slope1 * slope1 + slope2 * slope2)
-        edge_flux[...] = jnp.where(c == 0, 0.0, slope2 * weight)
-
-    def sweep(k, last, block):
-        @pl.loop(0, pieces)
-        def _(step):
-            start = pl.multiple_of(block * own + step * CHUNK, 8)
-            R = CHUNK
-            lane_t = lax.broadcasted_iota(jnp.int32, (R + 8, 128), 1)
-            row_t = lax.broadcasted_iota(jnp.int32, (R + 8, W), 0) + (r * H + start - 8)
-            lane_w = lax.broadcasted_iota(jnp.int32, (R + 8, W), 1)
-            blocked = (row_t < 0) | (row_t >= nr * H - 1)
-            columns = edge_next[pl.ds(start, R + 8), :]
-            fluxes_in = edge_flux[pl.ds(start, R), :]
-            now = field[k][0, pl.ds(start, R + 16), :]
-            flux0_before = None
-            for f in range(-1, F):
-                after = field[k][f + 2, pl.ds(start, R + 16), :]
-                here = now[: R + 8]
-                below = pltpu.roll(now, R + 15, 0)[: R + 8]
-                ahead = after[: R + 8]
-                wall = columns[:, f + 1 : f + 2]
-                beyond = jnp.where(c == nc - 1, here, jnp.broadcast_to(wall, here.shape))
-                right = jnp.where(lane_w == W - 1, beyond, pltpu.roll(here, W - 1, 1))
-                slope0 = ahead - here
-                if f == F - 1:
-                    slope0 = jnp.where(z == nz - 1, 0.0, slope0)
-                slope1 = jnp.where(blocked, 0.0, below - here)
-                slope2 = right - here
-                weight = lax.rsqrt(
-                    smooth_floor + slope0 * slope0 + slope1 * slope1 + slope2 * slope2
+        edge_flux[pl.ds(low, count), :] = jnp.where(c == 0, 0.0, slope2 * weight)
+
+    def sweep(k, last, start):
+        R = CHUNK
+        lane_t = lax.broadcasted_iota(jnp.int32, (R + 8, 128), 1)
+        row_t = lax.broadcasted_iota(jnp.int32, (R + 8, W), 0) + (r * H + start - 8)
+        lane_w = lax.broadcasted_iota(jnp.int32, (R + 8, W), 1)
+        blocked = (row_t < 0) | (row_t >= nr * H - 1)
+        columns = edge_next[pl.ds(start, R + 8), :]
+        fluxes_in = edge_flux[pl.ds(start, R), :]
+        now = field[k][0, pl.ds(start, R + 16), :]
+        flux0_before = None
+        for f in range(-1, F):
+            after = field[k][f + 2, pl.ds(start, R + 16), :]
+            here = now[: R + 8]
+            below = pltpu.roll(now, R + 15, 0)[: R + 8]
+            ahead = after[: R + 8]
+            wall = columns[:, f + 1 : f + 2]
+            beyond = jnp.where(c == nc - 1, here, jnp.broadcast_to(wall, here.shape))
+            right = jnp.where(lane_w == W - 1, beyond, pltpu.roll(here, W - 1, 1))
+            slope0 = ahead - here
+            if f == F - 1:
+                slope0 = jnp.where(z == nz - 1, 0.0, slope0)
+            slope1 = jnp.where(blocked, 0.0, below - here)
+            slope2 = right - here
+            weight = lax.rsqrt(
+                smooth_floor + slope0 * slope0 + slope1 * slope1 + slope2 * slope2
+            )
+            flux0 = (slope0 * weight)[8:]
+            if f < 0:
+                flux0 = jnp.where(z == 0, 0.0, flux0)
+            else:
+                flux1 = jnp.where(row_t < 0, 0.0, slope1 * weight)
+                flux2 = (slope2 * weight)[8:]
+                above = pltpu.roll(flux1, 1, 0)[8:]
+                left = jnp.where(
+                    lane_w[8:] == 0,
+                    jnp.broadcast_to(fluxes_in[:, f : f + 1], flux2.shape),
+                    pltpu.roll(flux2, 1, 1),
                 )
-                flux0 = (slope0 * weight)[8:]
-                if f < 0:
-                    flux0 = jnp.where(z == 0, 0.0, flux0)
+                spread = flux0 - flux0_before + (flux1[8:] - above) + (flux2 - left)
+                center = here[8:]
+                at = pl.ds(start, R)
+                value = center + relax_rate * (
+                    target[f, at, :] - center + smooth_weight * spread
+                )
+                if last:
+                    shrunk = value - jnp.clip(value, -shrink_level, shrink_level)
+                    result[f, at, :] = shrunk
+                    anchor[f, at, :] = anchor[f, at, :] - shrunk
                 else:
-                    flux1 = jnp.where(row_t < 0, 0.0, slope1 * weight)
-                    flux2 = (slope2 * weight)[8:]
-                    above = pltpu.roll(flux1, 1, 0)[8:]
-                    left = jnp.where(
-                        lane_w[8:] == 0,
-                        jnp.broadcast_to(fluxes_in[:, f : f + 1], flux2.shape),
-                        pltpu.roll(flux2, 1, 1),
-                    )
-                    spread = flux0 - flux0_before + (flux1[8:] - above) + (flux2 - left)
-                    center = here[8:]
-                    at = pl.ds(start, R)
-                    value = center + relax_rate * (
-                        target[f, at, :] - center + smooth_weight * spread
-                    )
-                    if last:
-                        shrunk = value - jnp.clip(value, -shrink_level, shrink_level)
-                        result[f, at, :] = shrunk
-                        anchor[f, at, :] = anchor[f, at, :] - shrunk
-                    else:
-                        field[k + 1][f + 1, pl.ds(start + 8, R), :] = value
-                flux0_before = flux0
-                now = after
-            if last:
-                @pl.when((z != block) & ~held(block))
-                def _():
-                    move(block, step).start()
+                    field[k + 1][f + 1, pl.ds(start + 8, R), :] = value
+            flux0_before = flux0
+            now = after
 
     def products(left_of, right_of, lefts, rights, first, count, start, store):
         def body(step, totals):
@@ -367,7 +419,7 @@
             return tuple(out)
 
         totals = lax.fori_loop(
-            0, count // 8, body, tuple(start(i, j) for i in lefts for j in rights), unroll=2 if count % 16 == 0 else 1
+            0, count // 8, body, tuple(start(i, j) for i in lefts for j in rights), unroll=3 if count % 24 == 0 else 1
         )
         n = 0
         for i in lefts:
@@ -376,9 +428,7 @@
                 n += 1
 
     def held(block):
-        right = (z < block) & (block == nz - 1) & (nz - 1 - z >= 2)
-        left = (z > block) & (block == z - 1) & (z >= 2)
-        return right | left
+        return (block - z >= 2) | (z - block >= 2)
 
     def move(block, piece):
         rows = pl.ds(pl.multiple_of(block * own + piece * CHUNK, 8), CHUNK)
@@ -398,12 +448,15 @@
             device_id=(r, c, source), device_id_type=MESH,
         )
 
-    loads[0].wait()
-    send_halos(0, (10, 11))
-    send_halos(0, range(4, 10))
-    pack_columns(0)
-    send_halos(0, range(4))
-    send_halos(0, range(12, 10 + 2 * nz))
+    send_faces(0, 0, 1)
+    for h in range(2):
+        loads[h].wait()
+        pack_columns(0, h)
+        send_halos(0, columns_of(h))
+    send_halos(0, strips)
+    send_halos(0, corners)
+    send_faces(0, 1, steps)
+
     zero_tile = jnp.zeros((8, 128), jnp.float32)
 
     def store_gram(i, j, value):
@@ -412,74 +465,141 @@
         if i // 4 != j // 4:
             sums[i, j : j + 1, :] = row
 
-    gram_blocks = [(i, j) for i in range(0, rank, 4) for j in range(i, rank, 4)]
-
-    def gram_part(which):
-        for n in which:
-            i, j = gram_blocks[n]
-            products(
-                basis, basis, range(i, i + 4), range(j, j + 4), 0, H,
-                lambda i, j: zero_tile, store_gram,
-            )
+    lane_r = lax.broadcasted_iota(jnp.int32, (rank, 128), 1)
+    row_r = lax.broadcasted_iota(jnp.int32, (rank, 128), 0)
+
+    def gram_share():
+        for i in range(0, rank, 4):
+            for j in range(i, rank, 4):
+                products(
+                    basis, basis, range(i, i + 4), range(j, j + 4), z * own, own,
+                    lambda i, j: zero_tile, store_gram,
+                )
+        tile = jnp.zeros((rank, 128), jnp.float32)
+        for q in range(rank):
+            tile = jnp.where(lane_r == q, jnp.sum(sums[q], axis=1, keepdims=True), tile)
+        grams[z] = tile
+
+    def share_gram(d):
+        return pltpu.make_async_remote_copy(
+            src_ref=grams.at[z], dst_ref=grams.at[z],
+            send_sem=gram_send.at[d], recv_sem=gram_recv.at[d],
+            device_id=(r, c, lax.rem(z + d, nz)), device_id_type=MESH,
+        )
+
+    def take_gram(d):
+        source = lax.rem(z - d + nz, nz)
+        return pltpu.make_async_remote_copy(
+            src_ref=grams.at[z], dst_ref=grams.at[source],
+            send_sem=gram_send.at[d], recv_sem=gram_recv.at[d],
+            device_id=(r, c, source), device_id_type=MESH,
+        )
 
     def store_cross(i, j, value):
         cross[j, i] = value
 
-    for load in loads[1:]:
-        load.wait()
-
-    @pl.loop(0, H // 8)
-    def _(step):
-        rows = pl.ds(pl.multiple_of(step * 8, 8), 8)
-        totals = [None] * F
-        for q in range(rank):
-            plane = basis[q, rows, :]
+    def find_target(h):
+        for load in loads[3 + 3 * h : 6 + 3 * h]:
+            load.wait()
+
+        @pl.loop(0, half // 8)
+        def _(step):
+            rows = pl.ds(pl.multiple_of(half_start(h) + step * 8, 8), 8)
+            totals = [None] * F
+            for q in range(rank):
+                plane = basis[q, rows, :]
+                for f in range(F):
+                    term = coeff_ref[f, q] * plane
+                    totals[f] = term if totals[f] is None else totals[f] + term
             for f in range(F):
-                term = coeff_ref[f, q] * plane
-                totals[f] = term if totals[f] is None else totals[f] + term
-        for f in range(F):
-            lifted = dual_scale * mult[f, rows, :]
-            anchor[f, rows, :] = video[f, rows, :] + lifted
-            target[f, rows, :] = video[f, rows, :] - totals[f] + lifted
-
-    count = len(gram_blocks)
-    cuts = (0, count * 2 // 5, count * 7 // 10, count)
-    gram_part(range(cuts[0], cuts[1]))
+                lifted = dual_scale * mult[f, rows, :]
+                anchor[f, rows, :] = video[f, rows, :] + lifted
+                target[f, rows, :] = video[f, rows, :] - totals[f] + lifted
+
+    loads[2].wait()
+    find_target(0)
+
+    def advance(k, step):
+        start = pl.multiple_of(chunk_at(step) * CHUNK, 8)
+        sweep(k, k == PASSES - 1, start)
+        if k == PASSES - 1:
+            place, piece = chunk_at(step) // pieces, lax.rem(chunk_at(step), pieces)
+
+            @pl.when((place - z == 1) | (z - place == 1))
+            def _():
+                move(place, piece).start()
+
+            for i in range(0, rank, 4):
+                products(
+                    basis, anchor, range(i, i + 4), range(F), start, CHUNK,
+                    lambda i, j: cross[j, i], store_cross,
+                )
+
+    cross[...] = jnp.zeros_like(cross)
+    middle = steps // 2
     for k in range(PASSES):
         last = k == PASSES - 1
-        wait_halos(k, range(10))
-        prepare_columns(k)
+        wait_halos(k, columns_of(0))
+        prepare_columns(k, 0)
+        wait_face(k, 0)
+
+        @pl.loop(0, middle - 1)
+        def _(step, k=k):
+            wait_face(k, step + 1)
+            advance(k, step)
+
+        if k == 1:
+            gram_share()
+        wait_halos(k, columns_of(1))
+        wait_halos(k, corners)
+        prepare_columns(k, 1)
+        wait_face(k, middle)
+        advance(k, middle - 1)
+        if not last:
+            pack_columns(k + 1, 0)
+            send_halos(k + 1, columns_of(0))
+            send_faces(k + 1, 0, middle)
+        if k == 0:
+            find_target(1)
+
+        @pl.loop(middle, steps - 1)
+        def _(step, k=k):
+            wait_face(k, step + 1)
+            advance(k, step)
+
+        wait_halos(k, strips)
+        advance(k, steps - 1)
+        if not last:
+            send_halos(k + 1, strips)
+            send_halos(k + 1, corners)
+            pack_columns(k + 1, 1)
+            send_halos(k + 1, columns_of(1))
+            send_faces(k + 1, middle, steps)
+            if k == PASSES - 2:
+                for d in range(1, nz):
+                    share_gram(d).start()
+
+    inner = (z > 0) & (z < nz - 1)
+
+    def send_held(turn, low, high):
         for b in range(nz):
-            if b == 0:
-                wait_halos(k, (10, 11))
-            if b + 1 < nz:
-                wait_halos(k, (12 + 2 * b, 13 + 2 * b))
-            sweep(k, last, b)
-            if last:
-                for i in range(0, rank, 4):
-                    products(
-                        basis, anchor, range(i, i + 4), range(F), b * own, own,
-                        (lambda i, j: zero_tile) if b == 0 else (lambda i, j: cross[j, i]),
-                        store_cross,
-                    )
-            elif 2 * b < nz:
-                send_halos(k + 1, (10 + 2 * b, 11 + 2 * b))
-        if not last:
-            send_halos(k + 1, range(4, 10))
-            pack_columns(k + 1)
-            send_halos(k + 1, range(4))
-            send_halos(k + 1, range(10 + 2 * ((nz + 1) // 2), 10 + 2 * nz))
-            gram_part(range(cuts[k + 1], cuts[k + 2]))
-
+            @pl.when(held(b) & turn)
+            def _(b=b):
+                for p in range(low, high):
+                    move(b, p).start()
+
+    send_held(inner, 0, 1)
     for j in range(F):
         for i in range(rank):
             sums[rank + j, i : i + 1, :] = jnp.sum(cross[j, i], axis=0, keepdims=True)
 
-    lane_r = lax.broadcasted_iota(jnp.int32, (rank, 128), 1)
-    row_r = lax.broadcasted_iota(jnp.int32, (rank, 128), 0)
     part = jnp.zeros((rank, 128), jnp.float32)
-    for q in range(rank + F):
+    for q in range(rank, rank + F):
         part = jnp.where(lane_r == q, jnp.sum(sums[q], axis=1, keepdims=True), part)
+    for d in range(1, nz):
+        take_gram(d).wait_recv()
+    for i in range(nz):
+        part = part + grams[i]
     group = nr * nc
     me = r * nc + c
     parts[me] = part
@@ -534,16 +654,14 @@
 
     for d in range(1, nz):
         share_rows(d).start()
-    for b in range(nz):
-        @pl.when((z != b) & held(b))
-        def _(b=b):
-            for p in range(pieces):
-                move(b, p).start()
+
+    send_held(inner, 1, pieces)
     square[...] = jnp.zeros_like(square)
     square[0:rank, :] = solved
     coeff_out[...] = square[...].T[rank : rank + F, 0:rank]
     for d in range(1, nz):
         take_rows(d).wait_recv()
+    send_held(~inner, 0, pieces)
     frames = F * nz
     wide = jnp.zeros((rank, 128), jnp.float32)
     for i in range(nz):
@@ -580,6 +698,14 @@
             for q in range(8):
                 fresh[half + q, rows, :] = totals[q]
 
+    for k in range(PASSES):
+        finish_sends(k)
+    for d in range(1, nz):
+        share_rows(d).wait_send()
+        share_gram(d).wait_send()
+    for d in range(1, group):
+        share_part(d).wait_send()
+
     for n in range(nz - 1):
         near = n + (n >= z).astype(jnp.int32)
         far = nz - 1 - (n + (n >= nz - 1 - z).astype(jnp.int32))
@@ -597,26 +723,22 @@
                         value = value + table_smem[q, rank + source * F + f] * planes[f]
                     fresh[q, rows, :] = value
 
-    for k in range(PASSES):
-        finish_sends(k)
     for b in range(nz):
         @pl.when(z != b)
         def _(b=b):
             for p in range(pieces):
                 move(b, p).wait_send()
-    for d in range(1, nz):
-        share_rows(d).wait_send()
-    for d in range(1, group):
-        share_part(d).wait_send()
 
 
 def deliver(shrunk, coeff, fresh, shrunk_hbm, coeff_hbm, fresh_hbm, sems):
-    copies = [
-        pltpu.make_async_copy(source, place, sems.at[i])
-        for i, (source, place) in enumerate(
-            ((fresh, fresh_hbm), (shrunk, shrunk_hbm), (coeff, coeff_hbm))
-        )
-    ]
+    copies = [pltpu.make_async_copy(coeff, coeff_hbm, sems.at[0])]
+    for source, place in ((fresh, fresh_hbm), (shrunk, shrunk_hbm)):
+        share = source.shape[0] // 4
+        for i in range(4):
+            part = pl.ds(i * share, share)
+            copies.append(
+                pltpu.make_async_copy(source.at[part], place.at[part], sems.at[len(copies)])
+            )
     for copy in copies:
         copy.start()
     for copy in copies:
@@ -648,25 +770,30 @@
             vmem((F, H, W), f32),
             vmem((F, H, W), f32),
             vmem((F * nz, own, W), f32),
-            vmem((PASSES, 2, 8, H), f32),
-            vmem((PASSES, 4, 8, H), f32),
+            vmem((PASSES, 2, 16, H // 2), f32),
+            vmem((PASSES, 2, 16, H // 2), f32),
             vmem((PASSES, 2, F, 8, 128), f32),
-            vmem((H + 16, 128), f32),
+            vmem((H + 8, 128), f32),
             vmem((H, 128), f32),
             vmem((H, 128), f32),
+            vmem((H + 8, 128), f32),
+            vmem((H + 8, 128), f32),
             vmem((F, rank, 8, 128), f32),
             vmem((rank + F, rank, 128), f32),
+            vmem((nz, rank, 128), f32),
             vmem((group, rank, 128), f32),
             vmem((nz, rank, 128), f32),
             vmem((128, 128), f32),
             vmem((rank, 128), f32),
             pltpu.SMEM((F, rank), f32),
             pltpu.SMEM((rank, 128), f32),
-            dma((5,)),
-            dma((PASSES, 10 + 2 * nz)),
-            dma((PASSES, 10 + 2 * nz)),
+            dma((9,)),
+            dma((PASSES, 14 + 2 * (H // CHUNK))),
+            dma((PASSES, 14 + 2 * (H // CHUNK))),
             dma((group,)),
             dma((group,)),
+            dma((nz,)),
+            dma((nz,)),
             dma((nz,)),
             dma((nz,)),
             dma((nz, pieces)),
@@ -691,7 +818,7 @@
         ),
         in_specs=[on_chip] * 3,
         out_specs=[hbm] * 3,
-        scratch_shapes=[dma((3,))],
+        scratch_shapes=[dma((9,))],
     )(*(pltpu.with_memory_space_constraint(x, pltpu.VMEM) for x in found))
 
 
@@ -701,7 +828,8 @@
     nz = lax.axis_size("frame")
     fits = (
         H % nz == 0 and (H // nz) % 8 == 0 and (H // nz) % CHUNK == 0 and W % 128 == 0
-        and F <= 8 and rank % 8 == 0 and 2 * rank + F * nz <= 128
+        and H % 16 == 0 and (H // CHUNK) % 2 == 0 and lax.axis_size("row") <= 2
+        and F % 4 == 0 and F < 8 and rank % 8 == 0 and 2 * rank + F * nz <= 128
     )
     run = whole_kernel if fits else local
     return run(video, multiplier, foreground, basis, coefficients)

time: 61.5 us -> 60 us (0.976)
  the two profiles are of different devices: /device:TPU:30 before, /device:TPU:8 now
where the time goes in v2:
time: 60 us; the launch traced here: 59.9 us
  Pallas kernels  59.2 us (99%)
  between operations  0.64 us (1%)
    pallas_call x1, Pallas kernels, whole_kernel(): pl.pallas_call(functools.partial(kernel, (F, H, W, rank, nr, nc, nz)), ou...  57.8 us
    pallas_call x1, Pallas kernels, whole_kernel(): pl.pallas_call(deliver, out_shape=(jax.ShapeDtypeStruct((F, H, W), f32),...  1.48 us

profile of v2, /device:TPU:8, one launch (start us, length us, event | category | flops | bytes accessed | tf_op | source)
XLA Modules:
  0.0 59.9 jit_solution(12579663239651980874)
XLA Ops:
  0.6 57.8 %shard_map.76 = (f32[4,288,256]{2,1,0:T(8,128)S(1)}, f32[4,16]{1,0:T(4,128)S(1)}, f32[16,72,256]{2,1,0:T(8,128)S(1)}) custom-call(f32[4,16]{1,0:T(4,128)} %coeff_hbm.1, f32[4,288,256]{2,1,0:T(8,128)} %video_hbm.1, f32[4,288,256]{2,1,0:T(8,128)} %mult_hbm.1, f32[4,288,256]{2,1,0:T(8,128)} %fore_hbm.1, f32[16,288,256]{2,1,0:T(8,128)} %basis_hbm.1), custom_call_target="tpu_custom_call" | custom-call | tf_op jit(solution)/shard_map/pallas_call | solution.py:760
  58.4 1.5 %shard_map.77 = (f32[4,288,256]{2,1,0:T(8,128)}, f32[4,16]{1,0:T(4,128)}, f32[16,72,256]{2,1,0:T(8,128)}) custom-call(f32[4,288,256]{2,1,0:T(8,128)S(1)} %get-tuple-element.6.shrunk, f32[4,16]{1,0:T(4,128)S(1)} %get-tuple-element.7.coeff, f32[16,72,256]{2,1,0:T(8,128)S(1)} %get-tuple-element.8.fresh), custom_call_target="tpu_custom_call" | custom-call | tf_op jit(solution)/shard_map/pallas_call | solution.py:812

commit v3 on v2

--- a/solution.py
+++ b/solution.py
@@ -121,6 +121,7 @@
 
 MESH = pl.DeviceIdType.MESH
 CHUNK = 24
+SEGMENTS = 4
 
 
 def eliminate(matrix, size):
@@ -138,7 +139,7 @@
     sizes, coeff_hbm, video_hbm, mult_hbm, fore_hbm, basis_hbm,
     result, coeff_out, fresh,
     field0, field1, field2, video, mult, basis, anchor, target, owned,
-    packed, arrived, corner, edge_next, edge_flux, first_cols, left_now, left_next,
+    packed, arrived, corner, edge_next, edge_flux, first_cols, left_now, left_next, bottom_row,
     cross, sums, grams, parts, shares, square, table, coeff_ref, table_smem,
     in_sems, halo_send, halo_recv, part_send, part_recv,
     gram_send, gram_recv, share_send, share_recv, move_send, move_recv, small_sem,
@@ -160,6 +161,12 @@
 
     def rows_at(step, offset=0):
         return pl.ds(pl.multiple_of(offset + chunk_at(step) * CHUNK, 8), CHUNK)
+
+    span = H // SEGMENTS
+    per = steps // SEGMENTS
+
+    def segment_start(j):
+        return pl.multiple_of((j + flip * (SEGMENTS - 1 - 2 * j)) * span, 8)
 
     def half_start(h):
         return pl.multiple_of((h + flip * (1 - 2 * h)) * half, 8)
@@ -195,17 +202,9 @@
         load.start()
 
     barrier = pltpu.get_barrier_semaphore()
-    for d in range(1, nr * nc):
-        other = lax.rem(r * nc + c + d, nr * nc)
-        pl.semaphore_signal(
-            barrier, inc=1, device_id=(other // nc, lax.rem(other, nc), z), device_id_type=MESH
-        )
-    for d in range(1, nz):
-        pl.semaphore_signal(
-            barrier, inc=1, device_id=(r, c, lax.rem(z + d, nz)), device_id_type=MESH
-        )
-    diagonals = ((1, 0, -1), (-1, 0, 1), (0, 1, -1), (0, -1, 1))
-    for step in diagonals:
+    beside = ((0, 0, 1), (0, 1, 0), (1, 0, 0), (1, 0, -1), (0, 1, -1), (1, -1, 0))
+    beside += tuple(tuple(-s for s in step) for step in beside)
+    for step in beside:
         @pl.when(inside(*step))
         def _(step=step):
             pl.semaphore_signal(
@@ -214,45 +213,41 @@
                 device_id=(r + step[0], c + step[1], z + step[2]),
                 device_id_type=MESH,
             )
-    expected = jnp.int32(nr * nc - 1 + nz - 1)
-    for step in diagonals:
+    expected = jnp.int32(0)
+    for step in beside:
         expected = expected + inside(*step).astype(jnp.int32)
     for load in loads[2:]:
         load.start()
 
     pl.semaphore_wait(barrier, expected)
 
-    lane_h = lax.broadcasted_iota(jnp.int32, (half, 128), 1)
-
-    def pack_columns(k, h):
-        base = half_start(h)
-        tile = jnp.zeros((half, 128), jnp.float32)
+    lane_h = lax.broadcasted_iota(jnp.int32, (span, 128), 1)
+
+    def pack_columns(k, j):
+        base = segment_start(j)
+        tile = jnp.zeros((span, 128), jnp.float32)
         for f in range(F):
             for lane, at in ((f, 0), (8 + f, W - 1)):
-                lanes = field[k][f + 1, pl.ds(base + 8, half), (at // 128) * 128 : (at // 128) * 128 + 128]
+                lanes = field[k][f + 1, pl.ds(base + 8, span), (at // 128) * 128 : (at // 128) * 128 + 128]
                 tile = jnp.where(lane_h == lane, lanes[:, at % 128 : at % 128 + 1], tile)
-        first_cols[pl.ds(base, half), :] = tile
-        packed[k, h] = tile.T[:16, :]
-
-    strips = range(8, 12)
-    corners = (12, 13)
-
-    def columns_of(h):
-        return range(4 * h, 4 * h + 4)
+        first_cols[pl.ds(base + 8, span), :] = tile
+        packed[k, j] = tile.T[:16, :]
+
+    strips = range(4)
+    corners = (4, 5)
+
+    def column_list(k, j):
+        return (
+            (packed.at[k, j, 0:F], arrived.at[k, j, 1 : F + 1], (0, -1, 0)),
+            (packed.at[k, j, 8 : 8 + F], arrived.at[k, j, 8 : 8 + F], (0, 1, 0)),
+            (packed.at[k, j, F - 1 : F], arrived.at[k, j, 0:1], (0, -1, 1)),
+            (packed.at[k, j, 8:9], arrived.at[k, j, 8 + F : 9 + F], (0, 1, -1)),
+        )
 
     def halo_list(k):
         fk = field[k]
         mid = slice(1, F + 1)
-        return tuple(
-            strip
-            for h in range(2)
-            for strip in (
-                (packed.at[k, h, 0:F], arrived.at[k, h, 1 : F + 1], (0, -1, 0)),
-                (packed.at[k, h, 8 : 8 + F], arrived.at[k, h, 8 : 8 + F], (0, 1, 0)),
-                (packed.at[k, h, F - 1 : F], arrived.at[k, h, 0:1], (0, -1, 1)),
-                (packed.at[k, h, 8:9], arrived.at[k, h, 8 + F : 9 + F], (0, 1, -1)),
-            )
-        ) + (
+        return (
             (fk.at[mid, H : H + 8, :], fk.at[mid, 0:8, :], (1, 0, 0)),
             (fk.at[mid, 8:16, :], fk.at[mid, H + 8 : H + 16, :], (-1, 0, 0)),
             (fk.at[F, 8:9, :], fk.at[0, H + 8 : H + 9, :], (-1, 0, 1)),
@@ -261,20 +256,34 @@
             (fk.at[mid, 8:16, W - 128 : W], corner.at[k, 1], (-1, 1, 0)),
         )
 
-    def halo_copy(k, i, src, dst, step):
+    def halo_copy(k, i, leave, src, dst, step):
         return pltpu.make_async_remote_copy(
             src_ref=src, dst_ref=dst,
-            send_sem=halo_send.at[k, i], recv_sem=halo_recv.at[k, i],
+            send_sem=halo_send.at[k % 2, leave], recv_sem=halo_recv.at[k % 2, i],
             device_id=(r + step[0], c + step[1], z + step[2]), device_id_type=MESH,
         )
+
+    def send_columns(k, j):
+        for i, (src, dst, step) in enumerate(column_list(k, j)):
+            @pl.when(inside(*step))
+            def _(i=i, src=src, dst=dst, step=step):
+                halo_copy(k, 6 + 4 * j + i, 6 + i, src, dst, step).start()
+
+    def wait_columns(k, j):
+        for i, (src, dst, step) in enumerate(column_list(k, j)):
+            @pl.when(inside(*(-s for s in step)))
+            def _(i=i, src=src, dst=dst, step=step):
+                halo_copy(k, 6 + 4 * j + i, 6 + i, src, dst, step).wait_recv()
 
     def face(k, step, up):
         fk = field[k]
         rows = rows_at(step, 8)
-        at = 14 + 2 * step + (0 if up else 1)
+        at = 6 + 4 * SEGMENTS + 2 * step + (0 if up else 1)
         mine, theirs = (F, 0) if up else (1, F + 1)
         src = fore_hbm.at[mine - 1, rows_at(step)] if k == 0 else fk.at[mine, rows]
-        return halo_copy(k, at, src, fk.at[theirs, rows], (0, 0, 1 if up else -1))
+        return halo_copy(
+            k, at, 10 if up else 11, src, fk.at[theirs, rows], (0, 0, 1 if up else -1)
+        )
 
     def send_faces(k, low, high):
         @pl.loop(low, high)
@@ -297,7 +306,7 @@
 
             @pl.when(inside(*step))
             def _(i=i, src=src, dst=dst, step=step):
-                halo_copy(k, i, src, dst, step).start()
+                halo_copy(k, i, i, src, dst, step).start()
 
     def wait_halos(k, which):
         every = halo_list(k)
@@ -306,100 +315,131 @@
 
             @pl.when(inside(*(-s for s in step)))
             def _(i=i, src=src, dst=dst, step=step):
-                halo_copy(k, i, src, dst, step).wait_recv()
+                halo_copy(k, i, i, src, dst, step).wait_recv()
 
     def finish_sends(k):
         for i, (src, dst, step) in enumerate(halo_list(k)):
             @pl.when(inside(*step))
             def _(i=i, src=src, dst=dst, step=step):
-                halo_copy(k, i, src, dst, step).wait_send()
-
-        @pl.loop(0, steps)
-        def _(step):
-            for up in (True, False):
-                @pl.when(inside(0, 0, 1 if up else -1))
-                def _(up=up):
-                    face(k, step, up).wait_send()
-
-    def prepare_columns(k, h):
-        base = half_start(h)
+                halo_copy(k, i, i, src, dst, step).wait_send()
+
+        every = (
+            (packed.at[k, :, 0:F], arrived.at[k, :, 1 : F + 1], (0, -1, 0)),
+            (packed.at[k, :, 8 : 8 + F], arrived.at[k, :, 8 : 8 + F], (0, 1, 0)),
+            (packed.at[k, :, F - 1 : F], arrived.at[k, :, 0:1], (0, -1, 1)),
+            (packed.at[k, :, 8:9], arrived.at[k, :, 8 + F : 9 + F], (0, 1, -1)),
+            (field[k].at[F, 8 : H + 8, :], field[k].at[0, 8 : H + 8, :], (0, 0, 1)),
+            (field[k].at[1, 8 : H + 8, :], field[k].at[F + 1, 8 : H + 8, :], (0, 0, -1)),
+        )
+        for i, (src, dst, step) in enumerate(every):
+            @pl.when(inside(*step))
+            def _(i=i, src=src, dst=dst, step=step):
+                halo_copy(k, 0, 6 + i, src, dst, step).wait_send()
+
+    def prepare_columns(k, j):
+        base = segment_start(j)
         spread = jnp.concatenate(
-            [arrived[k, h], jnp.zeros((112, half), jnp.float32)], axis=0
+            [arrived[k, j], jnp.zeros((112, span), jnp.float32)], axis=0
         ).T
-        edge_next[pl.ds(base + 8, half), :] = spread
-        left_now[pl.ds(base, half), :] = pltpu.roll(spread, 120, 1)
-        left_next[pl.ds(base, half), :] = pltpu.roll(spread, 119, 1)
-        low, count, bottom = base, half, jnp.zeros((1, 128), jnp.float32)
-        if h == 1:
-            lane8 = lax.broadcasted_iota(jnp.int32, (8, 128), 1)
-            top = jnp.zeros((8, 128), jnp.float32)
-            for f in range(F):
-                top = jnp.where(lane8 == f + 1, corner[k, 0, f][:, 0:1], top)
-                bottom = jnp.where(lane8[:1] == f, corner[k, 1, f][0:1, 127:128], bottom)
-            edge_next[0:8, :] = top
-            low, count = pl.multiple_of((1 - flip) * (half - 8), 8), half + 8
+        edge_next[pl.ds(base + 8, span), :] = spread
+        left_now[pl.ds(base + 8, span), :] = pltpu.roll(spread, 120, 1)
+        left_next[pl.ds(base + 8, span), :] = pltpu.roll(spread, 119, 1)
+        low, count = pl.multiple_of(base + 8 * flip, 8), span + 8
         here = left_now[pl.ds(low, count), :]
         ahead = left_next[pl.ds(low, count), :]
         lane = lax.broadcasted_iota(jnp.int32, (count, 128), 1)
-        row = lax.broadcasted_iota(jnp.int32, (count, 128), 0) + low
+        row = lax.broadcasted_iota(jnp.int32, (count, 128), 0) + (low - 8)
         slope0 = jnp.where((lane == F - 1) & (z == nz - 1), 0.0, ahead - here)
         after = left_now[pl.ds(low, count + 8), :]
-        below = jnp.where(row == H - 1, bottom, pltpu.roll(after, count + 7, 0)[:count])
+        below = jnp.where(
+            row == H - 1, bottom_row[0:1, :], pltpu.roll(after, count + 7, 0)[:count]
+        )
         slope1 = jnp.where((row == H - 1) & (r == nr - 1), 0.0, below - here)
         slope2 = first_cols[pl.ds(low, count), :] - here
         weight = lax.rsqrt(smooth_floor + slope0 * slope0 + slope1 * slope1 + slope2 * slope2)
         edge_flux[pl.ds(low, count), :] = jnp.where(c == 0, 0.0, slope2 * weight)
 
+    def take_corners(k):
+        wait_halos(k, corners)
+        lane8 = lax.broadcasted_iota(jnp.int32, (8, 128), 1)
+        top = jnp.zeros((8, 128), jnp.float32)
+        bottom = jnp.zeros((8, 128), jnp.float32)
+        for f in range(F):
+            top = jnp.where(lane8 == f + 1, corner[k, 0, f][:, 0:1], top)
+            bottom = jnp.where(lane8 == f, corner[k, 1, f][:, 127:128], bottom)
+        edge_next[0:8, :] = top
+        bottom_row[...] = bottom
+
     def sweep(k, last, start):
         R = CHUNK
-        lane_t = lax.broadcasted_iota(jnp.int32, (R + 8, 128), 1)
-        row_t = lax.broadcasted_iota(jnp.int32, (R + 8, W), 0) + (r * H + start - 8)
-        lane_w = lax.broadcasted_iota(jnp.int32, (R + 8, W), 1)
-        blocked = (row_t < 0) | (row_t >= nr * H - 1)
+        tiles = W // 128
+        row_8 = lax.broadcasted_iota(jnp.int32, (8, 128), 0) + (r * H + start)
+        above_image = row_8 - 8 < 0
+        last_image_row = row_8 + (R - 8) >= nr * H - 1
         columns = edge_next[pl.ds(start, R + 8), :]
-        fluxes_in = edge_flux[pl.ds(start, R), :]
-        now = field[k][0, pl.ds(start, R + 16), :]
+        fluxes_in = edge_flux[pl.ds(start + 8, R), :]
+        at = pl.ds(start, R)
+
+        def frame(f):
+            return [
+                field[k][f, pl.ds(start, R + 16), w * 128 : w * 128 + 128] for w in range(tiles)
+            ]
+
+        now = frame(0)
         flux0_before = None
         for f in range(-1, F):
-            after = field[k][f + 2, pl.ds(start, R + 16), :]
-            here = now[: R + 8]
-            below = pltpu.roll(now, R + 15, 0)[: R + 8]
-            ahead = after[: R + 8]
-            wall = columns[:, f + 1 : f + 2]
-            beyond = jnp.where(c == nc - 1, here, jnp.broadcast_to(wall, here.shape))
-            right = jnp.where(lane_w == W - 1, beyond, pltpu.roll(here, W - 1, 1))
-            slope0 = ahead - here
-            if f == F - 1:
-                slope0 = jnp.where(z == nz - 1, 0.0, slope0)
-            slope1 = jnp.where(blocked, 0.0, below - here)
-            slope2 = right - here
-            weight = lax.rsqrt(
-                smooth_floor + slope0 * slope0 + slope1 * slope1 + slope2 * slope2
-            )
-            flux0 = (slope0 * weight)[8:]
+            after = frame(f + 2)
+            skip = 8 if f < 0 else 0
+            n = R + 8 - skip
+            lane = lax.broadcasted_iota(jnp.int32, (n, 128), 1)
+            here = [t[skip : R + 8] for t in now]
+            turned = [pltpu.roll(t, 127, 1) for t in here]
+            wall = jnp.broadcast_to(columns[skip:, f + 1 : f + 2], (n, 128))
+            flux0, flux1, flux2 = [], [], []
+            for w in range(tiles):
+                slope0 = after[w][skip : R + 8] - here[w]
+                if f == F - 1:
+                    slope0 = jnp.where(z == nz - 1, 0.0, slope0)
+                slope1 = pltpu.roll(now[w][skip:], n + 7, 0)[:n] - here[w]
+                slope1 = jnp.concatenate(
+                    [slope1[: n - 8], jnp.where(last_image_row, 0.0, slope1[n - 8 :])], axis=0
+                )
+                beyond = turned[w + 1] if w + 1 < tiles else wall
+                slope2 = jnp.where(lane == 127, beyond, turned[w]) - here[w]
+                if w + 1 == tiles:
+                    slope2 = jnp.where((lane == 127) & (c == nc - 1), 0.0, slope2)
+                weight = lax.rsqrt(
+                    smooth_floor + slope0 * slope0 + slope1 * slope1 + slope2 * slope2
+                )
+                flux0.append((slope0 * weight)[8 - skip :])
+                if f >= 0:
+                    flux = slope1 * weight
+                    flux1.append(
+                        jnp.concatenate(
+                            [jnp.where(above_image, 0.0, flux[:8]), flux[8:]], axis=0
+                        )
+                    )
+                    flux2.append((slope2 * weight)[8:])
             if f < 0:
-                flux0 = jnp.where(z == 0, 0.0, flux0)
+                flux0 = [jnp.where(z == 0, 0.0, t) for t in flux0]
             else:
-                flux1 = jnp.where(row_t < 0, 0.0, slope1 * weight)
-                flux2 = (slope2 * weight)[8:]
-                above = pltpu.roll(flux1, 1, 0)[8:]
-                left = jnp.where(
-                    lane_w[8:] == 0,
-                    jnp.broadcast_to(fluxes_in[:, f : f + 1], flux2.shape),
-                    pltpu.roll(flux2, 1, 1),
-                )
-                spread = flux0 - flux0_before + (flux1[8:] - above) + (flux2 - left)
-                center = here[8:]
-                at = pl.ds(start, R)
-                value = center + relax_rate * (
-                    target[f, at, :] - center + smooth_weight * spread
-                )
-                if last:
-                    shrunk = value - jnp.clip(value, -shrink_level, shrink_level)
-                    result[f, at, :] = shrunk
-                    anchor[f, at, :] = anchor[f, at, :] - shrunk
-                else:
-                    field[k + 1][f + 1, pl.ds(start + 8, R), :] = value
+                moved = [pltpu.roll(t, 1, 1) for t in flux2]
+                entry = jnp.broadcast_to(fluxes_in[:, f : f + 1], (R, 128))
+                lane = lax.broadcasted_iota(jnp.int32, (R, 128), 1)
+                for w in range(tiles):
+                    left = jnp.where(lane == 0, moved[w - 1] if w > 0 else entry, moved[w])
+                    above = pltpu.roll(flux1[w], 1, 0)[8:]
+                    spread = (flux0[w] - flux0_before[w]) + (flux1[w][8:] - above) + (flux2[w] - left)
+                    lanes = slice(w * 128, w * 128 + 128)
+                    value = (1.0 - relax_rate) * here[w][8:] + (
+                        target[f, at, lanes] + (relax_rate * smooth_weight) * spread
+                    )
+                    if last:
+                        shrunk = value - jnp.clip(value, -shrink_level, shrink_level)
+                        result[f, at, lanes] = shrunk
+                        anchor[f, at, lanes] = anchor[f, at, lanes] - shrunk
+                    else:
+                        field[k + 1][f + 1, pl.ds(start + 8, R), lanes] = value
             flux0_before = flux0
             now = after
 
@@ -435,7 +475,7 @@
         spot = pl.ds(pl.multiple_of(piece * CHUNK, 8), CHUNK)
         return pltpu.make_async_remote_copy(
             src_ref=anchor.at[:, rows, :], dst_ref=owned.at[pl.ds(z * F, F), spot, :],
-            send_sem=move_send.at[block, piece], recv_sem=move_recv.at[z, piece],
+            send_sem=move_send.at[block], recv_sem=move_recv.at[z, piece],
             device_id=(r, c, block), device_id_type=MESH,
         )
 
@@ -444,18 +484,20 @@
         spot = pl.ds(pl.multiple_of(piece * CHUNK, 8), CHUNK)
         return pltpu.make_async_remote_copy(
             src_ref=anchor.at[:, rows, :], dst_ref=owned.at[pl.ds(source * F, F), spot, :],
-            send_sem=move_send.at[source, piece], recv_sem=move_recv.at[source, piece],
+            send_sem=move_send.at[source], recv_sem=move_recv.at[source, piece],
             device_id=(r, c, source), device_id_type=MESH,
         )
 
     send_faces(0, 0, 1)
-    for h in range(2):
-        loads[h].wait()
-        pack_columns(0, h)
-        send_halos(0, columns_of(h))
-    send_halos(0, strips)
-    send_halos(0, corners)
-    send_faces(0, 1, steps)
+    for j in range(SEGMENTS):
+        if j % (SEGMENTS // 2) == 0:
+            loads[j // (SEGMENTS // 2)].wait()
+        pack_columns(0, j)
+        send_columns(0, j)
+        if j == SEGMENTS // 2:
+            send_halos(0, strips)
+            send_halos(0, corners)
+        send_faces(0, max(1, j * per), (j + 1) * per)
 
     zero_tile = jnp.zeros((8, 128), jnp.float32)
 
@@ -480,10 +522,16 @@
             tile = jnp.where(lane_r == q, jnp.sum(sums[q], axis=1, keepdims=True), tile)
         grams[z] = tile
 
+    def all_sent(block, sem):
+        return pltpu.make_async_remote_copy(
+            src_ref=block, dst_ref=block, send_sem=sem.at[0], recv_sem=sem.at[0],
+            device_id=(r, c, lax.rem(z + 1, nz)), device_id_type=MESH,
+        )
+
     def share_gram(d):
         return pltpu.make_async_remote_copy(
             src_ref=grams.at[z], dst_ref=grams.at[z],
-            send_sem=gram_send.at[d], recv_sem=gram_recv.at[d],
+            send_sem=gram_send.at[0], recv_sem=gram_recv.at[d],
             device_id=(r, c, lax.rem(z + d, nz)), device_id_type=MESH,
         )
 
@@ -491,7 +539,7 @@
         source = lax.rem(z - d + nz, nz)
         return pltpu.make_async_remote_copy(
             src_ref=grams.at[z], dst_ref=grams.at[source],
-            send_sem=gram_send.at[d], recv_sem=gram_recv.at[d],
+            send_sem=gram_send.at[0], recv_sem=gram_recv.at[d],
             device_id=(r, c, source), device_id_type=MESH,
         )
 
@@ -514,10 +562,12 @@
             for f in range(F):
                 lifted = dual_scale * mult[f, rows, :]
                 anchor[f, rows, :] = video[f, rows, :] + lifted
-                target[f, rows, :] = video[f, rows, :] - totals[f] + lifted
+                target[f, rows, :] = relax_rate * (video[f, rows, :] - totals[f] + lifted)
 
     loads[2].wait()
     find_target(0)
+    find_target(1)
+    gram_share()
 
     def advance(k, step):
         start = pl.multiple_of(chunk_at(step) * CHUNK, 8)
@@ -536,48 +586,52 @@
                 )
 
     cross[...] = jnp.zeros_like(cross)
-    middle = steps // 2
+    bottom_row[...] = jnp.zeros_like(bottom_row)
     for k in range(PASSES):
         last = k == PASSES - 1
-        wait_halos(k, columns_of(0))
+        if k > 0 and not last:
+            finish_sends(k - 1)
+        wait_columns(k, 0)
         prepare_columns(k, 0)
         wait_face(k, 0)
 
-        @pl.loop(0, middle - 1)
-        def _(step, k=k):
-            wait_face(k, step + 1)
-            advance(k, step)
-
-        if k == 1:
-            gram_share()
-        wait_halos(k, columns_of(1))
-        wait_halos(k, corners)
-        prepare_columns(k, 1)
-        wait_face(k, middle)
-        advance(k, middle - 1)
-        if not last:
-            pack_columns(k + 1, 0)
-            send_halos(k + 1, columns_of(0))
-            send_faces(k + 1, 0, middle)
-        if k == 0:
-            find_target(1)
-
-        @pl.loop(middle, steps - 1)
-        def _(step, k=k):
-            wait_face(k, step + 1)
-            advance(k, step)
-
-        wait_halos(k, strips)
-        advance(k, steps - 1)
-        if not last:
-            send_halos(k + 1, strips)
-            send_halos(k + 1, corners)
-            pack_columns(k + 1, 1)
-            send_halos(k + 1, columns_of(1))
-            send_faces(k + 1, middle, steps)
-            if k == PASSES - 2:
-                for d in range(1, nz):
-                    share_gram(d).start()
+        @pl.loop(0, SEGMENTS)
+        def _(j, k=k, last=last):
+            @pl.loop(j * per, (j + 1) * per - 1)
+            def _(step):
+                wait_face(k, step + 1)
+                advance(k, step)
+
+            final = j == SEGMENTS - 1
+
+            @pl.when(j == SEGMENTS - 2)
+            def _():
+                take_corners(k)
+
+            @pl.when(~final)
+            def _():
+                wait_columns(k, j + 1)
+                prepare_columns(k, j + 1)
+                wait_face(k, (j + 1) * per)
+
+            @pl.when(final)
+            def _():
+                wait_halos(k, strips)
+
+            advance(k, (j + 1) * per - 1)
+            if not last:
+                @pl.when(final)
+                def _():
+                    send_halos(k + 1, strips)
+                    send_halos(k + 1, corners)
+
+                pack_columns(k + 1, j)
+                send_columns(k + 1, j)
+                send_faces(k + 1, j * per, (j + 1) * per)
+
+        if k == PASSES - 2:
+            for d in range(1, nz):
+                share_gram(d).start()
 
     inner = (z > 0) & (z < nz - 1)
 
@@ -588,7 +642,13 @@
                 for p in range(low, high):
                     move(b, p).start()
 
-    send_held(inner, 0, 1)
+    for far, near in ((nz - 1, 0), (0, nz - 1)):
+        place = far - 1 if far > near else far + 1
+
+        @pl.when((z == near) & held(jnp.int32(place)))
+        def _(place=place):
+            move(place, 0).start()
+
     for j in range(F):
         for i in range(rank):
             sums[rank + j, i : i + 1, :] = jnp.sum(cross[j, i], axis=0, keepdims=True)
@@ -608,7 +668,7 @@
         other = lax.rem(me + d, group)
         return pltpu.make_async_remote_copy(
             src_ref=parts.at[me], dst_ref=parts.at[me],
-            send_sem=part_send.at[d], recv_sem=part_recv.at[d],
+            send_sem=part_send.at[0], recv_sem=part_recv.at[d],
             device_id=(other // nc, lax.rem(other, nc), z), device_id_type=MESH,
         )
 
@@ -616,7 +676,7 @@
         other = lax.rem(me - d + group, group)
         return pltpu.make_async_remote_copy(
             src_ref=parts.at[me], dst_ref=parts.at[other],
-            send_sem=part_send.at[d], recv_sem=part_recv.at[d],
+            send_sem=part_send.at[0], recv_sem=part_recv.at[d],
             device_id=(other // nc, lax.rem(other, nc), z), device_id_type=MESH,
         )
 
@@ -640,7 +700,7 @@
     def share_rows(d):
         return pltpu.make_async_remote_copy(
             src_ref=shares.at[z], dst_ref=shares.at[z],
-            send_sem=share_send.at[d], recv_sem=share_recv.at[d],
+            send_sem=share_send.at[0], recv_sem=share_recv.at[d],
             device_id=(r, c, lax.rem(z + d, nz)), device_id_type=MESH,
         )
 
@@ -648,20 +708,28 @@
         source = lax.rem(z - d + nz, nz)
         return pltpu.make_async_remote_copy(
             src_ref=shares.at[z], dst_ref=shares.at[source],
-            send_sem=share_send.at[d], recv_sem=share_recv.at[d],
+            send_sem=share_send.at[0], recv_sem=share_recv.at[d],
             device_id=(r, c, source), device_id_type=MESH,
         )
 
     for d in range(1, nz):
         share_rows(d).start()
 
-    send_held(inner, 1, pieces)
+    send_held(inner, 0, pieces)
     square[...] = jnp.zeros_like(square)
     square[0:rank, :] = solved
     coeff_out[...] = square[...].T[rank : rank + F, 0:rank]
     for d in range(1, nz):
         take_rows(d).wait_recv()
-    send_held(~inner, 0, pieces)
+    for b in range(nz):
+        @pl.when(held(b) & ~inner)
+        def _(b=b):
+            first = jnp.where(((z == 0) & (b == nz - 2)) | ((z == nz - 1) & (b == 1)), 1, 0)
+
+            @pl.loop(first, pieces)
+            def _(p):
+                move(b, p).start()
+
     frames = F * nz
     wide = jnp.zeros((rank, 128), jnp.float32)
     for i in range(nz):
@@ -678,7 +746,7 @@
     system = jnp.where(diagonal, gram + frame_ridge, gram) + wide
     system = system + jnp.where(lane_r == row_r + rank + frames, frame_ridge, 0.0)
     table[...] = eliminate(system, rank)
-    to_scalar = pltpu.make_async_copy(table, table_smem, small_sem.at[1])
+    to_scalar = pltpu.make_async_copy(table, table_smem, small_sem.at[0])
     to_scalar.start()
     to_scalar.wait()
     my_base = z * own
@@ -698,18 +766,18 @@
             for q in range(8):
                 fresh[half + q, rows, :] = totals[q]
 
-    for k in range(PASSES):
+    for k in range(PASSES - 2, PASSES):
         finish_sends(k)
-    for d in range(1, nz):
-        share_rows(d).wait_send()
-        share_gram(d).wait_send()
-    for d in range(1, group):
-        share_part(d).wait_send()
+    for src, sem in ((shares, share_send), (grams, gram_send)):
+        all_sent(src.at[0 : nz - 1], sem).wait_send()
+    all_sent(parts.at[0 : group - 1], part_send).wait_send()
 
     for n in range(nz - 1):
         near = n + (n >= z).astype(jnp.int32)
         far = nz - 1 - (n + (n >= nz - 1 - z).astype(jnp.int32))
+        distance = 1 if n == 0 else nz - n
         source = jnp.where(2 * z < nz, near, far)
+        source = jnp.where(z == 0, distance, jnp.where(z == nz - 1, nz - 1 - distance, source))
 
         @pl.loop(0, pieces)
         def _(piece, source=source):
@@ -726,8 +794,12 @@
     for b in range(nz):
         @pl.when(z != b)
         def _(b=b):
-            for p in range(pieces):
-                move(b, p).wait_send()
+            rows = pl.ds(b * own, own)
+            pltpu.make_async_remote_copy(
+                src_ref=anchor.at[:, rows, :], dst_ref=owned.at[pl.ds(z * F, F)],
+                send_sem=move_send.at[b], recv_sem=move_recv.at[z, 0],
+                device_id=(r, c, b), device_id_type=MESH,
+            ).wait_send()
 
 
 def deliver(shrunk, coeff, fresh, shrunk_hbm, coeff_hbm, fresh_hbm, sems):
@@ -770,14 +842,15 @@
             vmem((F, H, W), f32),
             vmem((F, H, W), f32),
             vmem((F * nz, own, W), f32),
-            vmem((PASSES, 2, 16, H // 2), f32),
-            vmem((PASSES, 2, 16, H // 2), f32),
+            vmem((PASSES, SEGMENTS, 16, H // SEGMENTS), f32),
+            vmem((PASSES, SEGMENTS, 16, H // SEGMENTS), f32),
             vmem((PASSES, 2, F, 8, 128), f32),
             vmem((H + 8, 128), f32),
-            vmem((H, 128), f32),
-            vmem((H, 128), f32),
-            vmem((H + 8, 128), f32),
-            vmem((H + 8, 128), f32),
+            vmem((H + 16, 128), f32),
+            vmem((H + 16, 128), f32),
+            vmem((H + 24, 128), f32),
+            vmem((H + 24, 128), f32),
+            vmem((8, 128), f32),
             vmem((F, rank, 8, 128), f32),
             vmem((rank + F, rank, 128), f32),
             vmem((nz, rank, 128), f32),
@@ -788,17 +861,17 @@
             pltpu.SMEM((F, rank), f32),
             pltpu.SMEM((rank, 128), f32),
             dma((9,)),
-            dma((PASSES, 14 + 2 * (H // CHUNK))),
-            dma((PASSES, 14 + 2 * (H // CHUNK))),
+            dma((2, 12)),
+            dma((2, 6 + 4 * SEGMENTS + 2 * (H // CHUNK))),
+            dma((1,)),
             dma((group,)),
-            dma((group,)),
+            dma((1,)),
             dma((nz,)),
-            dma((nz,)),
+            dma((1,)),
             dma((nz,)),
             dma((nz,)),
             dma((nz, pieces)),
-            dma((nz, pieces)),
-            dma((2,)),
+            dma((1,)),
         ],
         compiler_params=pltpu.CompilerParams(
             collective_id=0, has_side_effects=True, vmem_limit_bytes=32 * 1024 * 1024
@@ -828,7 +901,7 @@
     nz = lax.axis_size("frame")
     fits = (
         H % nz == 0 and (H // nz) % 8 == 0 and (H // nz) % CHUNK == 0 and W % 128 == 0
-        and H % 16 == 0 and (H // CHUNK) % 2 == 0 and lax.axis_size("row") <= 2
+        and H % 16 == 0 and H % (SEGMENTS * CHUNK) == 0 and lax.axis_size("row") <= 2
         and F % 4 == 0 and F < 8 and rank % 8 == 0 and 2 * rank + F * nz <= 128
     )
     run = whole_kernel if fits else local

time: 60 us -> 57.5 us (0.958)
  the two profiles are of different devices: /device:TPU:8 before, /device:TPU:0 now
where the time goes in v3:
time: 57.5 us; the launch traced here: 57.3 us
  Pallas kernels  56.7 us (99%)
  between operations  0.64 us (1%)
    pallas_call x1, Pallas kernels, whole_kernel(): pl.pallas_call(functools.partial(kernel, (F, H, W, rank, nr, nc, nz)), ou...  55.2 us
    pallas_call x1, Pallas kernels, whole_kernel(): pl.pallas_call(deliver, out_shape=(jax.ShapeDtypeStruct((F, H, W), f32),...  1.48 us

profile of v3, /device:TPU:0, one launch (start us, length us, event | category | flops | bytes accessed | tf_op | source)
XLA Modules:
  0.0 57.3 jit_solution(54579342562837194)
XLA Ops:
  0.6 55.2 %shard_map.76 = (f32[4,288,256]{2,1,0:T(8,128)S(1)}, f32[4,16]{1,0:T(4,128)S(1)}, f32[16,72,256]{2,1,0:T(8,128)S(1)}) custom-call(f32[4,16]{1,0:T(4,128)} %coeff_hbm.1, f32[4,288,256]{2,1,0:T(8,128)} %video_hbm.1, f32[4,288,256]{2,1,0:T(8,128)} %mult_hbm.1, f32[4,288,256]{2,1,0:T(8,128)} %fore_hbm.1, f32[16,288,256]{2,1,0:T(8,128)} %basis_hbm.1), custom_call_target="tpu_custom_call" | custom-call | tf_op jit(solution)/shard_map/pallas_call | solution.py:832
  55.8 1.5 %shard_map.77 = (f32[4,288,256]{2,1,0:T(8,128)}, f32[4,16]{1,0:T(4,128)}, f32[16,72,256]{2,1,0:T(8,128)}) custom-call(f32[4,288,256]{2,1,0:T(8,128)S(1)} %get-tuple-element.6.shrunk, f32[4,16]{1,0:T(4,128)S(1)} %get-tuple-element.7.coeff, f32[16,72,256]{2,1,0:T(8,128)S(1)} %get-tuple-element.8.fresh), custom_call_target="tpu_custom_call" | custom-call | tf_op jit(solution)/shard_map/pallas_call | solution.py:885

commit v4 on v3

--- a/solution.py
+++ b/solution.py
@@ -140,9 +140,9 @@
     result, coeff_out, fresh,
     field0, field1, field2, video, mult, basis, anchor, target, owned,
     packed, arrived, corner, edge_next, edge_flux, first_cols, left_now, left_next, bottom_row,
-    cross, sums, grams, parts, shares, square, table, coeff_ref, table_smem,
+    cross, sums, grams, gram_parts, inverse, parts, shares, square, table, coeff_ref, table_smem,
     in_sems, halo_send, halo_recv, part_send, part_recv,
-    gram_send, gram_recv, share_send, share_recv, move_send, move_recv, small_sem,
+    gram_send, gram_recv, total_send, total_recv, share_send, share_recv, move_send, move_recv, small_sem,
 ):
     field = (field0, field1, field2)
     F, H, W, rank, nr, nc, nz = sizes
@@ -170,6 +170,8 @@
 
     def half_start(h):
         return pl.multiple_of((h + flip * (1 - 2 * h)) * half, 8)
+
+    inner = (z > 0) & (z < nz - 1)
 
     def inside(dr, dc, dz):
         ok = None
@@ -267,18 +269,25 @@
         for i, (src, dst, step) in enumerate(column_list(k, j)):
             @pl.when(inside(*step))
             def _(i=i, src=src, dst=dst, step=step):
-                halo_copy(k, 6 + 4 * j + i, 6 + i, src, dst, step).start()
+                halo_copy(k, 6 + 2 * j + i % 2, 6 + i, src, dst, step).start()
 
     def wait_columns(k, j):
-        for i, (src, dst, step) in enumerate(column_list(k, j)):
-            @pl.when(inside(*(-s for s in step)))
-            def _(i=i, src=src, dst=dst, step=step):
-                halo_copy(k, 6 + 4 * j + i, 6 + i, src, dst, step).wait_recv()
+        for side, step, corner_step, small, large in (
+            (0, (0, -1, 0), (0, -1, 1), slice(1, F + 1), slice(0, F + 1)),
+            (1, (0, 1, 0), (0, 1, -1), slice(8, 8 + F), slice(8, 9 + F)),
+        ):
+            near = inside(*(-s for s in step))
+            both = inside(*(-s for s in corner_step))
+            for turn, rows in ((near & ~both, small), (both, large)):
+                @pl.when(turn)
+                def _(side=side, step=step, rows=rows):
+                    ref = arrived.at[k, j, rows]
+                    halo_copy(k, 6 + 2 * j + side, 0, ref, ref, step).wait_recv()
 
     def face(k, step, up):
         fk = field[k]
         rows = rows_at(step, 8)
-        at = 6 + 4 * SEGMENTS + 2 * step + (0 if up else 1)
+        at = 6 + 2 * SEGMENTS + step
         mine, theirs = (F, 0) if up else (1, F + 1)
         src = fore_hbm.at[mine - 1, rows_at(step)] if k == 0 else fk.at[mine, rows]
         return halo_copy(
@@ -294,10 +303,11 @@
                     face(k, step, up).start()
 
     def wait_face(k, step):
-        for up in (True, False):
-            @pl.when(inside(0, 0, -1 if up else 1))
-            def _(up=up):
-                face(k, step, up).wait_recv()
+        for turn, frames in ((inner, slice(0, 2)), (~inner, slice(0, 1))):
+            @pl.when(turn)
+            def _(frames=frames):
+                ref = field[k].at[frames, rows_at(step, 8), :]
+                halo_copy(k, 6 + 2 * SEGMENTS + step, 0, ref, ref, (0, 0, 1)).wait_recv()
 
     def send_halos(k, which):
         every = halo_list(k)
@@ -520,7 +530,18 @@
         tile = jnp.zeros((rank, 128), jnp.float32)
         for q in range(rank):
             tile = jnp.where(lane_r == q, jnp.sum(sums[q], axis=1, keepdims=True), tile)
+        lane = lax.broadcasted_iota(jnp.int32, (8, 128), 1)
+        tile = jnp.where(lane < rank, tile[:8], pltpu.roll(tile[8:], rank, 1))
+        tile = jnp.where(lane < 2 * rank, tile, pltpu.roll(pltpu.roll(tile, 4, 0), 2 * rank, 1))
+        tile = jnp.where(lane < 4 * rank, tile, pltpu.roll(pltpu.roll(tile, 6, 0), 4 * rank, 1))
         grams[z] = tile
+
+    def unfold(tile):
+        row = lax.broadcasted_iota(jnp.int32, (8, 128), 0)
+        tile = jnp.where(row < 2, tile, pltpu.roll(pltpu.roll(tile, 2, 0), 128 - 4 * rank, 1))
+        tile = jnp.where(row < 4, tile, pltpu.roll(pltpu.roll(tile, 4, 0), 128 - 2 * rank, 1))
+        tile = jnp.concatenate([tile, pltpu.roll(tile, 128 - rank, 1)], axis=0)
+        return jnp.where(lane_r < rank, tile, 0.0)
 
     def all_sent(block, sem):
         return pltpu.make_async_remote_copy(
@@ -530,7 +551,7 @@
 
     def share_gram(d):
         return pltpu.make_async_remote_copy(
-            src_ref=grams.at[z], dst_ref=grams.at[z],
+            src_ref=grams.at[z, 0:2], dst_ref=grams.at[z, 0:2],
             send_sem=gram_send.at[0], recv_sem=gram_recv.at[d],
             device_id=(r, c, lax.rem(z + d, nz)), device_id_type=MESH,
         )
@@ -538,9 +559,28 @@
     def take_gram(d):
         source = lax.rem(z - d + nz, nz)
         return pltpu.make_async_remote_copy(
-            src_ref=grams.at[z], dst_ref=grams.at[source],
+            src_ref=grams.at[z, 0:2], dst_ref=grams.at[source, 0:2],
             send_sem=gram_send.at[0], recv_sem=gram_recv.at[d],
             device_id=(r, c, source), device_id_type=MESH,
+        )
+
+    group = nr * nc
+    me = r * nc + c
+
+    def share_total(d):
+        other = lax.rem(me + d, group)
+        return pltpu.make_async_remote_copy(
+            src_ref=gram_parts.at[me, 0:2], dst_ref=gram_parts.at[me, 0:2],
+            send_sem=total_send.at[0], recv_sem=total_recv.at[d],
+            device_id=(other // nc, lax.rem(other, nc), z), device_id_type=MESH,
+        )
+
+    def take_total(d):
+        other = lax.rem(me - d + group, group)
+        return pltpu.make_async_remote_copy(
+            src_ref=gram_parts.at[me, 0:2], dst_ref=gram_parts.at[other, 0:2],
+            send_sem=total_send.at[0], recv_sem=total_recv.at[d],
+            device_id=(other // nc, lax.rem(other, nc), z), device_id_type=MESH,
         )
 
     def store_cross(i, j, value):
@@ -603,6 +643,22 @@
                 advance(k, step)
 
             final = j == SEGMENTS - 1
+            if k == PASSES - 2:
+                @pl.when(j == 2)
+                def _():
+                    for d in range(1, nz):
+                        share_gram(d).start()
+            if k == PASSES - 1:
+                @pl.when(j == 2)
+                def _():
+                    for d in range(1, nz):
+                        take_gram(d).wait_recv()
+                    total = grams[0]
+                    for i in range(1, nz):
+                        total = total + grams[i]
+                    gram_parts[me] = total
+                    for d in range(1, group):
+                        share_total(d).start()
 
             @pl.when(j == SEGMENTS - 2)
             def _():
@@ -629,11 +685,6 @@
                 send_columns(k + 1, j)
                 send_faces(k + 1, j * per, (j + 1) * per)
 
-        if k == PASSES - 2:
-            for d in range(1, nz):
-                share_gram(d).start()
-
-    inner = (z > 0) & (z < nz - 1)
 
     def send_held(turn, low, high):
         for b in range(nz):
@@ -656,12 +707,6 @@
     part = jnp.zeros((rank, 128), jnp.float32)
     for q in range(rank, rank + F):
         part = jnp.where(lane_r == q, jnp.sum(sums[q], axis=1, keepdims=True), part)
-    for d in range(1, nz):
-        take_gram(d).wait_recv()
-    for i in range(nz):
-        part = part + grams[i]
-    group = nr * nc
-    me = r * nc + c
     parts[me] = part
 
     def share_part(d):
@@ -689,17 +734,34 @@
         for f in range(F):
             before = jnp.where((row_r == q) & (lane_r == rank + f), coeff_ref[f, q], before)
     for d in range(1, group):
+        take_total(d).wait_recv()
+    total = gram_parts[0]
+    for i in range(1, group):
+        total = total + gram_parts[i]
+    diagonal = lane_r == row_r
+    system = unfold(total) + jnp.where(
+        diagonal, pixel_ridge, jnp.where(lane_r == row_r + rank, 1.0, 0.0)
+    )
+    system = eliminate(system, rank)
+    for q in range(rank):
+        inverse[q] = jnp.broadcast_to(system[:, rank + q : rank + q + 1], (rank, 128))
+    for d in range(1, group):
         take_part(d).wait_recv()
     total = parts[0]
     for i in range(1, group):
         total = total + parts[i]
-    total = total + pixel_ridge * (jnp.where(diagonal, 1.0, 0.0) + before)
-    solved = eliminate(total, rank)
-    shares[z] = solved
+    total = total + pixel_ridge * before
+    solved = inverse[0] * total[0:1, :]
+    for q in range(1, rank):
+        solved = solved + inverse[q] * total[q : q + 1, :]
+    square[...] = jnp.zeros_like(square)
+    square[0:rank, :] = solved
+    mine = square[...].T[rank : rank + F, :]
+    shares[pl.ds(z * F, F), :] = mine
 
     def share_rows(d):
         return pltpu.make_async_remote_copy(
-            src_ref=shares.at[z], dst_ref=shares.at[z],
+            src_ref=shares.at[pl.ds(z * F, F)], dst_ref=shares.at[pl.ds(z * F, F)],
             send_sem=share_send.at[0], recv_sem=share_recv.at[d],
             device_id=(r, c, lax.rem(z + d, nz)), device_id_type=MESH,
         )
@@ -707,7 +769,7 @@
     def take_rows(d):
         source = lax.rem(z - d + nz, nz)
         return pltpu.make_async_remote_copy(
-            src_ref=shares.at[z], dst_ref=shares.at[source],
+            src_ref=shares.at[pl.ds(z * F, F)], dst_ref=shares.at[pl.ds(source * F, F)],
             send_sem=share_send.at[0], recv_sem=share_recv.at[d],
             device_id=(r, c, source), device_id_type=MESH,
         )
@@ -716,9 +778,7 @@
         share_rows(d).start()
 
     send_held(inner, 0, pieces)
-    square[...] = jnp.zeros_like(square)
-    square[0:rank, :] = solved
-    coeff_out[...] = square[...].T[rank : rank + F, 0:rank]
+    coeff_out[...] = mine[:, 0:rank]
     for d in range(1, nz):
         take_rows(d).wait_recv()
     for b in range(nz):
@@ -731,12 +791,8 @@
                 move(b, p).start()
 
     frames = F * nz
-    wide = jnp.zeros((rank, 128), jnp.float32)
-    for i in range(nz):
-        placed = shares[i] if i == 0 else pltpu.roll(shares[i], i * F, 1)
-        wide = jnp.where(
-            (lane_r >= rank + i * F) & (lane_r < rank + (i + 1) * F), placed, wide
-        )
+    square[0:frames, :] = shares[...]
+    wide = pltpu.roll(square[...].T[0:rank, :], rank, 1)
     square[0:rank, :] = wide
     gram = lax.dot_general(
         wide, square[...], (((1,), (1,)), ((), ())),
@@ -768,8 +824,9 @@
 
     for k in range(PASSES - 2, PASSES):
         finish_sends(k)
-    for src, sem in ((shares, share_send), (grams, gram_send)):
-        all_sent(src.at[0 : nz - 1], sem).wait_send()
+    all_sent(shares.at[0 : (nz - 1) * F], share_send).wait_send()
+    all_sent(grams.at[0 : nz - 1, 0:2], gram_send).wait_send()
+    all_sent(gram_parts.at[0 : group - 1, 0:2], total_send).wait_send()
     all_sent(parts.at[0 : group - 1], part_send).wait_send()
 
     for n in range(nz - 1):
@@ -853,20 +910,24 @@
             vmem((8, 128), f32),
             vmem((F, rank, 8, 128), f32),
             vmem((rank + F, rank, 128), f32),
-            vmem((nz, rank, 128), f32),
+            vmem((nz, 8, 128), f32),
+            vmem((group, 8, 128), f32),
+            vmem((rank, rank, 128), f32),
             vmem((group, rank, 128), f32),
-            vmem((nz, rank, 128), f32),
+            vmem((nz * F, 128), f32),
             vmem((128, 128), f32),
             vmem((rank, 128), f32),
             pltpu.SMEM((F, rank), f32),
             pltpu.SMEM((rank, 128), f32),
             dma((9,)),
             dma((2, 12)),
-            dma((2, 6 + 4 * SEGMENTS + 2 * (H // CHUNK))),
+            dma((2, 6 + 2 * SEGMENTS + H // CHUNK)),
             dma((1,)),
             dma((group,)),
             dma((1,)),
             dma((nz,)),
+            dma((1,)),
+            dma((group,)),
             dma((1,)),
             dma((nz,)),
             dma((nz,)),
@@ -902,7 +963,7 @@
     fits = (
         H % nz == 0 and (H // nz) % 8 == 0 and (H // nz) % CHUNK == 0 and W % 128 == 0
         and H % 16 == 0 and H % (SEGMENTS * CHUNK) == 0 and lax.axis_size("row") <= 2
-        and F % 4 == 0 and F < 8 and rank % 8 == 0 and 2 * rank + F * nz <= 128
+        and F % 4 == 0 and F < 8 and rank == 16 and nz >= 2 and F * nz == rank and 2 * rank + F * nz <= 128
     )
     run = whole_kernel if fits else local
     return run(video, multiplier, foreground, basis, coefficients)

time: 57.5 us -> 56.2 us (0.977)
  Pallas kernels: 56.7 us -> 55.4 us
    pallas_call x1, Pallas kernels: 55.2 us -> 53.9 us  [whole_kernel(): pl.pallas_call(functools.partial(kernel, (F, H, W, rank, nr, nc, nz)), ou...]
where the time goes in v4:
time: 56.2 us; the launch traced here: 56.1 us
  Pallas kernels  55.4 us (99%)
  between operations  0.64 us (1%)
    pallas_call x1, Pallas kernels, whole_kernel(): pl.pallas_call(functools.partial(kernel, (F, H, W, rank, nr, nc, nz)), ou...  53.9 us
    pallas_call x1, Pallas kernels, whole_kernel(): pl.pallas_call(deliver, out_shape=(jax.ShapeDtypeStruct((F, H, W), f32),...  1.48 us

profile of v4, /device:TPU:0, one launch (start us, length us, event | category | flops | bytes accessed | tf_op | source)
XLA Modules:
  0.0 56.1 jit_solution(16924909937537584969)
XLA Ops:
  0.6 53.9 %shard_map.76 = (f32[4,288,256]{2,1,0:T(8,128)S(1)}, f32[4,16]{1,0:T(4,128)S(1)}, f32[16,72,256]{2,1,0:T(8,128)S(1)}) custom-call(f32[4,16]{1,0:T(4,128)} %coeff_hbm.1, f32[4,288,256]{2,1,0:T(8,128)} %video_hbm.1, f32[4,288,256]{2,1,0:T(8,128)} %mult_hbm.1, f32[4,288,256]{2,1,0:T(8,128)} %fore_hbm.1, f32[16,288,256]{2,1,0:T(8,128)} %basis_hbm.1), custom_call_target="tpu_custom_call" | custom-call | tf_op jit(solution)/shard_map/pallas_call | solution.py:889
  54.6 1.5 %shard_map.77 = (f32[4,288,256]{2,1,0:T(8,128)}, f32[4,16]{1,0:T(4,128)}, f32[16,72,256]{2,1,0:T(8,128)}) custom-call(f32[4,288,256]{2,1,0:T(8,128)S(1)} %get-tuple-element.6.shrunk, f32[4,16]{1,0:T(4,128)S(1)} %get-tuple-element.7.coeff, f32[16,72,256]{2,1,0:T(8,128)S(1)} %get-tuple-element.8.fresh), custom_call_target="tpu_custom_call" | custom-call | tf_op jit(solution)/shard_map/pallas_call | solution.py:946

commit v5 on v4

--- a/solution.py
+++ b/solution.py
@@ -269,7 +269,7 @@
         for i, (src, dst, step) in enumerate(column_list(k, j)):
             @pl.when(inside(*step))
             def _(i=i, src=src, dst=dst, step=step):
-                halo_copy(k, 6 + 2 * j + i % 2, 6 + i, src, dst, step).start()
+                halo_copy(k, 3 + 2 * j + i % 2, 3 + i, src, dst, step).start()
 
     def wait_columns(k, j):
         for side, step, corner_step, small, large in (
@@ -282,16 +282,16 @@
                 @pl.when(turn)
                 def _(side=side, step=step, rows=rows):
                     ref = arrived.at[k, j, rows]
-                    halo_copy(k, 6 + 2 * j + side, 0, ref, ref, step).wait_recv()
+                    halo_copy(k, 3 + 2 * j + side, 0, ref, ref, step).wait_recv()
 
     def face(k, step, up):
         fk = field[k]
         rows = rows_at(step, 8)
-        at = 6 + 2 * SEGMENTS + step
+        at = 3 + 2 * SEGMENTS + step
         mine, theirs = (F, 0) if up else (1, F + 1)
         src = fore_hbm.at[mine - 1, rows_at(step)] if k == 0 else fk.at[mine, rows]
         return halo_copy(
-            k, at, 10 if up else 11, src, fk.at[theirs, rows], (0, 0, 1 if up else -1)
+            k, at, 7 if up else 8, src, fk.at[theirs, rows], (0, 0, 1 if up else -1)
         )
 
     def send_faces(k, low, high):
@@ -307,7 +307,7 @@
             @pl.when(turn)
             def _(frames=frames):
                 ref = field[k].at[frames, rows_at(step, 8), :]
-                halo_copy(k, 6 + 2 * SEGMENTS + step, 0, ref, ref, (0, 0, 1)).wait_recv()
+                halo_copy(k, 3 + 2 * SEGMENTS + step, 0, ref, ref, (0, 0, 1)).wait_recv()
 
     def send_halos(k, which):
         every = halo_list(k)
@@ -316,7 +316,7 @@
 
             @pl.when(inside(*step))
             def _(i=i, src=src, dst=dst, step=step):
-                halo_copy(k, i, i, src, dst, step).start()
+                halo_copy(k, i // 2, i // 2, src, dst, step).start()
 
     def wait_halos(k, which):
         every = halo_list(k)
@@ -325,13 +325,13 @@
 
             @pl.when(inside(*(-s for s in step)))
             def _(i=i, src=src, dst=dst, step=step):
-                halo_copy(k, i, i, src, dst, step).wait_recv()
+                halo_copy(k, i // 2, i // 2, src, dst, step).wait_recv()
 
     def finish_sends(k):
         for i, (src, dst, step) in enumerate(halo_list(k)):
             @pl.when(inside(*step))
             def _(i=i, src=src, dst=dst, step=step):
-                halo_copy(k, i, i, src, dst, step).wait_send()
+                halo_copy(k, i // 2, i // 2, src, dst, step).wait_send()
 
         every = (
             (packed.at[k, :, 0:F], arrived.at[k, :, 1 : F + 1], (0, -1, 0)),
@@ -344,7 +344,7 @@
         for i, (src, dst, step) in enumerate(every):
             @pl.when(inside(*step))
             def _(i=i, src=src, dst=dst, step=step):
-                halo_copy(k, 0, 6 + i, src, dst, step).wait_send()
+                halo_copy(k, 0, 3 + i, src, dst, step).wait_send()
 
     def prepare_columns(k, j):
         base = segment_start(j)
@@ -549,19 +549,17 @@
             device_id=(r, c, lax.rem(z + 1, nz)), device_id_type=MESH,
         )
 
+    def all_here(block, sem):
+        return pltpu.make_async_remote_copy(
+            src_ref=block, dst_ref=block, send_sem=sem.at[0], recv_sem=sem.at[0],
+            device_id=(r, c, lax.rem(z + 1, nz)), device_id_type=MESH,
+        )
+
     def share_gram(d):
         return pltpu.make_async_remote_copy(
             src_ref=grams.at[z, 0:2], dst_ref=grams.at[z, 0:2],
-            send_sem=gram_send.at[0], recv_sem=gram_recv.at[d],
+            send_sem=gram_send.at[0], recv_sem=gram_recv.at[0],
             device_id=(r, c, lax.rem(z + d, nz)), device_id_type=MESH,
-        )
-
-    def take_gram(d):
-        source = lax.rem(z - d + nz, nz)
-        return pltpu.make_async_remote_copy(
-            src_ref=grams.at[z, 0:2], dst_ref=grams.at[source, 0:2],
-            send_sem=gram_send.at[0], recv_sem=gram_recv.at[d],
-            device_id=(r, c, source), device_id_type=MESH,
         )
 
     group = nr * nc
@@ -571,15 +569,7 @@
         other = lax.rem(me + d, group)
         return pltpu.make_async_remote_copy(
             src_ref=gram_parts.at[me, 0:2], dst_ref=gram_parts.at[me, 0:2],
-            send_sem=total_send.at[0], recv_sem=total_recv.at[d],
-            device_id=(other // nc, lax.rem(other, nc), z), device_id_type=MESH,
-        )
-
-    def take_total(d):
-        other = lax.rem(me - d + group, group)
-        return pltpu.make_async_remote_copy(
-            src_ref=gram_parts.at[me, 0:2], dst_ref=gram_parts.at[other, 0:2],
-            send_sem=total_send.at[0], recv_sem=total_recv.at[d],
+            send_sem=total_send.at[0], recv_sem=total_recv.at[0],
             device_id=(other // nc, lax.rem(other, nc), z), device_id_type=MESH,
         )
 
@@ -644,15 +634,14 @@
 
             final = j == SEGMENTS - 1
             if k == PASSES - 2:
-                @pl.when(j == 2)
+                @pl.when(j == 1)
                 def _():
                     for d in range(1, nz):
                         share_gram(d).start()
             if k == PASSES - 1:
-                @pl.when(j == 2)
+                @pl.when(j == 1)
                 def _():
-                    for d in range(1, nz):
-                        take_gram(d).wait_recv()
+                    all_here(grams.at[0 : nz - 1, 0:2], gram_recv).wait_recv()
                     total = grams[0]
                     for i in range(1, nz):
                         total = total + grams[i]
@@ -713,15 +702,7 @@
         other = lax.rem(me + d, group)
         return pltpu.make_async_remote_copy(
             src_ref=parts.at[me], dst_ref=parts.at[me],
-            send_sem=part_send.at[0], recv_sem=part_recv.at[d],
-            device_id=(other // nc, lax.rem(other, nc), z), device_id_type=MESH,
-        )
-
-    def take_part(d):
-        other = lax.rem(me - d + group, group)
-        return pltpu.make_async_remote_copy(
-            src_ref=parts.at[me], dst_ref=parts.at[other],
-            send_sem=part_send.at[0], recv_sem=part_recv.at[d],
+            send_sem=part_send.at[0], recv_sem=part_recv.at[0],
             device_id=(other // nc, lax.rem(other, nc), z), device_id_type=MESH,
         )
 
@@ -733,8 +714,7 @@
     for q in range(rank):
         for f in range(F):
             before = jnp.where((row_r == q) & (lane_r == rank + f), coeff_ref[f, q], before)
-    for d in range(1, group):
-        take_total(d).wait_recv()
+    all_here(gram_parts.at[0 : group - 1, 0:2], total_recv).wait_recv()
     total = gram_parts[0]
     for i in range(1, group):
         total = total + gram_parts[i]
@@ -745,8 +725,7 @@
     system = eliminate(system, rank)
     for q in range(rank):
         inverse[q] = jnp.broadcast_to(system[:, rank + q : rank + q + 1], (rank, 128))
-    for d in range(1, group):
-        take_part(d).wait_recv()
+    all_here(parts.at[0 : group - 1], part_recv).wait_recv()
     total = parts[0]
     for i in range(1, group):
         total = total + parts[i]
@@ -762,16 +741,8 @@
     def share_rows(d):
         return pltpu.make_async_remote_copy(
             src_ref=shares.at[pl.ds(z * F, F)], dst_ref=shares.at[pl.ds(z * F, F)],
-            send_sem=share_send.at[0], recv_sem=share_recv.at[d],
+            send_sem=share_send.at[0], recv_sem=share_recv.at[0],
             device_id=(r, c, lax.rem(z + d, nz)), device_id_type=MESH,
-        )
-
-    def take_rows(d):
-        source = lax.rem(z - d + nz, nz)
-        return pltpu.make_async_remote_copy(
-            src_ref=shares.at[pl.ds(z * F, F)], dst_ref=shares.at[pl.ds(source * F, F)],
-            send_sem=share_send.at[0], recv_sem=share_recv.at[d],
-            device_id=(r, c, source), device_id_type=MESH,
         )
 
     for d in range(1, nz):
@@ -779,8 +750,7 @@
 
     send_held(inner, 0, pieces)
     coeff_out[...] = mine[:, 0:rank]
-    for d in range(1, nz):
-        take_rows(d).wait_recv()
+    all_here(shares.at[0 : (nz - 1) * F], share_recv).wait_recv()
     for b in range(nz):
         @pl.when(held(b) & ~inner)
         def _(b=b):
@@ -920,16 +890,16 @@
             pltpu.SMEM((F, rank), f32),
             pltpu.SMEM((rank, 128), f32),
             dma((9,)),
-            dma((2, 12)),
-            dma((2, 6 + 2 * SEGMENTS + H // CHUNK)),
+            dma((2, 9)),
+            dma((2, 3 + 2 * SEGMENTS + H // CHUNK)),
             dma((1,)),
-            dma((group,)),
             dma((1,)),
-            dma((nz,)),
             dma((1,)),
-            dma((group,)),
             dma((1,)),
-            dma((nz,)),
+            dma((1,)),
+            dma((1,)),
+            dma((1,)),
+            dma((1,)),
             dma((nz,)),
             dma((nz, pieces)),
             dma((1,)),

time: 56.2 us -> 55.9 us (level)
  no operation moved by 1% of the time
where the time goes in v5:
time: 55.9 us; the launch traced here: 55.8 us
  Pallas kernels  55.1 us (99%)
  between operations  0.64 us (1%)
    pallas_call x1, Pallas kernels, whole_kernel(): pl.pallas_call(functools.partial(kernel, (F, H, W, rank, nr, nc, nz)), ou...  53.6 us
    pallas_call x1, Pallas kernels, whole_kernel(): pl.pallas_call(deliver, out_shape=(jax.ShapeDtypeStruct((F, H, W), f32),...  1.48 us

profile of v5, /device:TPU:0, one launch (start us, length us, event | category | flops | bytes accessed | tf_op | source)
XLA Modules:
  0.0 55.8 jit_solution(2012646334311629631)
XLA Ops:
  0.6 53.6 %shard_map.76 = (f32[4,288,256]{2,1,0:T(8,128)S(1)}, f32[4,16]{1,0:T(4,128)S(1)}, f32[16,72,256]{2,1,0:T(8,128)S(1)}) custom-call(f32[4,16]{1,0:T(4,128)} %coeff_hbm.1, f32[4,288,256]{2,1,0:T(8,128)} %video_hbm.1, f32[4,288,256]{2,1,0:T(8,128)} %mult_hbm.1, f32[4,288,256]{2,1,0:T(8,128)} %fore_hbm.1, f32[16,288,256]{2,1,0:T(8,128)} %basis_hbm.1), custom_call_target="tpu_custom_call" | custom-call | tf_op jit(solution)/shard_map/pallas_call | solution.py:859
  54.3 1.5 %shard_map.77 = (f32[4,288,256]{2,1,0:T(8,128)}, f32[4,16]{1,0:T(4,128)}, f32[16,72,256]{2,1,0:T(8,128)}) custom-call(f32[4,288,256]{2,1,0:T(8,128)S(1)} %get-tuple-element.6.shrunk, f32[4,16]{1,0:T(4,128)S(1)} %get-tuple-element.7.coeff, f32[16,72,256]{2,1,0:T(8,128)S(1)} %get-tuple-element.8.fresh), custom_call_target="tpu_custom_call" | custom-call | tf_op jit(solution)/shard_map/pallas_call | solution.py:916

commit v6 on v1

v6 whole, which is shorter than its diff:
```python
import functools

import jax
import jax.numpy as jnp
from jax import lax
from jax.experimental import pallas as pl
from jax.experimental.pallas import tpu as pltpu
from jax.sharding import PartitionSpec as P

PASSES = 3


relax_rate = 0.8
smooth_weight = 0.5
smooth_floor = 0.25
shrink_level = 0.4
dual_scale = 0.8
ridge_share = 0.1


def with_halo(block, sides, width):
    for axis, dim in sides:
        count = lax.axis_size(axis)
        forward = [(i, i + 1) for i in range(count - 1)]
        backward = [(target, source) for source, target in forward]
        low = lax.ppermute(
            lax.slice_in_dim(block, block.shape[dim] - width, None, axis=dim), axis, forward
        )
        high = lax.ppermute(lax.slice_in_dim(block, 0, width, axis=dim), axis, backward)
        block = jnp.concatenate([low, block, high], axis=dim)
    return block


def forward_cells(padded, direction, shape):
    starts = [0, 0, 0]
    starts[direction] = 1
    limits = [starts[axis_dim] + shape[axis_dim] for axis_dim in range(3)]
    return lax.slice(padded, starts, limits)


def descend(padded, source, anchor, extent):
    shape = tuple((int(length) - 1 for length in padded.shape))
    here_cells = padded[:-1, :-1, :-1]
    slopes = []
    for direction in range(3):
        ahead_cells = forward_cells(padded, direction, shape)
        places = anchor[direction] + jnp.arange(shape[direction], dtype=jnp.int32)
        inside = (places >= 0) & (places < extent[direction] - 1)
        layout = [1, 1, 1]
        layout[direction] = shape[direction]
        inside = inside.reshape(layout)
        slopes.append(jnp.where(inside, ahead_cells - here_cells, jnp.zeros_like(here_cells)))
    weight = lax.rsqrt(
        smooth_floor + slopes[0] * slopes[0] + slopes[1] * slopes[1] + slopes[2] * slopes[2]
    )
    fluxes = [slope_part * weight for slope_part in slopes]
    spread = (
        fluxes[0][1:, 1:, 1:]
        - fluxes[0][:-1, 1:, 1:]
        + (fluxes[1][1:, 1:, 1:] - fluxes[1][1:, :-1, 1:])
        + (fluxes[2][1:, 1:, 1:] - fluxes[2][1:, 1:, :-1])
    )
    center = padded[1:-1, 1:-1, 1:-1]
    return center + relax_rate * (source - center + smooth_weight * spread)


def solve_definite(matrix, right_side):
    factor_lower = jnp.linalg.cholesky(matrix)
    half_solved = lax.linalg.triangular_solve(factor_lower, right_side, left_side=True, lower=True)
    return lax.linalg.triangular_solve(
        factor_lower, half_solved, left_side=True, lower=True, transpose_a=True
    )


def local(video, multiplier, foreground, basis, coefficients):
    highest = lax.Precision.HIGHEST
    frames_here, rows_here, cols_here = video.shape
    rank_size = basis.shape[0]
    frame_count = lax.axis_size("frame")
    row_count = lax.axis_size("row")
    col_count = lax.axis_size("col")
    extent = (frames_here * frame_count, rows_here * row_count, cols_here * col_count)
    frame_slot = lax.axis_index("frame")
    corner = (
        frame_slot * frames_here,
        lax.axis_index("row") * rows_here,
        lax.axis_index("col") * cols_here,
    )
    pixels = rows_here * cols_here
    flat_basis = basis.reshape(rank_size, pixels)
    background = jnp.dot(coefficients, flat_basis, precision=highest).reshape(video.shape)
    target = video - background + dual_scale * multiplier
    current = foreground
    for sweep in range(PASSES):
        padded = with_halo(current, (("row", 1), ("col", 2), ("frame", 0)), 1)
        current = descend(padded, target, tuple((start_cell - 1 for start_cell in corner)), extent)
    shrunk = current - jnp.clip(current, -shrink_level, shrink_level)
    residual_target = video + dual_scale * multiplier - shrunk
    flat_target = residual_target.reshape(frames_here, pixels)
    gram_part = jnp.dot(flat_basis, flat_basis.T, precision=highest)
    cross_part = jnp.dot(flat_basis, flat_target.T, precision=highest)
    gram_sum, cross_sum = lax.psum((gram_part, cross_part), ("row", "col"))
    identity_matrix = jnp.eye(rank_size, dtype=gram_sum.dtype)
    pixel_ridge = ridge_share * pixels * row_count * col_count
    coeff_rows = solve_definite(
        gram_sum + pixel_ridge * identity_matrix, cross_sum + pixel_ridge * coefficients.T
    )
    total_part = jnp.dot(coeff_rows, flat_target, precision=highest).reshape(
        rank_size, rows_here, cols_here
    )
    frame_gram_part = jnp.dot(coeff_rows, coeff_rows.T, precision=highest)
    owned_rows = rows_here // frame_count
    owned_sums = lax.psum_scatter(total_part, "frame", scatter_dimension=1, tiled=True)
    frame_gram = lax.psum(frame_gram_part, "frame")
    old_owned = lax.dynamic_slice_in_dim(basis, frame_slot * owned_rows, owned_rows, 1)
    frame_ridge = ridge_share * frames_here * frame_count
    right_side = (owned_sums + frame_ridge * old_owned).reshape(rank_size, owned_rows * cols_here)
    new_basis = solve_definite(frame_gram + frame_ridge * identity_matrix, right_side)
    return (shrunk, coeff_rows.T, new_basis.reshape(rank_size, owned_rows, cols_here))


MESH = pl.DeviceIdType.MESH
CHUNK = 24
SEGMENTS = 4


def eliminate(matrix, size):
    lanes = lax.broadcasted_iota(jnp.int32, matrix.shape, 1)
    rows = lax.broadcasted_iota(jnp.int32, matrix.shape, 0)
    for k in range(size):
        pivot = matrix[k : k + 1, k : k + 1]
        scaled = matrix[k : k + 1, :] / pivot
        column = jnp.sum(jnp.where(lanes == k, matrix, 0.0), axis=1, keepdims=True)
        matrix = jnp.where(rows == k, scaled, matrix - column * scaled)
    return matrix


def kernel(
    sizes, coeff_hbm, video_hbm, mult_hbm, fore_hbm, basis_hbm,
    result, coeff_out, fresh,
    field0, field1, field2, video, mult, basis, anchor, target, owned,
    packed, arrived, corner, edge_next, edge_flux, first_cols, left_now, left_next, bottom_row,
    cross, sums, grams, gram_parts, inverse, parts, shares, square, table, coeff_ref, table_smem,
    move_send, move_recv,
):
    field = (field0, field1, field2)
    F, H, W, rank, nr, nc, nz = sizes
    r = lax.axis_index("row")
    c = lax.axis_index("col")
    z = lax.axis_index("frame")
    own = H // nz
    pieces = own // CHUNK
    half = H // 2
    flip = lax.rem(r, 2)

    steps = H // CHUNK

    def chunk_at(step):
        return step + flip * (steps - 1 - 2 * step)

    def rows_at(step, offset=0):
        return pl.ds(pl.multiple_of(offset + chunk_at(step) * CHUNK, 8), CHUNK)

    span = H // SEGMENTS
    per = steps // SEGMENTS

    def segment_start(j):
        return pl.multiple_of((j + flip * (SEGMENTS - 1 - 2 * j)) * span, 8)

    def half_start(h):
        return pl.multiple_of((h + flip * (1 - 2 * h)) * half, 8)

    inner = (z > 0) & (z < nz - 1)

    def inside(dr, dc, dz):
        ok = None
        for at, step, count in ((r, dr, nr), (c, dc, nc), (z, dz, nz)):
            if step != 0:
                test = (at + step >= 0) & (at + step < count)
                ok = test if ok is None else ok & test
        return ok

    def take(source, piece):
        rows = pl.ds(pl.multiple_of(z * own + piece * CHUNK, 8), CHUNK)
        spot = pl.ds(pl.multiple_of(piece * CHUNK, 8), CHUNK)
        return pltpu.make_async_remote_copy(
            src_ref=anchor.at[:, rows, :], dst_ref=owned.at[pl.ds(source * F, F), spot, :],
            send_sem=move_send.at[source], recv_sem=move_recv.at[source, piece],
            device_id=(r, c, source), device_id_type=MESH,
        )

    def work(
        in_sems, halo_send, halo_recv, part_send, part_recv, gram_send, gram_recv,
        total_send, total_recv, share_send, share_recv, small_sem,
    ):
        halves = [pl.ds(half_start(h), half) for h in range(2)]
        loads = [
            pltpu.make_async_copy(src, dst, in_sems.at[i])
            for i, (src, dst) in enumerate(
                [
                    (
                        fore_hbm.at[:, halves[h], :],
                        field0.at[1 : F + 1, pl.ds(pl.multiple_of(half_start(h) + 8, 8), half), :],
                    )
                    for h in range(2)
                ]
                + [(coeff_hbm, coeff_ref)]
                + [
                    (src.at[:, rows, :], dst.at[:, rows, :])
                    for rows in halves
                    for src, dst in ((video_hbm, video), (mult_hbm, mult), (basis_hbm, basis))
                ]
            )
        ]
        for load in loads[:2]:
            load.start()

        barrier = pltpu.get_barrier_semaphore()
        beside = ((0, 0, 1), (0, 1, 0), (1, 0, 0), (1, 0, -1), (0, 1, -1), (1, -1, 0))
        beside += tuple(tuple(-s for s in step) for step in beside)
        for step in beside:
            @pl.when(inside(*step))
            def _(step=step):
                pl.semaphore_signal(
                    barrier,
                    inc=1,
                    device_id=(r + step[0], c + step[1], z + step[2]),
                    device_id_type=MESH,
                )
        expected = jnp.int32(0)
        for step in beside:
            expected = expected + inside(*step).astype(jnp.int32)
        for load in loads[2:]:
            load.start()

        pl.semaphore_wait(barrier, expected)

        lane_h = lax.broadcasted_iota(jnp.int32, (span, 128), 1)

        def pack_columns(k, j):
            base = segment_start(j)
            tile = jnp.zeros((span, 128), jnp.float32)
            for f in range(F):
                for lane, at in ((f, 0), (8 + f, W - 1)):
                    lanes = field[k][f + 1, pl.ds(base + 8, span), (at // 128) * 128 : (at // 128) * 128 + 128]
                    tile = jnp.where(lane_h == lane, lanes[:, at % 128 : at % 128 + 1], tile)
            first_cols[pl.ds(base + 8, span), :] = tile
            packed[k, j] = tile.T[:16, :]

        strips = range(4)
        corners = (4, 5)

        def column_list(k, j):
            return (
                (packed.at[k, j, 0:F], arrived.at[k, j, 1 : F + 1], (0, -1, 0)),
                (packed.at[k, j, 8 : 8 + F], arrived.at[k, j, 8 : 8 + F], (0, 1, 0)),
                (packed.at[k, j, F - 1 : F], arrived.at[k, j, 0:1], (0, -1, 1)),
                (packed.at[k, j, 8:9], arrived.at[k, j, 8 + F : 9 + F], (0, 1, -1)),
            )

        def halo_list(k):
            fk = field[k]
            mid = slice(1, F + 1)
            return (
                (fk.at[mid, H : H + 8, :], fk.at[mid, 0:8, :], (1, 0, 0)),
                (fk.at[mid, 8:16, :], fk.at[mid, H + 8 : H + 16, :], (-1, 0, 0)),
                (fk.at[F, 8:9, :], fk.at[0, H + 8 : H + 9, :], (-1, 0, 1)),
                (fk.at[1, H + 7 : H + 8, :], fk.at[F + 1, 7:8, :], (1, 0, -1)),
                (fk.at[mid, H : H + 8, 0:128], corner.at[k, 0], (1, -1, 0)),
                (fk.at[mid, 8:16, W - 128 : W], corner.at[k, 1], (-1, 1, 0)),
            )

        def halo_copy(k, i, leave, src, dst, step):
            return pltpu.make_async_remote_copy(
                src_ref=src, dst_ref=dst,
                send_sem=halo_send.at[k % 2, leave], recv_sem=halo_recv.at[k % 2, i],
                device_id=(r + step[0], c + step[1], z + step[2]), device_id_type=MESH,
            )

        def send_columns(k, j):
            for i, (src, dst, step) in enumerate(column_list(k, j)):
                @pl.when(inside(*step))
                def _(i=i, src=src, dst=dst, step=step):
                    halo_copy(k, 3 + 2 * j + i % 2, 3 + i, src, dst, step).start()

        def wait_columns(k, j):
            for side, step, corner_step, small, large in (
                (0, (0, -1, 0), (0, -1, 1), slice(1, F + 1), slice(0, F + 1)),
                (1, (0, 1, 0), (0, 1, -1), slice(8, 8 + F), slice(8, 9 + F)),
            ):
                near = inside(*(-s for s in step))
                both = inside(*(-s for s in corner_step))
                for turn, rows in ((near & ~both, small), (both, large)):
                    @pl.when(turn)
                    def _(side=side, step=step, rows=rows):
                        ref = arrived.at[k, j, rows]
                        halo_copy(k, 3 + 2 * j + side, 0, ref, ref, step).wait_recv()

        def face(k, step, up):
            fk = field[k]
            rows = rows_at(step, 8)
            at = 3 + 2 * SEGMENTS + step
            mine, theirs = (F, 0) if up else (1, F + 1)
            src = fore_hbm.at[mine - 1, rows_at(step)] if k == 0 else fk.at[mine, rows]
            return halo_copy(
                k, at, 7 if up else 8, src, fk.at[theirs, rows], (0, 0, 1 if up else -1)
            )

        def send_faces(k, low, high):
            @pl.loop(low, high)
            def _(step):
                for up in (True, False):
                    @pl.when(inside(0, 0, 1 if up else -1))
                    def _(up=up):
                        face(k, step, up).start()

        def wait_face(k, step):
            for turn, frames in ((inner, slice(0, 2)), (~inner, slice(0, 1))):
                @pl.when(turn)
                def _(frames=frames):
                    ref = field[k].at[frames, rows_at(step, 8), :]
                    halo_copy(k, 3 + 2 * SEGMENTS + step, 0, ref, ref, (0, 0, 1)).wait_recv()

        def send_halos(k, which):
            every = halo_list(k)
            for i in which:
                src, dst, step = every[i]

                @pl.when(inside(*step))
                def _(i=i, src=src, dst=dst, step=step):
                    halo_copy(k, i // 2, i // 2, src, dst, step).start()

        def wait_halos(k, which):
            every = halo_list(k)
            for i in which:
                src, dst, step = every[i]

                @pl.when(inside(*(-s for s in step)))
                def _(i=i, src=src, dst=dst, step=step):
                    halo_copy(k, i // 2, i // 2, src, dst, step).wait_recv()

        def finish_sends(k):
            for i, (src, dst, step) in enumerate(halo_list(k)):
                @pl.when(inside(*step))
                def _(i=i, src=src, dst=dst, step=step):
                    halo_copy(k, i // 2, i // 2, src, dst, step).wait_send()

            every = (
                (packed.at[k, :, 0:F], arrived.at[k, :, 1 : F + 1], (0, -1, 0)),
                (packed.at[k, :, 8 : 8 + F], arrived.at[k, :, 8 : 8 + F], (0, 1, 0)),
                (packed.at[k, :, F - 1 : F], arrived.at[k, :, 0:1], (0, -1, 1)),
                (packed.at[k, :, 8:9], arrived.at[k, :, 8 + F : 9 + F], (0, 1, -1)),
                (field[k].at[F, 8 : H + 8, :], field[k].at[0, 8 : H + 8, :], (0, 0, 1)),
                (field[k].at[1, 8 : H + 8, :], field[k].at[F + 1, 8 : H + 8, :], (0, 0, -1)),
            )
            for i, (src, dst, step) in enumerate(every):
                @pl.when(inside(*step))
                def _(i=i, src=src, dst=dst, step=step):
                    halo_copy(k, 0, 3 + i, src, dst, step).wait_send()

        def prepare_columns(k, j):
            base = segment_start(j)
            spread = jnp.concatenate(
                [arrived[k, j], jnp.zeros((112, span), jnp.float32)], axis=0
            ).T
            edge_next[pl.ds(base + 8, span), :] = spread
            left_now[pl.ds(base + 8, span), :] = pltpu.roll(spread, 120, 1)
            left_next[pl.ds(base + 8, span), :] = pltpu.roll(spread, 119, 1)
            low, count = pl.multiple_of(base + 8 * flip, 8), span + 8
            here = left_now[pl.ds(low, count), :]
            ahead = left_next[pl.ds(low, count), :]
            lane = lax.broadcasted_iota(jnp.int32, (count, 128), 1)
            row = lax.broadcasted_iota(jnp.int32, (count, 128), 0) + (low - 8)
            slope0 = jnp.where((lane == F - 1) & (z == nz - 1), 0.0, ahead - here)
            after = left_now[pl.ds(low, count + 8), :]
            below = jnp.where(
                row == H - 1, bottom_row[0:1, :], pltpu.roll(after, count + 7, 0)[:count]
            )
            slope1 = jnp.where((row == H - 1) & (r == nr - 1), 0.0, below - here)
            slope2 = first_cols[pl.ds(low, count), :] - here
            weight = lax.rsqrt(smooth_floor + slope0 * slope0 + slope1 * slope1 + slope2 * slope2)
            edge_flux[pl.ds(low, count), :] = jnp.where(c == 0, 0.0, slope2 * weight)

        def take_corners(k):
            wait_halos(k, corners)
            lane8 = lax.broadcasted_iota(jnp.int32, (8, 128), 1)
            top = jnp.zeros((8, 128), jnp.float32)
            bottom = jnp.zeros((8, 128), jnp.float32)
            for f in range(F):
                top = jnp.where(lane8 == f + 1, corner[k, 0, f][:, 0:1], top)
                bottom = jnp.where(lane8 == f, corner[k, 1, f][:, 127:128], bottom)
            edge_next[0:8, :] = top
            bottom_row[...] = bottom

        def sweep(k, last, start):
            R = CHUNK
            tiles = W // 128
            row_8 = lax.broadcasted_iota(jnp.int32, (8, 128), 0) + (r * H + start)
            above_image = row_8 - 8 < 0
            last_image_row = row_8 + (R - 8) >= nr * H - 1
            columns = edge_next[pl.ds(start, R + 8), :]
            fluxes_in = edge_flux[pl.ds(start + 8, R), :]
            at = pl.ds(start, R)

            def frame(f):
                return [
                    field[k][f, pl.ds(start, R + 16), w * 128 : w * 128 + 128] for w in range(tiles)
                ]

            now = frame(0)
            flux0_before = None
            for f in range(-1, F):
                after = frame(f + 2)
                skip = 8 if f < 0 else 0
                n = R + 8 - skip
                lane = lax.broadcasted_iota(jnp.int32, (n, 128), 1)
                here = [t[skip : R + 8] for t in now]
                turned = [pltpu.roll(t, 127, 1) for t in here]
                wall = jnp.broadcast_to(columns[skip:, f + 1 : f + 2], (n, 128))
                flux0, flux1, flux2 = [], [], []
                for w in range(tiles):
                    slope0 = after[w][skip : R + 8] - here[w]
                    if f == F - 1:
                        slope0 = jnp.where(z == nz - 1, 0.0, slope0)
                    slope1 = pltpu.roll(now[w][skip:], n + 7, 0)[:n] - here[w]
                    slope1 = jnp.concatenate(
                        [slope1[: n - 8], jnp.where(last_image_row, 0.0, slope1[n - 8 :])], axis=0
                    )
                    beyond = turned[w + 1] if w + 1 < tiles else wall
                    slope2 = jnp.where(lane == 127, beyond, turned[w]) - here[w]
                    if w + 1 == tiles:
                        slope2 = jnp.where((lane == 127) & (c == nc - 1), 0.0, slope2)
                    weight = lax.rsqrt(
                        smooth_floor + slope0 * slope0 + slope1 * slope1 + slope2 * slope2
                    )
                    flux0.append((slope0 * weight)[8 - skip :])
                    if f >= 0:
                        flux = slope1 * weight
                        flux1.append(
                            jnp.concatenate(
                                [jnp.where(above_image, 0.0, flux[:8]), flux[8:]], axis=0
                            )
                        )
                        flux2.append((slope2 * weight)[8:])
                if f < 0:
                    flux0 = [jnp.where(z == 0, 0.0, t) for t in flux0]
                else:
                    moved = [pltpu.roll(t, 1, 1) for t in flux2]
                    entry = jnp.broadcast_to(fluxes_in[:, f : f + 1], (R, 128))
                    lane = lax.broadcasted_iota(jnp.int32, (R, 128), 1)
                    for w in range(tiles):
                        left = jnp.where(lane == 0, moved[w - 1] if w > 0 else entry, moved[w])
                        above = pltpu.roll(flux1[w], 1, 0)[8:]
                        spread = (flux0[w] - flux0_before[w]) + (flux1[w][8:] - above) + (flux2[w] - left)
                        lanes = slice(w * 128, w * 128 + 128)
                        value = (1.0 - relax_rate) * here[w][8:] + (
                            target[f, at, lanes] + (relax_rate * smooth_weight) * spread
                        )
                        if last:
                            shrunk = value - jnp.clip(value, -shrink_level, shrink_level)
                            result[f, at, lanes] = shrunk
                            anchor[f, at, lanes] = anchor[f, at, lanes] - shrunk
                        else:
                            field[k + 1][f + 1, pl.ds(start + 8, R), lanes] = value
                flux0_before = flux0
                now = after

        def products(left_of, right_of, lefts, rights, first, count, start, store):
            def body(step, totals):
                rows = pl.ds(pl.multiple_of(first + step * 8, 8), 8)
                a = [left_of[i, rows, :] for i in lefts]
                b = [right_of[j, rows, :] for j in rights]
                out = []
                for x in range(len(lefts)):
                    for y in range(len(rights)):
                        prod = a[x] * b[y]
                        total = totals[len(out)]
                        for w in range(W // 128):
                            total = total + prod[:, w * 128 : w * 128 + 128]
                        out.append(total)
                return tuple(out)

            totals = lax.fori_loop(
                0, count // 8, body, tuple(start(i, j) for i in lefts for j in rights), unroll=3 if count % 24 == 0 else 1
            )
            n = 0
            for i in lefts:
                for j in rights:
                    store(i, j, totals[n])
                    n += 1

        def held(block):
            return (block - z >= 2) | (z - block >= 2)

        def move(block, piece):
            rows = pl.ds(pl.multiple_of(block * own + piece * CHUNK, 8), CHUNK)
            spot = pl.ds(pl.multiple_of(piece * CHUNK, 8), CHUNK)
            return pltpu.make_async_remote_copy(
                src_ref=anchor.at[:, rows, :], dst_ref=owned.at[pl.ds(z * F, F), spot, :],
                send_sem=move_send.at[block], recv_sem=move_recv.at[z, piece],
                device_id=(r, c, block), device_id_type=MESH,
            )

        send_faces(0, 0, 1)
        for j in range(SEGMENTS):
            if j % (SEGMENTS // 2) == 0:
                loads[j // (SEGMENTS // 2)].wait()
            pack_columns(0, j)
            send_columns(0, j)
            if j == SEGMENTS // 2:
                send_halos(0, strips)
                send_halos(0, corners)
            send_faces(0, max(1, j * per), (j + 1) * per)

        zero_tile = jnp.zeros((8, 128), jnp.float32)

        def store_gram(i, j, value):
            row = jnp.sum(value, axis=0, keepdims=True)
            sums[j, i : i + 1, :] = row
            if i // 4 != j // 4:
                sums[i, j : j + 1, :] = row

        lane_r = lax.broadcasted_iota(jnp.int32, (rank, 128), 1)
        row_r = lax.broadcasted_iota(jnp.int32, (rank, 128), 0)

        def gram_share():
            for i in range(0, rank, 4):
                for j in range(i, rank, 4):
                    products(
                        basis, basis, range(i, i + 4), range(j, j + 4), z * own, own,
                        lambda i, j: zero_tile, store_gram,
                    )
            tile = jnp.zeros((rank, 128), jnp.float32)
            for q in range(rank):
                tile = jnp.where(lane_r == q, jnp.sum(sums[q], axis=1, keepdims=True), tile)
            lane = lax.broadcasted_iota(jnp.int32, (8, 128), 1)
            tile = jnp.where(lane < rank, tile[:8], pltpu.roll(tile[8:], rank, 1))
            tile = jnp.where(lane < 2 * rank, tile, pltpu.roll(pltpu.roll(tile, 4, 0), 2 * rank, 1))
            tile = jnp.where(lane < 4 * rank, tile, pltpu.roll(pltpu.roll(tile, 6, 0), 4 * rank, 1))
            grams[z] = tile

        def unfold(tile):
            row = lax.broadcasted_iota(jnp.int32, (8, 128), 0)
            tile = jnp.where(row < 2, tile, pltpu.roll(pltpu.roll(tile, 2, 0), 128 - 4 * rank, 1))
            tile = jnp.where(row < 4, tile, pltpu.roll(pltpu.roll(tile, 4, 0), 128 - 2 * rank, 1))
            tile = jnp.concatenate([tile, pltpu.roll(tile, 128 - rank, 1)], axis=0)
            return jnp.where(lane_r < rank, tile, 0.0)

        def all_sent(block, sem):
            return pltpu.make_async_remote_copy(
                src_ref=block, dst_ref=block, send_sem=sem.at[0], recv_sem=sem.at[0],
                device_id=(r, c, lax.rem(z + 1, nz)), device_id_type=MESH,
            )

        def all_here(block, sem):
            return pltpu.make_async_remote_copy(
                src_ref=block, dst_ref=block, send_sem=sem.at[0], recv_sem=sem.at[0],
                device_id=(r, c, lax.rem(z + 1, nz)), device_id_type=MESH,
            )

        def share_gram(d):
            return pltpu.make_async_remote_copy(
                src_ref=grams.at[z, 0:2], dst_ref=grams.at[z, 0:2],
                send_sem=gram_send.at[0], recv_sem=gram_recv.at[0],
                device_id=(r, c, lax.rem(z + d, nz)), device_id_type=MESH,
            )

        group = nr * nc
        me = r * nc + c

        def share_total(d):
            other = lax.rem(me + d, group)
            return pltpu.make_async_remote_copy(
                src_ref=gram_parts.at[me, 0:2], dst_ref=gram_parts.at[me, 0:2],
                send_sem=total_send.at[0], recv_sem=total_recv.at[0],
                device_id=(other // nc, lax.rem(other, nc), z), device_id_type=MESH,
            )

        def store_cross(i, j, value):
            cross[j, i] = value

        def find_target(h):
            for load in loads[3 + 3 * h : 6 + 3 * h]:
                load.wait()

            @pl.loop(0, half // 8)
            def _(step):
                rows = pl.ds(pl.multiple_of(half_start(h) + step * 8, 8), 8)
                totals = [None] * F
                for q in range(rank):
                    plane = basis[q, rows, :]
                    for f in range(F):
                        term = coeff_ref[f, q] * plane
                        totals[f] = term if totals[f] is None else totals[f] + term
                for f in range(F):
                    lifted = dual_scale * mult[f, rows, :]
                    anchor[f, rows, :] = video[f, rows, :] + lifted
                    target[f, rows, :] = relax_rate * (video[f, rows, :] - totals[f] + lifted)

        loads[2].wait()
        find_target(0)
        find_target(1)
        gram_share()

        def advance(k, step):
            start = pl.multiple_of(chunk_at(step) * CHUNK, 8)
            sweep(k, k == PASSES - 1, start)
            if k == PASSES - 1:
                place, piece = chunk_at(step) // pieces, lax.rem(chunk_at(step), pieces)

                @pl.when((place - z == 1) | (z - place == 1))
                def _():
                    move(place, piece).start()

                for i in range(0, rank, 4):
                    products(
                        basis, anchor, range(i, i + 4), range(F), start, CHUNK,
                        lambda i, j: cross[j, i], store_cross,
                    )

        cross[...] = jnp.zeros_like(cross)
        bottom_row[...] = jnp.zeros_like(bottom_row)
        for k in range(PASSES):
            last = k == PASSES - 1
            if k > 0 and not last:
                finish_sends(k - 1)
            wait_columns(k, 0)
            prepare_columns(k, 0)
            wait_face(k, 0)

            @pl.loop(0, SEGMENTS)
            def _(j, k=k, last=last):
                @pl.loop(j * per, (j + 1) * per - 1)
                def _(step):
                    wait_face(k, step + 1)
                    advance(k, step)

                final = j == SEGMENTS - 1
                if k == PASSES - 2:
                    @pl.when(j == 1)
                    def _():
                        for d in range(1, nz):
                            share_gram(d).start()
                if k == PASSES - 1:
                    @pl.when(j == 1)
                    def _():
                        all_here(grams.at[0 : nz - 1, 0:2], gram_recv).wait_recv()
                        total = grams[0]
                        for i in range(1, nz):
                            total = total + grams[i]
                        gram_parts[me] = total
                        for d in range(1, group):
                            share_total(d).start()

                @pl.when(j == SEGMENTS - 2)
                def _():
                    take_corners(k)

                @pl.when(~final)
                def _():
                    wait_columns(k, j + 1)
                    prepare_columns(k, j + 1)
                    wait_face(k, (j + 1) * per)

                @pl.when(final)
                def _():
                    wait_halos(k, strips)

                advance(k, (j + 1) * per - 1)
                if not last:
                    @pl.when(final)
                    def _():
                        send_halos(k + 1, strips)
                        send_halos(k + 1, corners)

                    pack_columns(k + 1, j)
                    send_columns(k + 1, j)
                    send_faces(k + 1, j * per, (j + 1) * per)


        def send_held(turn, low, high):
            for b in range(nz):
                @pl.when(held(b) & turn)
                def _(b=b):
                    for p in range(low, high):
                        move(b, p).start()

        for far, near in ((nz - 1, 0), (0, nz - 1)):
            place = far - 1 if far > near else far + 1

            @pl.when((z == near) & held(jnp.int32(place)))
            def _(place=place):
                move(place, 0).start()

        for j in range(F):
            for i in range(rank):
                sums[rank + j, i : i + 1, :] = jnp.sum(cross[j, i], axis=0, keepdims=True)

        part = jnp.zeros((rank, 128), jnp.float32)
        for q in range(rank, rank + F):
            part = jnp.where(lane_r == q, jnp.sum(sums[q], axis=1, keepdims=True), part)
        parts[me] = part

        def share_part(d):
            other = lax.rem(me + d, group)
            return pltpu.make_async_remote_copy(
                src_ref=parts.at[me], dst_ref=parts.at[me],
                send_sem=part_send.at[0], recv_sem=part_recv.at[0],
                device_id=(other // nc, lax.rem(other, nc), z), device_id_type=MESH,
            )

        for d in range(1, group):
            share_part(d).start()
        pixel_ridge = ridge_share * H * W * group
        diagonal = lane_r == row_r
        before = jnp.zeros((rank, 128), jnp.float32)
        for q in range(rank):
            for f in range(F):
                before = jnp.where((row_r == q) & (lane_r == rank + f), coeff_ref[f, q], before)
        all_here(gram_parts.at[0 : group - 1, 0:2], total_recv).wait_recv()
        total = gram_parts[0]
        for i in range(1, group):
            total = total + gram_parts[i]
        diagonal = lane_r == row_r
        system = unfold(total) + jnp.where(
            diagonal, pixel_ridge, jnp.where(lane_r == row_r + rank, 1.0, 0.0)
        )
        system = eliminate(system, rank)
        for q in range(rank):
            inverse[q] = jnp.broadcast_to(system[:, rank + q : rank + q + 1], (rank, 128))
        all_here(parts.at[0 : group - 1], part_recv).wait_recv()
        total = parts[0]
        for i in range(1, group):
            total = total + parts[i]
        total = total + pixel_ridge * before
        solved = inverse[0] * total[0:1, :]
        for q in range(1, rank):
            solved = solved + inverse[q] * total[q : q + 1, :]
        square[...] = jnp.zeros_like(square)
        square[0:rank, :] = solved
        mine = square[...].T[rank : rank + F, :]
        shares[pl.ds(z * F, F), :] = mine

        def share_rows(d):
            return pltpu.make_async_remote_copy(
                src_ref=shares.at[pl.ds(z * F, F)], dst_ref=shares.at[pl.ds(z * F, F)],
                send_sem=share_send.at[0], recv_sem=share_recv.at[0],
                device_id=(r, c, lax.rem(z + d, nz)), device_id_type=MESH,
            )

        for d in range(1, nz):
            share_rows(d).start()

        send_held(inner, 0, pieces)
        coeff_out[...] = mine[:, 0:rank]
        all_here(shares.at[0 : (nz - 1) * F], share_recv).wait_recv()
        for b in range(nz):
            @pl.when(held(b) & ~inner)
            def _(b=b):
                first = jnp.where(((z == 0) & (b == nz - 2)) | ((z == nz - 1) & (b == 1)), 1, 0)

                @pl.loop(first, pieces)
                def _(p):
                    move(b, p).start()

        frames = F * nz
        square[0:frames, :] = shares[...]
        wide = pltpu.roll(square[...].T[0:rank, :], rank, 1)
        square[0:rank, :] = wide
        gram = lax.dot_general(
            wide, square[...], (((1,), (1,)), ((), ())),
            precision=lax.Precision.HIGHEST, preferred_element_type=jnp.float32,
        )
        frame_ridge = ridge_share * frames
        system = jnp.where(diagonal, gram + frame_ridge, gram) + wide
        system = system + jnp.where(lane_r == row_r + rank + frames, frame_ridge, 0.0)
        table[...] = eliminate(system, rank)
        to_scalar = pltpu.make_async_copy(table, table_smem, small_sem.at[0])
        to_scalar.start()
        to_scalar.wait()
        my_base = z * own

        @pl.loop(0, own // 8)
        def _(step):
            rows = pl.ds(pl.multiple_of(step * 8, 8), 8)
            old = pl.ds(pl.multiple_of(my_base + step * 8, 8), 8)
            for half in range(0, rank, 8):
                totals = [None] * 8
                for f in range(F + rank):
                    plane = anchor[f, old, :] if f < F else basis[f - F, old, :]
                    place = rank + z * F + f if f < F else rank + frames + f - F
                    for q in range(8):
                        term = table_smem[half + q, place] * plane
                        totals[q] = term if totals[q] is None else totals[q] + term
                for q in range(8):
                    fresh[half + q, rows, :] = totals[q]

        for k in range(PASSES - 2, PASSES):
            finish_sends(k)
        all_sent(shares.at[0 : (nz - 1) * F], share_send).wait_send()
        all_sent(grams.at[0 : nz - 1, 0:2], gram_send).wait_send()
        all_sent(gram_parts.at[0 : group - 1, 0:2], total_send).wait_send()
        all_sent(parts.at[0 : group - 1], part_send).wait_send()

    dma = pltpu.SemaphoreType.DMA
    one = dma((1,))
    pl.run_scoped(
        work,
        dma((9,)),
        dma((2, 9)),
        dma((2, 3 + 2 * SEGMENTS + steps)),
        *(one,) * 9,
    )

    for n in range(nz - 1):
        near = n + (n >= z).astype(jnp.int32)
        far = nz - 1 - (n + (n >= nz - 1 - z).astype(jnp.int32))
        distance = 1 if n == 0 else nz - n
        source = jnp.where(2 * z < nz, near, far)
        source = jnp.where(z == 0, distance, jnp.where(z == nz - 1, nz - 1 - distance, source))

        @pl.loop(0, pieces)
        def _(piece, source=source):
            take(source, piece).wait_recv()
            for step in range(CHUNK // 8):
                rows = pl.ds(pl.multiple_of(piece * CHUNK + step * 8, 8), 8)
                planes = [owned[source * F + f, rows, :] for f in range(F)]
                for q in range(rank):
                    value = fresh[q, rows, :]
                    for f in range(F):
                        value = value + table_smem[q, rank + source * F + f] * planes[f]
                    fresh[q, rows, :] = value

    for b in range(nz):
        @pl.when(z != b)
        def _(b=b):
            rows = pl.ds(b * own, own)
            pltpu.make_async_remote_copy(
                src_ref=anchor.at[:, rows, :], dst_ref=owned.at[pl.ds(z * F, F)],
                send_sem=move_send.at[b], recv_sem=move_recv.at[z, 0],
                device_id=(r, c, b), device_id_type=MESH,
            ).wait_send()


def deliver(shrunk, coeff, fresh, shrunk_hbm, coeff_hbm, fresh_hbm, sems):
    copies = [pltpu.make_async_copy(coeff, coeff_hbm, sems.at[0])]
    for source, place in ((fresh, fresh_hbm), (shrunk, shrunk_hbm)):
        share = source.shape[0] // 4
        for i in range(4):
            part = pl.ds(i * share, share)
            copies.append(
                pltpu.make_async_copy(source.at[part], place.at[part], sems.at[len(copies)])
            )
    for copy in copies:
        copy.start()
    for copy in copies:
        copy.wait()


def whole_kernel(video, multiplier, foreground, basis, coefficients):
    F, H, W = video.shape
    rank = basis.shape[0]
    nr, nc, nz = (lax.axis_size(name) for name in ("row", "col", "frame"))
    f32 = jnp.float32
    own = H // nz
    group = nr * nc
    vmem = pltpu.VMEM
    dma = pltpu.SemaphoreType.DMA
    pieces = own // CHUNK
    hbm = pl.BlockSpec(memory_space=pl.ANY)
    on_chip = pl.BlockSpec(memory_space=pltpu.VMEM)
    found = pl.pallas_call(
        functools.partial(kernel, (F, H, W, rank, nr, nc, nz)),
        out_shape=(vmem((F, H, W), f32), vmem((F, rank), f32), vmem((rank, own, W), f32)),
        in_specs=[hbm] * 5,
        out_specs=[on_chip] * 3,
        scratch_shapes=[vmem((F + 2, H + 16, W), f32)] * PASSES
        + [
            vmem((F, H, W), f32),
            vmem((F, H, W), f32),
            vmem((rank, H, W), f32),
            vmem((F, H, W), f32),
            vmem((F, H, W), f32),
            vmem((F * nz, own, W), f32),
            vmem((PASSES, SEGMENTS, 16, H // SEGMENTS), f32),
            vmem((PASSES, SEGMENTS, 16, H // SEGMENTS), f32),
            vmem((PASSES, 2, F, 8, 128), f32),
            vmem((H + 8, 128), f32),
            vmem((H + 16, 128), f32),
            vmem((H + 16, 128), f32),
            vmem((H + 24, 128), f32),
            vmem((H + 24, 128), f32),
            vmem((8, 128), f32),
            vmem((F, rank, 8, 128), f32),
            vmem((rank + F, rank, 128), f32),
            vmem((nz, 8, 128), f32),
            vmem((group, 8, 128), f32),
            vmem((rank, rank, 128), f32),
            vmem((group, rank, 128), f32),
            vmem((nz * F, 128), f32),
            vmem((128, 128), f32),
            vmem((rank, 128), f32),
            pltpu.SMEM((F, rank), f32),
            pltpu.SMEM((rank, 128), f32),
            dma((nz,)),
            dma((nz, pieces)),
        ],
        compiler_params=pltpu.CompilerParams(
            collective_id=0, has_side_effects=True, vmem_limit_bytes=32 * 1024 * 1024
        ),
    )(
        *(
            pltpu.with_memory_space_constraint(x, pltpu.HBM)
            for x in (coefficients, video, multiplier, foreground, basis)
        )
    )
    return pl.pallas_call(
        deliver,
        out_shape=(
            jax.ShapeDtypeStruct((F, H, W), f32),
            jax.ShapeDtypeStruct((F, rank), f32),
            jax.ShapeDtypeStruct((rank, own, W), f32),
        ),
        in_specs=[on_chip] * 3,
        out_specs=[hbm] * 3,
        scratch_shapes=[dma((9,))],
    )(*(pltpu.with_memory_space_constraint(x, pltpu.VMEM) for x in found))


def body(video, multiplier, foreground, basis, coefficients):
    F, H, W = video.shape
    rank = basis.shape[0]
    nz = lax.axis_size("frame")
    fits = (
        H % nz == 0 and (H // nz) % 8 == 0 and (H // nz) % CHUNK == 0 and W % 128 == 0
        and H % 16 == 0 and H % (SEGMENTS * CHUNK) == 0 and lax.axis_size("row") <= 2
        and F % 4 == 0 and F < 8 and rank == 16 and nz >= 2 and F * nz == rank and 2 * rank + F * nz <= 128
    )
    run = whole_kernel if fits else local
    return run(video, multiplier, foreground, basis, coefficients)


def solution(mesh):
    placed = (
        P("frame", "row", "col"),
        P("frame", "row", "col"),
        P("frame", "row", "col"),
        P(None, "row", "col"),
        P("frame", None),
    )
    return jax.shard_map(
        body,
        mesh=mesh,
        in_specs=placed,
        out_specs=(P("frame", "row", "col"), P("frame", None), P(None, ("row", "frame"), "col")),
        check_vma=False,
    )
```

time: 61.5 us -> 55.2 us (0.90)
  the two profiles are of different devices: /device:TPU:30 before, /device:TPU:0 now
where the time goes in v6:
time: 55.2 us; the launch traced here: 55 us
  Pallas kernels  54.4 us (99%)
  between operations  0.64 us (1%)
    pallas_call x1, Pallas kernels, whole_kernel(): pl.pallas_call(functools.partial(kernel, (F, H, W, rank, nr, nc, nz)), ou...  52.9 us
    pallas_call x1, Pallas kernels, whole_kernel(): pl.pallas_call(deliver, out_shape=(jax.ShapeDtypeStruct((F, H, W), f32),...  1.48 us

profile of v6, /device:TPU:0, one launch (start us, length us, event | category | flops | bytes accessed | tf_op | source)
XLA Modules:
  0.0 55.0 jit_solution(13400573906059588240)
XLA Ops:
  0.6 52.9 %shard_map.76 = (f32[4,288,256]{2,1,0:T(8,128)S(1)}, f32[4,16]{1,0:T(4,128)S(1)}, f32[16,72,256]{2,1,0:T(8,128)S(1)}) custom-call(f32[4,16]{1,0:T(4,128)} %coeff_hbm.1, f32[4,288,256]{2,1,0:T(8,128)} %video_hbm.1, f32[4,288,256]{2,1,0:T(8,128)} %mult_hbm.1, f32[4,288,256]{2,1,0:T(8,128)} %fore_hbm.1, f32[16,288,256]{2,1,0:T(8,128)} %basis_hbm.1), custom_call_target="tpu_custom_call" | custom-call | tf_op jit(solution)/shard_map/pallas_call | solution.py:872
  53.6 1.5 %shard_map.77 = (f32[4,288,256]{2,1,0:T(8,128)}, f32[4,16]{1,0:T(4,128)}, f32[16,72,256]{2,1,0:T(8,128)}) custom-call(f32[4,288,256]{2,1,0:T(8,128)S(1)} %get-tuple-element.6.shrunk, f32[4,16]{1,0:T(4,128)S(1)} %get-tuple-element.7.coeff, f32[16,72,256]{2,1,0:T(8,128)S(1)} %get-tuple-element.8.fresh), custom_call_target="tpu_custom_call" | custom-call | tf_op jit(solution)/shard_map/pallas_call | solution.py:917

commit v7 on v6

--- a/solution.py
+++ b/solution.py
@@ -141,7 +141,6 @@
     field0, field1, field2, video, mult, basis, anchor, target, owned,
     packed, arrived, corner, edge_next, edge_flux, first_cols, left_now, left_next, bottom_row,
     cross, sums, grams, gram_parts, inverse, parts, shares, square, table, coeff_ref, table_smem,
-    move_send, move_recv,
 ):
     field = (field0, field1, field2)
     F, H, W, rank, nr, nc, nz = sizes
@@ -180,19 +179,19 @@
                 ok = test if ok is None else ok & test
         return ok
 
-    def take(source, piece):
-        rows = pl.ds(pl.multiple_of(z * own + piece * CHUNK, 8), CHUNK)
-        spot = pl.ds(pl.multiple_of(piece * CHUNK, 8), CHUNK)
-        return pltpu.make_async_remote_copy(
-            src_ref=anchor.at[:, rows, :], dst_ref=owned.at[pl.ds(source * F, F), spot, :],
-            send_sem=move_send.at[source], recv_sem=move_recv.at[source, piece],
-            device_id=(r, c, source), device_id_type=MESH,
-        )
-
     def work(
         in_sems, halo_send, halo_recv, part_send, part_recv, gram_send, gram_recv,
-        total_send, total_recv, share_send, share_recv, small_sem,
+        total_send, total_recv, share_send, share_recv, small_sem, move_send, move_recv,
     ):
+        def take(source, piece):
+            rows = pl.ds(pl.multiple_of(z * own + piece * CHUNK, 8), CHUNK)
+            spot = pl.ds(pl.multiple_of(piece * CHUNK, 8), CHUNK)
+            return pltpu.make_async_remote_copy(
+                src_ref=anchor.at[:, rows, :], dst_ref=owned.at[pl.ds(source * F, F), spot, :],
+                send_sem=move_send.at[source], recv_sem=move_recv.at[source, piece],
+                device_id=(r, c, source), device_id_type=MESH,
+            )
+
         halves = [pl.ds(half_start(h), half) for h in range(2)]
         loads = [
             pltpu.make_async_copy(src, dst, in_sems.at[i])
@@ -802,6 +801,35 @@
         all_sent(gram_parts.at[0 : group - 1, 0:2], total_send).wait_send()
         all_sent(parts.at[0 : group - 1], part_send).wait_send()
 
+        for n in range(nz - 1):
+            near = n + (n >= z).astype(jnp.int32)
+            far = nz - 1 - (n + (n >= nz - 1 - z).astype(jnp.int32))
+            distance = 1 if n == 0 else nz - n
+            source = jnp.where(2 * z < nz, near, far)
+            source = jnp.where(z == 0, distance, jnp.where(z == nz - 1, nz - 1 - distance, source))
+
+            @pl.loop(0, pieces)
+            def _(piece, source=source):
+                take(source, piece).wait_recv()
+                for step in range(CHUNK // 8):
+                    rows = pl.ds(pl.multiple_of(piece * CHUNK + step * 8, 8), 8)
+                    planes = [owned[source * F + f, rows, :] for f in range(F)]
+                    for q in range(rank):
+                        value = fresh[q, rows, :]
+                        for f in range(F):
+                            value = value + table_smem[q, rank + source * F + f] * planes[f]
+                        fresh[q, rows, :] = value
+
+        for b in range(nz):
+            @pl.when(z != b)
+            def _(b=b):
+                rows = pl.ds(b * own, own)
+                pltpu.make_async_remote_copy(
+                    src_ref=anchor.at[:, rows, :], dst_ref=owned.at[pl.ds(z * F, F)],
+                    send_sem=move_send.at[b], recv_sem=move_recv.at[z, 0],
+                    device_id=(r, c, b), device_id_type=MESH,
+                ).wait_send()
+
     dma = pltpu.SemaphoreType.DMA
     one = dma((1,))
     pl.run_scoped(
@@ -810,51 +838,27 @@
         dma((2, 9)),
         dma((2, 3 + 2 * SEGMENTS + steps)),
         *(one,) * 9,
-    )
-
-    for n in range(nz - 1):
-        near = n + (n >= z).astype(jnp.int32)
-        far = nz - 1 - (n + (n >= nz - 1 - z).astype(jnp.int32))
-        distance = 1 if n == 0 else nz - n
-        source = jnp.where(2 * z < nz, near, far)
-        source = jnp.where(z == 0, distance, jnp.where(z == nz - 1, nz - 1 - distance, source))
-
-        @pl.loop(0, pieces)
-        def _(piece, source=source):
-            take(source, piece).wait_recv()
-            for step in range(CHUNK // 8):
-                rows = pl.ds(pl.multiple_of(piece * CHUNK + step * 8, 8), 8)
-                planes = [owned[source * F + f, rows, :] for f in range(F)]
-                for q in range(rank):
-                    value = fresh[q, rows, :]
-                    for f in range(F):
-                        value = value + table_smem[q, rank + source * F + f] * planes[f]
-                    fresh[q, rows, :] = value
-
-    for b in range(nz):
-        @pl.when(z != b)
-        def _(b=b):
-            rows = pl.ds(b * own, own)
-            pltpu.make_async_remote_copy(
-                src_ref=anchor.at[:, rows, :], dst_ref=owned.at[pl.ds(z * F, F)],
-                send_sem=move_send.at[b], recv_sem=move_recv.at[z, 0],
-                device_id=(r, c, b), device_id_type=MESH,
-            ).wait_send()
-
-
-def deliver(shrunk, coeff, fresh, shrunk_hbm, coeff_hbm, fresh_hbm, sems):
-    copies = [pltpu.make_async_copy(coeff, coeff_hbm, sems.at[0])]
-    for source, place in ((fresh, fresh_hbm), (shrunk, shrunk_hbm)):
-        share = source.shape[0] // 4
-        for i in range(4):
-            part = pl.ds(i * share, share)
-            copies.append(
-                pltpu.make_async_copy(source.at[part], place.at[part], sems.at[len(copies)])
-            )
-    for copy in copies:
-        copy.start()
-    for copy in copies:
-        copy.wait()
+        dma((nz,)),
+        dma((nz, pieces)),
+    )
+
+
+def deliver(shrunk, coeff, fresh, shrunk_hbm, coeff_hbm, fresh_hbm):
+    def work(sems):
+        copies = [pltpu.make_async_copy(coeff, coeff_hbm, sems.at[0])]
+        for source, place in ((fresh, fresh_hbm), (shrunk, shrunk_hbm)):
+            share = source.shape[0] // 1
+            for i in range(1):
+                part = pl.ds(i * share, share)
+                copies.append(
+                    pltpu.make_async_copy(source.at[part], place.at[part], sems.at[len(copies)])
+                )
+        for copy in copies:
+            copy.start()
+        for copy in copies:
+            copy.wait()
+
+    pl.run_scoped(work, pltpu.SemaphoreType.DMA((3,)))
 
 
 def whole_kernel(video, multiplier, foreground, basis, coefficients):
@@ -902,8 +906,6 @@
             vmem((rank, 128), f32),
             pltpu.SMEM((F, rank), f32),
             pltpu.SMEM((rank, 128), f32),
-            dma((nz,)),
-            dma((nz, pieces)),
         ],
         compiler_params=pltpu.CompilerParams(
             collective_id=0, has_side_effects=True, vmem_limit_bytes=32 * 1024 * 1024
@@ -923,7 +925,6 @@
         ),
         in_specs=[on_chip] * 3,
         out_specs=[hbm] * 3,
-        scratch_shapes=[dma((9,))],
     )(*(pltpu.with_memory_space_constraint(x, pltpu.VMEM) for x in found))
 
 

time: 55.2 us -> 55 us (level)
  no operation moved by 1% of the time
where the time goes in v7:
time: 55 us; the launch traced here: 54.8 us
  Pallas kernels  54.2 us (99%)
  between operations  0.64 us (1%)
    pallas_call x1, Pallas kernels, whole_kernel(): pl.pallas_call(functools.partial(kernel, (F, H, W, rank, nr, nc, nz)), ou...  52.8 us
    pallas_call x1, Pallas kernels, whole_kernel(): pl.pallas_call(deliver, out_shape=(jax.ShapeDtypeStruct((F, H, W), f32),...  1.41 us

profile of v7, /device:TPU:0, one launch (start us, length us, event | category | flops | bytes accessed | tf_op | source)
XLA Modules:
  0.0 54.8 jit_solution(2804543576416940209)
XLA Ops:
  0.6 52.8 %shard_map.76 = (f32[4,288,256]{2,1,0:T(8,128)S(1)}, f32[4,16]{1,0:T(4,128)S(1)}, f32[16,72,256]{2,1,0:T(8,128)S(1)}) custom-call(f32[4,16]{1,0:T(4,128)} %coeff_hbm.1, f32[4,288,256]{2,1,0:T(8,128)} %video_hbm.1, f32[4,288,256]{2,1,0:T(8,128)} %mult_hbm.1, f32[4,288,256]{2,1,0:T(8,128)} %fore_hbm.1, f32[16,288,256]{2,1,0:T(8,128)} %basis_hbm.1), custom_call_target="tpu_custom_call" | custom-call | tf_op jit(solution)/shard_map/pallas_call | solution.py:876
  53.4 1.4 %shard_map.77 = (f32[4,288,256]{2,1,0:T(8,128)}, f32[4,16]{1,0:T(4,128)}, f32[16,72,256]{2,1,0:T(8,128)}) custom-call(f32[4,288,256]{2,1,0:T(8,128)S(1)} %get-tuple-element.6.shrunk, f32[4,16]{1,0:T(4,128)S(1)} %get-tuple-element.7.coeff, f32[16,72,256]{2,1,0:T(8,128)S(1)} %get-tuple-element.8.fresh), custom_call_target="tpu_custom_call" | custom-call | tf_op jit(solution)/shard_map/pallas_call | solution.py:919

commit v8 on v7

--- a/solution.py
+++ b/solution.py
@@ -211,9 +211,6 @@
                 ]
             )
         ]
-        for load in loads[:2]:
-            load.start()
-
         barrier = pltpu.get_barrier_semaphore()
         beside = ((0, 0, 1), (0, 1, 0), (1, 0, 0), (1, 0, -1), (0, 1, -1), (1, -1, 0))
         beside += tuple(tuple(-s for s in step) for step in beside)
@@ -229,7 +226,7 @@
         expected = jnp.int32(0)
         for step in beside:
             expected = expected + inside(*step).astype(jnp.int32)
-        for load in loads[2:]:
+        for load in loads:
             load.start()
 
         pl.semaphore_wait(barrier, expected)

time: 55 us -> 55 us (level)
  no operation moved by 1% of the time
where the time goes in v8:
time: 55 us; the launch traced here: 54.8 us
  Pallas kernels  54.2 us (99%)
  between operations  0.64 us (1%)
    pallas_call x1, Pallas kernels, whole_kernel(): pl.pallas_call(functools.partial(kernel, (F, H, W, rank, nr, nc, nz)), ou...  52.8 us
    pallas_call x1, Pallas kernels, whole_kernel(): pl.pallas_call(deliver, out_shape=(jax.ShapeDtypeStruct((F, H, W), f32),...  1.41 us

profile of v8, /device:TPU:0, one launch (start us, length us, event | category | flops | bytes accessed | tf_op | source)
XLA Modules:
  0.0 54.8 jit_solution(2180652604175743489)
XLA Ops:
  0.6 52.8 %shard_map.76 = (f32[4,288,256]{2,1,0:T(8,128)S(1)}, f32[4,16]{1,0:T(4,128)S(1)}, f32[16,72,256]{2,1,0:T(8,128)S(1)}) custom-call(f32[4,16]{1,0:T(4,128)} %coeff_hbm.1, f32[4,288,256]{2,1,0:T(8,128)} %video_hbm.1, f32[4,288,256]{2,1,0:T(8,128)} %mult_hbm.1, f32[4,288,256]{2,1,0:T(8,128)} %fore_hbm.1, f32[16,288,256]{2,1,0:T(8,128)} %basis_hbm.1), custom_call_target="tpu_custom_call" | custom-call | tf_op jit(solution)/shard_map/pallas_call | solution.py:873
  53.4 1.4 %shard_map.77 = (f32[4,288,256]{2,1,0:T(8,128)}, f32[4,16]{1,0:T(4,128)}, f32[16,72,256]{2,1,0:T(8,128)}) custom-call(f32[4,288,256]{2,1,0:T(8,128)S(1)} %get-tuple-element.6.shrunk, f32[4,16]{1,0:T(4,128)S(1)} %get-tuple-element.7.coeff, f32[16,72,256]{2,1,0:T(8,128)S(1)} %get-tuple-element.8.fresh), custom_call_target="tpu_custom_call" | custom-call | tf_op jit(solution)/shard_map/pallas_call | solution.py:916

commit v9 on v7

--- a/solution.py
+++ b/solution.py
@@ -753,8 +753,8 @@
         send_held(inner, 0, pieces)
         coeff_out[...] = mine[:, 0:rank]
         all_here(shares.at[0 : (nz - 1) * F], share_recv).wait_recv()
-        for b in range(nz):
-            @pl.when(held(b) & ~inner)
+        for end, b in [(0, b) for b in reversed(range(nz))] + [(nz - 1, b) for b in range(nz)]:
+            @pl.when(held(b) & (z == end))
             def _(b=b):
                 first = jnp.where(((z == 0) & (b == nz - 2)) | ((z == nz - 1) & (b == 1)), 1, 0)
 

time: 55 us -> 55 us (level)
  no operation moved by 1% of the time
where the time goes in v9:
time: 55 us; the launch traced here: 54.8 us
  Pallas kernels  54.2 us (99%)
  between operations  0.64 us (1%)
    pallas_call x1, Pallas kernels, whole_kernel(): pl.pallas_call(functools.partial(kernel, (F, H, W, rank, nr, nc, nz)), ou...  52.8 us
    pallas_call x1, Pallas kernels, whole_kernel(): pl.pallas_call(deliver, out_shape=(jax.ShapeDtypeStruct((F, H, W), f32),...  1.41 us

profile of v9, /device:TPU:0, one launch (start us, length us, event | category | flops | bytes accessed | tf_op | source)
XLA Modules:
  0.0 54.8 jit_solution(14181930434807517013)
XLA Ops:
  0.6 52.8 %shard_map.76 = (f32[4,288,256]{2,1,0:T(8,128)S(1)}, f32[4,16]{1,0:T(4,128)S(1)}, f32[16,72,256]{2,1,0:T(8,128)S(1)}) custom-call(f32[4,16]{1,0:T(4,128)} %coeff_hbm.1, f32[4,288,256]{2,1,0:T(8,128)} %video_hbm.1, f32[4,288,256]{2,1,0:T(8,128)} %mult_hbm.1, f32[4,288,256]{2,1,0:T(8,128)} %fore_hbm.1, f32[16,288,256]{2,1,0:T(8,128)} %basis_hbm.1), custom_call_target="tpu_custom_call" | custom-call | tf_op jit(solution)/shard_map/pallas_call | solution.py:876
  53.4 1.4 %shard_map.77 = (f32[4,288,256]{2,1,0:T(8,128)}, f32[4,16]{1,0:T(4,128)}, f32[16,72,256]{2,1,0:T(8,128)}) custom-call(f32[4,288,256]{2,1,0:T(8,128)S(1)} %get-tuple-element.6.shrunk, f32[4,16]{1,0:T(4,128)S(1)} %get-tuple-element.7.coeff, f32[16,72,256]{2,1,0:T(8,128)S(1)} %get-tuple-element.8.fresh), custom_call_target="tpu_custom_call" | custom-call | tf_op jit(solution)/shard_map/pallas_call | solution.py:919
